TPU v7x, 32 devices: a whole 2x2x4 slice. The times are simulated.
32 devices in a mesh: img: 16 (over z, y, x), mlp: 2 (over core).
Axes of the slice: x: 2, y: 2, z: 4, core: 2. Of those that a mesh axis runs over, the one named last changes fastest.
Arguments:
- images: bfloat16 [160, 197, 768], P(('img', 'mlp')), may hold values from -13 to 13
- keep_mask: int32 [160, 197], P(('img', 'mlp')), may hold values from 0 to 1, as said below
- ln1_gain: float32 [768], replicated, may hold values from 0.5 to 1.5
- ln1_bias: float32 [768], replicated, may hold values from -3 to 3
- w_qkv: bfloat16 [768, 2304], replicated, may hold values from -0.21875 to 0.21875
- bias_q: bfloat16 [768], replicated, may hold values from -4 to 4
- bias_v: bfloat16 [768], replicated, may hold values from -0.75 to 0.75
- w_proj: bfloat16 [768, 768], replicated, may hold values from -1.5 to 1.5
- b_proj: bfloat16 [768], replicated, may hold values from -4 to 4
- ln2_gain: float32 [768], replicated, may hold values from 0.5 to 1.5
- ln2_bias: float32 [768], replicated, may hold values from -3 to 3
- w_fc1: bfloat16 [768, 3072], P(None, 'mlp'), may hold values from -0.21875 to 0.21875
- b_fc1: bfloat16 [3072], P('mlp'), may hold values from -4 to 4
- w_fc2: bfloat16 [3072, 768], P('mlp'), may hold values from -0.109375 to 0.109375
- b_fc2: bfloat16 [768], replicated, may hold values from -4 to 4
- cotangent: bfloat16 [160, 197, 768], P(('img', 'mlp')), may hold values from -6 to 6
Outputs:
- layer_out: bfloat16 [160, 197, 768], P(('img', 'mlp'))
- grad_images: float32 [160, 197, 768], P(('img', 'mlp'))
- grad_ln1_gain: float32 [768], replicated
- grad_ln1_bias: float32 [768], replicated
- grad_w_qkv: float32 [768, 2304], replicated
- grad_bias_q: float32 [768], replicated
- grad_bias_v: float32 [768], replicated
- grad_w_proj: float32 [768, 768], replicated
- grad_b_proj: float32 [768], replicated
- grad_ln2_gain: float32 [768], replicated
- grad_ln2_bias: float32 [768], replicated
- grad_w_fc1: float32 [768, 3072], P(None, 'mlp')
- grad_b_fc1: float32 [3072], P('mlp')
- grad_w_fc2: float32 [3072, 768], P('mlp')
- grad_b_fc2: float32 [768], replicated
- root_means: float32 [3], replicated
Inputs may be any that keep to these rules, and one draw needn't show every extreme that they name: `keep_mask`: each image keeps between (201) // 5 and 157 of its patches, and both counts occur.
All inputs are finite; a program needn't handle non-finite values.
Results may differ from a plain program's by a relative error of at most 0.015.
Values may be sent and summed in bfloat16 or wider, within the bound.
A program may use at most 192 MiB of HBM per device.

v0:
```python
import jax
import jax.numpy as jnp
from jax import lax
from jax.sharding import PartitionSpec as P

HEAD_DIM = 64


NORM_EPS = 1e-06


def norm_rows(input_rows, norm_gain, norm_shift):
    center = input_rows - jnp.mean(input_rows, axis=1, keepdims=True)
    inverse = lax.rsqrt(jnp.mean(center * center, axis=1, keepdims=True) + NORM_EPS)
    scaled = center * inverse
    return (scaled * norm_gain + norm_shift, scaled, inverse)


def norm_back(gradient, scaled, inverse, norm_gain):
    weighted = gradient * norm_gain
    inner_term = (
        weighted
        - jnp.mean(weighted, axis=1, keepdims=True)
        - scaled * jnp.mean(weighted * scaled, axis=1, keepdims=True)
    )
    return (inner_term * inverse, jnp.sum(gradient * scaled, axis=0), jnp.sum(gradient, axis=0))


def exact_gelu(values):
    return jax.nn.gelu(values, approximate=False)


def row_total(values):
    return jnp.sum(values.astype(jnp.float32), axis=0)


def round_trip(values):
    return lax.optimization_barrier(values.astype(jnp.bfloat16)).astype(jnp.float32)


def on_device(
    images,
    keep_mask,
    ln1_gain,
    ln1_bias,
    w_qkv,
    bias_q,
    bias_v,
    w_proj,
    b_proj,
    ln2_gain,
    ln2_bias,
    w_fc1,
    b_fc1,
    w_fc2,
    b_fc2,
    cotangent,
):
    image_count, patches, model_width = images.shape
    head_count = model_width // HEAD_DIM
    total_rows = image_count * patches
    score_scale = HEAD_DIM ** (-0.5)
    head_shape = (image_count, patches, head_count, HEAD_DIM)
    input_rows = images.reshape(total_rows, model_width).astype(jnp.float32)
    keep_column = keep_mask.astype(jnp.float32).reshape(total_rows, 1)
    key_open = (keep_mask > 0)[:, None, None, :]
    normed, scaled_one, inverse_one = norm_rows(input_rows, ln1_gain, ln1_bias)
    normed_low = normed.astype(jnp.bfloat16)
    projected = jnp.dot(normed_low, w_qkv, preferred_element_type=jnp.float32)
    query_heads = (projected[:, :model_width] + bias_q).astype(jnp.bfloat16).reshape(head_shape)
    key_heads = projected[:, model_width : 2 * model_width].astype(jnp.bfloat16).reshape(head_shape)
    value_heads = (
        (projected[:, 2 * model_width :] + bias_v).astype(jnp.bfloat16).reshape(head_shape)
    )

    def attention_scores(query_part, key_part):
        raw_scores = (
            jnp.einsum("gqhe,gkhe->ghqk", query_part, key_part, preferred_element_type=jnp.float32)
            * score_scale
        )
        return jnp.where(key_open, raw_scores, -1e30)

    scores = attention_scores(query_heads, key_heads)
    row_peak = jnp.max(scores, axis=3, keepdims=True)
    raised = jnp.exp(scores - row_peak)
    row_totals = jnp.sum(raised, axis=3, keepdims=True)
    log_total = row_peak + jnp.log(row_totals)
    softmax_low = (raised / row_totals).astype(jnp.bfloat16)
    attended = jnp.einsum(
        "ghqk,gkhe->gqhe", softmax_low, value_heads, preferred_element_type=jnp.float32
    )
    attended = attended.reshape(total_rows, model_width).astype(jnp.bfloat16)
    attn_out = jnp.dot(attended, w_proj, preferred_element_type=jnp.float32) + b_proj
    middle = input_rows + keep_column * attn_out
    hidden_in, scaled_two, inverse_two = norm_rows(middle, ln2_gain, ln2_bias)
    hidden_low = hidden_in.astype(jnp.bfloat16)
    whole_rows = lax.all_gather(hidden_low, "mlp", axis=0, tiled=True)
    pre_act = jnp.dot(whole_rows, w_fc1, preferred_element_type=jnp.float32) + b_fc1
    activation, gelu_pull = jax.vjp(exact_gelu, pre_act)
    act_low = activation.astype(jnp.bfloat16)
    row_piece = act_low
    mlp_out = (
        lax.psum_scatter(
            jnp.dot(row_piece, w_fc2, preferred_element_type=jnp.float32).astype(jnp.bfloat16),
            "mlp",
            scatter_dimension=0,
            tiled=True,
        ).astype(jnp.float32)
        + b_fc2
    )
    block_output = middle + keep_column * mlp_out
    stream_sq = jnp.sum(keep_column * block_output * block_output)
    attn_sq = jnp.sum(keep_column * attn_out * attn_out)
    mlp_sq = jnp.sum(keep_column * mlp_out * mlp_out)
    counted = jnp.sum(keep_column)
    stream_sq, attn_sq, mlp_sq, counted = lax.psum(
        (stream_sq, attn_sq, mlp_sq, counted), ("img", "mlp")
    )
    grad_out = cotangent.reshape(total_rows, model_width).astype(jnp.float32)
    grad_mlp = (keep_column * grad_out).astype(jnp.bfloat16)
    grad_b_two = row_total(grad_mlp)
    whole_grad = lax.all_gather(grad_mlp, "mlp", axis=0, tiled=True)
    grad_act = jnp.dot(whole_grad, w_fc2.T, preferred_element_type=jnp.float32).astype(jnp.bfloat16)
    part_w_two = jnp.einsum("rf,rd->fd", act_low, whole_grad, preferred_element_type=jnp.float32)
    grad_pre = gelu_pull(grad_act.astype(jnp.float32))[0].astype(jnp.bfloat16)
    part_w_one = jnp.einsum("rd,rf->df", whole_rows, grad_pre, preferred_element_type=jnp.float32)
    part_b_one = row_total(grad_pre)
    row_piece = grad_pre
    grad_hidden = lax.psum_scatter(
        jnp.dot(row_piece, w_fc1.T, preferred_element_type=jnp.float32).astype(jnp.bfloat16),
        "mlp",
        scatter_dimension=0,
        tiled=True,
    ).astype(jnp.float32)
    sum_w_one, sum_b_one, sum_w_two = lax.psum((part_w_one, part_b_one, part_w_two), "img")
    grad_middle_part, grad_gain_two, grad_bias_two = norm_back(
        grad_hidden, scaled_two, inverse_two, ln2_gain
    )
    grad_middle = grad_out + grad_middle_part
    grad_attn = (keep_column * grad_middle).astype(jnp.bfloat16)
    grad_b_proj = row_total(grad_attn)
    grad_w_proj = jnp.einsum("rd,re->de", attended, grad_attn, preferred_element_type=jnp.float32)
    grad_attended = jnp.dot(grad_attn, w_proj.T, preferred_element_type=jnp.float32)
    grad_attended = grad_attended.astype(jnp.bfloat16).reshape(head_shape)
    scores_again = attention_scores(query_heads, key_heads)
    probs_again = jnp.exp(scores_again - log_total)
    probs_again_low = probs_again.astype(jnp.bfloat16)
    grad_value = jnp.einsum(
        "ghqk,gqhe->gkhe", probs_again_low, grad_attended, preferred_element_type=jnp.float32
    ).astype(jnp.bfloat16)
    grad_probs = round_trip(
        jnp.einsum(
            "gqhe,gkhe->ghqk", grad_attended, value_heads, preferred_element_type=jnp.float32
        )
    )
    grad_scores = probs_again * (
        grad_probs - jnp.sum(probs_again * grad_probs, axis=3, keepdims=True)
    )
    grad_scores = grad_scores.astype(jnp.bfloat16) * score_scale
    grad_query = jnp.einsum(
        "ghqk,gkhe->gqhe", grad_scores, key_heads, preferred_element_type=jnp.float32
    ).astype(jnp.bfloat16)
    grad_key = jnp.einsum(
        "ghqk,gqhe->gkhe", grad_scores, query_heads, preferred_element_type=jnp.float32
    ).astype(jnp.bfloat16)
    grad_query = grad_query.reshape(total_rows, model_width)
    grad_key = grad_key.reshape(total_rows, model_width)
    grad_value = grad_value.reshape(total_rows, model_width)
    grad_joined = jnp.concatenate([grad_query, grad_key, grad_value], axis=1)
    grad_bias_q = row_total(grad_query)
    grad_bias_v = row_total(grad_value)
    grad_w_qkv = jnp.einsum(
        "rd,rc->dc", normed_low, grad_joined, preferred_element_type=jnp.float32
    )
    grad_normed = jnp.dot(grad_joined, w_qkv.T, preferred_element_type=jnp.float32)
    grad_input_part, grad_gain_one, grad_bias_one = norm_back(
        grad_normed, scaled_one, inverse_one, ln1_gain
    )
    grad_images = (grad_middle + grad_input_part).reshape(image_count, patches, model_width)
    (
        sum_w_qkv,
        sum_bias_q,
        sum_bias_v,
        sum_w_proj,
        sum_b_proj,
        sum_gain_one,
        sum_bias_one,
        sum_gain_two,
        sum_bias_two,
        sum_b_two,
    ) = lax.psum(
        (
            grad_w_qkv,
            grad_bias_q,
            grad_bias_v,
            grad_w_proj,
            grad_b_proj,
            grad_gain_one,
            grad_bias_one,
            grad_gain_two,
            grad_bias_two,
            grad_b_two,
        ),
        ("img", "mlp"),
    )
    root_means = jnp.sqrt(jnp.stack([stream_sq, attn_sq, mlp_sq]) / (counted * model_width))
    layer_out = block_output.reshape(image_count, patches, model_width).astype(jnp.bfloat16)
    return (
        layer_out,
        grad_images,
        sum_gain_one,
        sum_bias_one,
        sum_w_qkv,
        sum_bias_q,
        sum_bias_v,
        sum_w_proj,
        sum_b_proj,
        sum_gain_two,
        sum_bias_two,
        sum_w_one,
        sum_b_one,
        sum_w_two,
        sum_b_two,
        root_means,
    )


def solution(mesh):
    return jax.shard_map(
        on_device,
        mesh=mesh,
        in_specs=(
            P(("img", "mlp"), None, None),
            P(("img", "mlp"), None),
            P(),
            P(),
            P(),
            P(),
            P(),
            P(),
            P(),
            P(),
            P(),
            P(None, "mlp"),
            P("mlp"),
            P("mlp", None),
            P(),
            P(("img", "mlp"), None, None),
        ),
        out_specs=(
            P(("img", "mlp"), None, None),
            P(("img", "mlp"), None, None),
            P(),
            P(),
            P(),
            P(),
            P(),
            P(),
            P(),
            P(),
            P(),
            P(None, "mlp"),
            P("mlp"),
            P("mlp", None),
            P(),
            P(),
        ),
        check_vma=False,
    )
```

profile of v0, /device:TPU:0, one launch (start us, length us, event | category | flops | bytes accessed | tf_op | source)
XLA Modules:
  0.0 860.4 jit_solution(18269459985343117664)
XLA Ops:
  40.5 6.0 copy.69
  64.0 6.0 copy.71
  102.3 13.5 %all-gather.5.cloned.1.call-done = bf16[2,985,768]{2,1,0:T(8,128)(2,1)} async-done(((bf16[1,985,768]{2,1,0:T(8,128)(2,1)}), bf16[2,985,768]{2,1,0:T(8,128)(2,1)}) %all-gather.5.cloned.1.call-update) | async-done | bytes 3025936 | tf_op jit(solution)/shard_map/all_gather | solution.py:97
  119.8 33.8 %multiply_convert_fusion = (bf16[1970,1536]{1,0:T(8,128)(2,1)}, f32[1970,1536]{1,0:T(8,128)}, f32[1970,1536]{1,0:T(8,128)}) fusion(f32[1536]{0:T(1024)} %convert_element_type.167, bf16[1970,768]{1,0:T(8,128)(2,1)} %reshape.167, bf16[768,1536]{1,0:T(8,128)(2,1)} %param.27), kind=kOutput, calls=%fused_computation.21 | convolution fusion | flops 4847523840 | bytes 35650560 | tf_op jit(solution)/shard_map/dot_general | solution.py:98
  157.7 17.3 %convert_reduce_fusion = (f32[1536]{0:T(1024)}, bf16[1970,1536]{1,0:T(8,128)(2,1)}) fusion(f32[1970,1536]{1,0:T(8,128)} %get-tuple-element.51, bf16[1970,768]{1,0:T(8,128)(2,1)} %reshape.169, bf16[1536,768]{1,0:T(8,128)(2,1)} %param.29, f32[1970,1536]{1,0:T(8,128)} %get-tuple-element.66, f32[1536]{0:T(1024)} %convert_element_type.167), kind=kOutput, calls=%fused_computation.20 | convolution fusion | flops 4705304064 | bytes 35656704 | tf_op jit(solution)/shard_map/dot_general | solution.py:123
  175.0 9.4 %convolution_convert_fusion.2 = bf16[1970,768]{1,0:T(8,128)(2,1)} fusion(bf16[1970,1536]{1,0:T(8,128)(2,1)} %get-tuple-element.73, bf16[768,1536]{1,0:T(8,128)(2,1)S(1)} %copy-done.49), kind=kOutput, calls=%fused_computation.61 | convolution fusion | flops 4649326080 | bytes 11437056 | tf_op jit(solution)/shard_map/dot_general | solution.py:130
  184.4 6.4 convolution_convert_fusion.3
  190.8 11.5 %fusion.61 = (bf16[992,768]{1,0:T(8,128)(2,1)}, bf16[992,768]{1,0:T(8,128)(2,1)}) fusion(bf16[1970,768]{1,0:T(8,128)(2,1)} %convolution_convert_fusion.3, bf16[1970,768]{1,0:T(8,128)(2,1)} %convolution_convert_fusion.2), kind=kCustom, calls=%all-reduce-scatter.2 | all-reduce-scatter fusion | flops 3047425 | bytes 9099776
  213.5 9.1 %concatenate.5 = bf16[999,768]{1,0:T(8,128)(2,1)} concatenate(bf16[7,768]{1,0:T(8,128)(2,1)} %collective-permute-done.1, bf16[992,768]{1,0:T(8,128)(2,1)} %get-tuple-element.46), dimensions={0} | concatenate | bytes 3068928
  222.6 9.0 %concatenate.4 = bf16[999,768]{1,0:T(8,128)(2,1)} concatenate(bf16[7,768]{1,0:T(8,128)(2,1)} %collective-permute-done, bf16[992,768]{1,0:T(8,128)(2,1)} %get-tuple-element.45), dimensions={0} | concatenate | bytes 3068928
  231.6 8.7 %fusion.39 = (f32[]{:T(128)}, f32[]{:T(128)}, bf16[985,768]{1,0:T(8,128)(2,1)}, f32[768]{0:T(1024)}, f32[985]{0:T(1024)S(1)}, /*index=5*/f32[]{:T(128)}, f32[985]{0:T(1024)S(1)}, f32[768]{0:T(1024)}) fusion(f32[985,768]{1,0:T(8,128)} %copy-done.12, f32[768]{0:T(1024)} %copy-done.28, f32[985]{0:T(1024)S(1)} %copy-done.26, f32[768]{0:T(1024)} %convert_element_type.171, ...), kind=kLoop, calls=%fused_computation.72 | loop fusion | flops 18152012 | bytes 10625796 | tf_op jit(solution)/shard_map/reduce_sum | solution.py:113
  261.0 6.7 convolution_convert_fusion.1
  267.8 8.7 %convert_reduce_fusion.2 = (f32[12,64]{1,0:T(8,128)}, bf16[5,197,12,64]{1,3,2,0:T(8,128)(2,1)}) fusion(bf16[5,197,12,64]{1,3,2,0:T(8,128)(2,1)S(1)} %copy-done.9, f32[5,12,197,197]{2,3,1,0:T(8,128)} %copy-done.1, f32[5,12,197]{2,1,0:T(8,128)S(1)} %copy-done.21), kind=kOutput, calls=%fused_computation.58 | convolution fusion | flops 304978880 | bytes 12390432 | tf_op jit(solution)/shard_map/ghqk,gqhe->gkhe/dot_general | solution.py:148
  276.4 19.6 %convert_bitcast_fusion.1 = bf16[5,197,12,64]{1,3,2,0:T(8,128)(2,1)} fusion(bf16[5,197,12,64]{1,3,2,0:T(8,128)(2,1)} %copy.69, bf16[5,12,197,197]{2,3,1,0:T(8,128)(2,1)} %convolution_convert_fusion.1, f32[5,12,197,197]{2,3,1,0:T(8,128)} %copy-done.1, f32[5,12,197]{2,1,0:T(8,128)} %log_add_fusion), kind=kOutput, calls=%fused_computation.95 | convolution fusion | flops 326764096 | bytes 17044440 | tf_op jit(solution)/shard_map/ghqk,gqhe->gkhe/dot_general | solution.py:163
  296.1 17.5 %convert_reduce_fusion.3 = (f32[12,64]{1,0:T(8,128)}, bf16[5,197,12,64]{1,3,2,0:T(8,128)(2,1)}) fusion(bf16[5,197,12,64]{1,3,2,0:T(8,128)(2,1)} %copy.70, bf16[5,12,197,197]{2,3,1,0:T(8,128)(2,1)} %convolution_convert_fusion.1, f32[5,12,197,197]{2,3,1,0:T(8,128)} %copy-done.1, f32[5,12,197]{2,1,0:T(8,128)} %log_add_fusion), kind=kOutput, calls=%fused_computation.59 | convolution fusion | flops 328276288 | bytes 17047512 | tf_op jit(solution)/shard_map/ghqk,gkhe->gqhe/dot_general | solution.py:160
  351.4 9.0 %fusion.59 = f32[768,2304]{1,0:T(8,128)} fusion(bf16[985,2304]{0,1:T(8,128)(2,1)} %constant_dynamic-update-slice_fusion, f32[985,768]{1,0:T(8,128)S(1)} %copy-done.5, f32[768]{0:T(1024)S(1)} %copy-done.52, f32[768]{0:T(1024)S(1)} %copy-done.44, f32[985]{0:T(1024)S(1)} %copy-done.34, f32[985]{0:T(1024)S(1)} %copy-done.31), kind=kOutput, calls=%fused_computation.123 | convolution fusion | flops 3489642240 | bytes 14656712 | tf_op jit(solution)/shard_map/rd,rc->dc/dot_general | solution.py:172
  360.5 9.7 %fusion.68 = f32[768,1536]{1,0:T(8,128)} fusion(bf16[1970,768]{1,0:T(8,128)(2,1)} %reshape.167, bf16[1970,1536]{1,0:T(8,128)(2,1)} %get-tuple-element.73), kind=kOutput, calls=%fused_computation.129 | convolution fusion | flops 4647813120 | bytes 13796352 | tf_op jit(solution)/shard_map/rd,rf->df/dot_general | solution.py:126
  370.2 8.7 %fusion.69 = f32[1536,768]{1,0:T(8,128)} fusion(bf16[1970,1536]{1,0:T(8,128)(2,1)} %get-tuple-element.50, bf16[1970,768]{1,0:T(8,128)(2,1)S(1)} %copy-done.16), kind=kOutput, calls=%fused_computation.130 | convolution fusion | flops 4647813120 | bytes 13796352 | tf_op jit(solution)/shard_map/rf,rd->fd/dot_general | solution.py:124
  382.7 45.3 %psum.129 = f32[1536]{0:T(1024)} all-reduce(f32[1536]{0:T(1024)} %get-tuple-element.72), channel_id=1, replica_groups=mesh['img'=16,'mlp'=2] {'img'}, use_global_device_ids=true, to_apply=%region_31.32 | all-reduce | flops 1536 | bytes 12288 | tf_op jit(solution)/shard_map/psum | solution.py:135
  433.0 9.1 %multiply_reduce_fusion.1 = (f32[768]{0:T(1024)}, f32[985]{0:T(1024)S(1)}, f32[985]{0:T(1024)S(1)}, f32[768]{0:T(1024)}, f32[985,768]{1,0:T(8,128)S(1)}) fusion(f32[985,768]{1,0:T(8,128)} %reshape.164, f32[985]{0:T(1024)S(1)} %copy-done.35, f32[985]{0:T(1024)S(1)} %copy-done.32, f32[768]{0:T(1024)} %param.18, ...), kind=kOutput, calls=%fused_computation.82 | convolution fusion | flops 3492664576 | bytes 14154640 | tf_op jit(solution)/shard_map/dot_general | solution.py:175
  448.5 39.1 %all-reduce.4 = (f32[768]{0:T(1024)}, f32[768]{0:T(1024)}, f32[768]{0:T(1024)}, f32[768]{0:T(1024)}, f32[768]{0:T(1024)}, /*index=5*/f32[768]{0:T(1024)}, f32[76...) all-reduce(f32[768]{0:T(1024)} %get-tuple-element.16, ...), channel_id=1, replica_groups=mesh['img'=16,'mlp'=2] {'img','mlp'}, use_global_device_ids=true, to_apply=%region_14.15 | all-reduce | flops 6148 | bytes 49184 | tf_op jit(solution)/shard_map/psum | solution.py:191
  490.7 63.8 %all-reduce.11.cloned.1.call-done = (f32[768,2304]{1,0:T(8,128)}, f32[768,768]{1,0:T(8,128)}) async-done(((f32[768,2304]{1,0:T(8,128)}, f32[768,768]{1,0:T(8,128)}), (f32[768,2304]{1,0:T(8,128)}, f32[768,768]{1,0:T(8,128)})) %all-reduce.11.cloned.1.call-update) | async-done | bytes 9437200 | tf_op jit(solution)/shard_map/psum | solution.py:191
  554.5 285.4 %all-reduce.13.cloned.1.call-done = (f32[768,1536]{1,0:T(8,128)}, f32[1536,768]{1,0:T(8,128)}) async-done(((f32[768,1536]{1,0:T(8,128)}, f32[1536,768]{1,0:T(8,128)}), (f32[768,1536]{1,0:T(8,128)}, f32[1536,768]{1,0:T(8,128)})) %all-reduce.13.cloned.1.call-update) | async-done | bytes 9437200 | tf_op jit(solution)/shard_map/psum | solution.py:135
  839.9 6.6 copy.106
  (194 shorter events, 184.9 us)
Async XLA Ops:
  7.2 18.0 %copy-start = (bf16[768,2304]{1,0:T(8,128)(2,1)S(1)}, bf16[768,2304]{1,0:T(8,128)(2,1)}, u32[]{:S(2)}) copy-start(bf16[768,2304]{1,0:T(8,128)(2,1)} %param.20) | copy-start | bytes 10616836
  7.2 108.5 %all-gather.5.cloned.1.call-start = ((), (), s32[]{:S(2)}) async-start(), calls=%async_computation | async-start | bytes 4571136 | tf_op jit(solution)/shard_map/all_gather | solution.py:97
  9.4 10.9 %copy-start.22 = (f32[5,197]{1,0:T(8,128)}, f32[5,197]{1,0:T(8,128)S(1)}, u32[]{:S(2)}) copy-start(f32[5,197]{1,0:T(8,128)S(1)} %convert_element_type.154) | copy-start | bytes 11824
  17.7 77.3 %copy-start.28 = (f32[768]{0:T(1024)}, f32[768]{0:T(1024)S(1)}, u32[]{:S(2)}) copy-start(f32[768]{0:T(1024)S(1)} %convert_element_type.165) | copy-start | bytes 9220
  20.4 74.7 %copy-start.25 = (f32[985]{0:T(1024)}, f32[985]{0:T(1024)S(1)}, u32[]{:S(2)}) copy-start(f32[985]{0:T(1024)S(1)} %mul.196) | copy-start | bytes 11824
  100.9 52.7 %all-gather.7.cloned.1.call-start = ((), (), s32[]{:S(2)}) async-start(), calls=%async_computation.1 | async-start | bytes 4571136 | tf_op jit(solution)/shard_map/all_gather | solution.py:122
  101.6 452.9 %all-reduce.11.cloned.1.call-start = ((), (), s32[]{:S(2)}) async-start(), calls=%async_computation.2 | async-start | bytes 18874368 | tf_op jit(solution)/shard_map/psum | solution.py:191
  157.7 17.3 %copy-start.49 = (bf16[768,1536]{1,0:T(8,128)(2,1)S(1)}, bf16[768,1536]{1,0:T(8,128)(2,1)}, u32[]{:S(2)}) copy-start(bf16[768,1536]{1,0:T(8,128)(2,1)} %param.27) | copy-start | bytes 7077892
  175.0 9.4 %copy-start.50 = (bf16[1536,768]{1,0:T(8,128)(2,1)S(1)}, bf16[1536,768]{1,0:T(8,128)(2,1)}, u32[]{:S(2)}) copy-start(bf16[1536,768]{1,0:T(8,128)(2,1)} %param.29) | copy-start | bytes 7077892
  175.0 9.4 %copy-start.53 = (bf16[1970,1536]{1,0:T(8,128)(2,1)S(1)}, bf16[1970,1536]{1,0:T(8,128)(2,1)}, u32[]{:S(2)}) copy-start(bf16[1970,1536]{1,0:T(8,128)(2,1)} %get-tuple-element.50) | copy-start | bytes 18155524
  190.8 22.1 %copy-start.48 = (bf16[768]{0:T(1024)(128)(2,1)S(1)}, bf16[768]{0:T(1024)(128)(2,1)}, u32[]{:S(2)}) copy-start(bf16[768]{0:T(1024)(128)(2,1)} %param.30) | copy-start | bytes 4612
  204.8 8.7 %collective-permute-start.1 = (bf16[7,768]{1,0:T(8,128)(2,1)}, bf16[7,768]{1,0:T(8,128)(2,1)}, u32[]{:S(2)}, u32[]{:S(2)}) collective-permute-start(bf16[7,768]{1,0:T(8,128)(2,1)} %slice.17), channel_id=1, source_target_pairs={{0,1},{2,3},{4,5},{6,7},{8,9},{10,11},{12,13},{14,15},{16,17},{18,... | collective-permute-start | bytes 32264
  207.5 15.0 %collective-permute-start = (bf16[7,768]{1,0:T(8,128)(2,1)}, bf16[7,768]{1,0:T(8,128)(2,1)}, u32[]{:S(2)}, u32[]{:S(2)}) collective-permute-start(bf16[7,768]{1,0:T(8,128)(2,1)} %slice.16), channel_id=1, source_target_pairs={{0,1},{2,3},{4,5},{6,7},{8,9},{10,11},{12,13},{14,15},{16,17},{18,... | collective-permute-start | bytes 32264
  213.5 18.1 %copy-start.26 = (f32[985]{0:T(1024)S(1)}, f32[985]{0:T(1024)}, u32[]{:S(2)}) copy-start(f32[985]{0:T(1024)} %copy-done.25) | copy-start | bytes 11824
  231.6 8.7 %copy-start.3 = (f32[985,768]{1,0:T(8,128)S(1)}, f32[985,768]{1,0:T(8,128)}, u32[]{:S(2)}) copy-start(f32[985,768]{1,0:T(8,128)} %copy-done.2) | copy-start | bytes 9077764
  231.6 8.7 %copy-start.8 = (f32[985,768]{1,0:T(8,128)S(1)}, f32[985,768]{1,0:T(8,128)}, u32[]{:S(2)}) copy-start(f32[985,768]{1,0:T(8,128)} %reshape.165) | copy-start | bytes 9077764
  360.5 479.5 %all-reduce.13.cloned.1.call-start = ((), (), s32[]{:S(2)}) async-start(), calls=%async_computation.3 | async-start | bytes 18874368 | tf_op jit(solution)/shard_map/psum | solution.py:135
  360.5 9.7 %copy-start.16 = (bf16[1970,768]{1,0:T(8,128)(2,1)S(1)}, bf16[1970,768]{1,0:T(8,128)(2,1)}, u32[]{:S(2)}) copy-start(bf16[1970,768]{1,0:T(8,128)(2,1)} %reshape.169) | copy-start | bytes 9077764
  380.3 50.7 %copy-start.29 = (f32[12,64]{1,0:T(8,128)S(1)}, f32[12,64]{1,0:T(8,128)}, u32[]{:S(2)}) copy-start(f32[12,64]{1,0:T(8,128)} %get-tuple-element.70) | copy-start | bytes 9220
  382.7 50.3 %copy-start.32 = (f32[985]{0:T(1024)S(1)}, f32[985]{0:T(1024)}, u32[]{:S(2)}) copy-start(f32[985]{0:T(1024)} %div.41) | copy-start | bytes 11824
  382.7 50.3 %copy-start.35 = (f32[985]{0:T(1024)S(1)}, f32[985]{0:T(1024)}, u32[]{:S(2)}) copy-start(f32[985]{0:T(1024)} %rsqrt.20) | copy-start | bytes 11824
  433.0 9.1 %copy-start.6 = (f32[985,768]{1,0:T(8,128)S(1)}, f32[985,768]{1,0:T(8,128)}, u32[]{:S(2)}) copy-start(f32[985,768]{1,0:T(8,128)} %reshape.164) | copy-start | bytes 9077764
  433.0 9.1 %copy-start.11 = (f32[985,768]{1,0:T(8,128)S(1)}, f32[985,768]{1,0:T(8,128)}, u32[]{:S(2)}) copy-start(f32[985,768]{1,0:T(8,128)} %get-tuple-element.49) | copy-start | bytes 9077764
  433.0 9.1 %copy-start.45 = (f32[768]{0:T(1024)S(1)}, f32[768]{0:T(1024)}, u32[]{:S(2)}) copy-start(f32[768]{0:T(1024)} %param.18) | copy-start | bytes 9220
  (38 other events, 163.8 us)
Sparse Core Ops, SparseCore 0:
  101.0 14.6 all-gather.4
  117.9 13.1 all-gather.6
  360.6 193.8 all-reduce.10
  561.3 278.6 all-reduce.12
where the time goes:
time: 874 us; the launch traced here: 860 us
  waiting for transfers between devices  363 us (42%)
  matrix products  178 us (20%)
  local copies, waits for them, and re-layouts  161 us (18%)
  blocking collectives  95.9 us (11%)
  other arithmetic  41.9 us (5%)
  between operations  15.7 us (2%)
    psum x1, waiting for transfers between devices, on_device(): lax.psum((part_w_one, part_b_one, part_w_two), 'img')  285 us
    psum x1, waiting for transfers between devices, on_device(): lax.psum((grad_w_qkv, grad_bias_q, grad_bias_v, grad_w_proj, grad_b_proj,...  63.8 us
    unnamed x125, local copies, waits for them, and re-layouts  53.9 us
    psum x1, blocking collectives, on_device(): lax.psum((part_w_one, part_b_one, part_w_two), 'img')  45.3 us
    psum x1, blocking collectives, on_device(): lax.psum((grad_w_qkv, grad_bias_q, grad_bias_v, grad_w_proj, grad_b_proj,...  39.1 us
    dot_general x1, matrix products, on_device(): jnp.dot(whole_rows, w_fc1, preferred_element_type=jnp.float32) + b_fc1  33.8 us
    dot_general x1, matrix products, on_device(): jnp.einsum('ghqk,gqhe->gkhe', grad_scores, query_heads, preferred_element...  19.6 us
    dot_general x1, matrix products, on_device(): jnp.einsum('ghqk,gkhe->gqhe', grad_scores, key_heads, preferred_element_t...  17.5 us
  transfers between devices with their start and end apart: 6, of which 3 were waited for; matrix products, arithmetic and copies ran while one was open for 11% of the time, Pallas kernels for 0%

commit v1 on v0

v1 whole, which is shorter than its diff:
```python
import functools

import jax
import jax.numpy as jnp
from jax import lax
from jax.experimental import pallas as pl
from jax.experimental.pallas import tpu as pltpu
from jax.sharding import PartitionSpec as P

HEAD_DIM = 64
NORM_EPS = 1e-06
F32 = jnp.float32
BF16 = jnp.bfloat16
ERFC_POLY = (
    -0.05792342897865154,
    0.27982426175045266,
    -0.47905523971588865,
    0.27061712140601424,
    -0.022718349995155727,
    0.2015184791612061,
    0.24328701077158832,
    0.2823637910445855,
    0.2820864086305586,
)


def dot(a, b):
    return jnp.dot(a, b, preferred_element_type=F32)


def dot_t(a, b):
    return lax.dot_general(a, b, (((1,), (1,)), ((), ())), preferred_element_type=F32)


def t_dot(a, b):
    return lax.dot_general(a, b, (((0,), (0,)), ((), ())), preferred_element_type=F32)


def slots_of(patches):
    most = 4 * patches // 5
    return -(-most // 16) * 16


def norm_rows(rows):
    center = rows - jnp.mean(rows, axis=1, keepdims=True)
    inverse = lax.rsqrt(jnp.mean(center * center, axis=1, keepdims=True) + NORM_EPS)
    return center * inverse, inverse


def norm_back(weighted, scaled, inverse):
    return inverse * (
        weighted
        - jnp.mean(weighted, axis=1, keepdims=True)
        - scaled * jnp.mean(weighted * scaled, axis=1, keepdims=True)
    )


def gelu_pair(values):
    reach = jnp.abs(values) * 0.7071067811865476
    inv = 1.0 / (1.0 + 0.5 * reach)
    decay = jnp.exp(-0.5 * (values * values))
    poly = jnp.full_like(values, ERFC_POLY[0])
    for coefficient in ERFC_POLY[1:]:
        poly = poly * inv + coefficient
    tail = (0.5 * inv) * poly * decay
    share = jnp.where(values > 0, 1.0 - tail, tail)
    return values * share, share + values * (decay * 0.3989422804014327)


def forward_kernel(
    slots,
    keep_ref, img_ref, cot_ref, g1_ref, b1_ref, wqkv_ref, bq_ref, bv_ref, wproj_ref, bproj_ref, g2_ref, b2_ref,
    sel_ref, x_ref, normed_ref, qkv_ref, probs_ref, att_ref, mid_ref, hid_ref, gm_ref, sums_ref,
):
    patches, width = img_ref.shape[1:]
    heads = width // HEAD_DIM
    keep = keep_ref[0].astype(F32)
    upto = lax.broadcasted_iota(jnp.int32, (patches, patches), 0) <= lax.broadcasted_iota(
        jnp.int32, (patches, patches), 1
    )
    keep8 = jnp.broadcast_to(keep, (8, patches)).astype(BF16)
    rank = dot(keep8, upto.astype(F32).astype(BF16))[0:1]
    count = jnp.sum(keep, axis=1, keepdims=True)
    slot = lax.broadcasted_iota(jnp.int32, (slots, patches), 0).astype(F32)
    sel = jnp.where((slot == rank - 1.0) & (keep > 0), 1.0, 0.0).astype(BF16)
    sel_ref[0] = sel
    gm_ref[...] = dot(sel, cot_ref[0]).astype(BF16)
    rows = dot(sel, img_ref[0])
    x_ref[...] = rows.astype(BF16)
    scaled, _ = norm_rows(rows)
    normed = (scaled * g1_ref[...] + b1_ref[...]).astype(BF16)
    normed_ref[...] = normed
    for part in range(3):
        cols = slice(part * width, (part + 1) * width)
        block = dot(normed, wqkv_ref[:, cols])
        if part == 0:
            block = block + bq_ref[...].astype(F32)
        if part == 2:
            block = block + bv_ref[...].astype(F32)
        qkv_ref[:, cols] = block.astype(BF16)
    closed = jnp.where(
        lax.broadcasted_iota(jnp.int32, (1, slots), 1).astype(F32) < count, 0.0, -1e30
    )
    first = lax.broadcasted_iota(jnp.int32, (1, 2 * HEAD_DIM), 1) < HEAD_DIM
    zero = jnp.zeros((), BF16)
    for pair in range(heads // 2):
        lanes = slice(pair * 128, pair * 128 + 128)
        query = qkv_ref[:, lanes] * jnp.asarray(HEAD_DIM ** -0.5, BF16)
        key = qkv_ref[:, width + pair * 128 : width + pair * 128 + 128]
        value = qkv_ref[:, 2 * width + pair * 128 : 2 * width + pair * 128 + 128]
        total = None
        for half in range(2):
            mine = first if half == 0 else jnp.logical_not(first)
            scores = dot_t(query, jnp.where(mine, key, zero)) + closed
            raised = jnp.exp(scores - jnp.max(scores, axis=1, keepdims=True))
            probs = (raised * (1.0 / jnp.sum(raised, axis=1, keepdims=True))).astype(BF16)
            probs_ref[0, 2 * pair + half] = probs
            term = dot(probs, jnp.where(mine, value, zero))
            total = term if total is None else total + term
        att_ref[:, lanes] = total.astype(BF16)
    attn_out = dot(att_ref[...], wproj_ref[...]) + bproj_ref[...].astype(F32)
    valid = lax.broadcasted_iota(jnp.int32, (slots, 1), 0).astype(F32) < count
    attn_kept = jnp.where(valid, attn_out, 0.0)
    middle = rows + attn_kept
    mid_ref[...] = middle
    sums_ref[0, 0:1] = jnp.sum(attn_kept * attn_kept, axis=0, keepdims=True)
    sums_ref[0, 1:2] = jnp.broadcast_to(count, (1, width))
    scaled, _ = norm_rows(middle)
    hid_ref[...] = (scaled * g2_ref[...] + b2_ref[...]).astype(BF16)


def mlp_kernel(hid_ref, gm_ref, w1_ref, b1_ref, w2_ref, out_ref, gh_ref, dw1_ref, dw2_ref, db1_ref):
    step = pl.program_id(0)
    hid, gm = hid_ref[...], gm_ref[...]
    w1, w2 = w1_ref[0], w2_ref[0]
    pre = dot(hid, w1) + b1_ref[0].astype(F32)
    act, slope = gelu_pair(pre)
    act = act.astype(BF16)
    grad_act = dot_t(gm, w2).astype(BF16).astype(F32)
    grad_pre_f = grad_act * slope
    grad_pre = grad_pre_f.astype(BF16)
    dw2_ref[0] = t_dot(act, gm).astype(BF16)
    dw1_ref[0] = t_dot(hid, grad_pre).astype(BF16)
    db1_ref[0] = jnp.sum(grad_pre.astype(F32), axis=0, keepdims=True)

    @pl.when(step == 0)
    def _():
        out_ref[...] = dot(act, w2)
        gh_ref[...] = dot_t(grad_pre, w1)

    @pl.when(step > 0)
    def _():
        out_ref[...] += dot(act, w2)
        gh_ref[...] += dot_t(grad_pre, w1)


def backward_kernel(
    images, slots, groups,
    sel_ref, x_ref, normed_ref, qkv_ref, probs_ref, att_ref, mid_ref, gm_ref, gh_ref, mlp_ref, valid_ref,
    g1_ref, g2_ref, bfc2_ref, wqkv_ref, wproj_ref, img_ref, cot_ref,
    lo_ref, gi_ref, dwp_ref, dwq_ref, vec_ref,
    gmid_ref, gatt_ref, gq_ref, gk_ref, gv_ref, gn_ref,
):
    step = pl.program_id(0)
    rows, width = x_ref.shape

    @pl.when(step == 0)
    def _():
        middle = mid_ref[...]
        valid = valid_ref[...] > 0
        mlp_out = jnp.where(valid, mlp_ref[...] + bfc2_ref[...].astype(F32), 0.0)
        block = middle + mlp_out
        kept = jnp.where(valid, block, 0.0)
        vec_ref[8:9] = jnp.sum(kept * kept, axis=0, keepdims=True)
        vec_ref[9:10] = jnp.sum(mlp_out * mlp_out, axis=0, keepdims=True)
        low = block.astype(BF16)
        for i in range(images):
            put = t_dot(sel_ref[i], low[i * slots : (i + 1) * slots])
            here = jnp.sum(sel_ref[i].astype(F32), axis=0, keepdims=True)
            lo_ref[i] = put.astype(BF16)
        scaled, inverse = norm_rows(middle)
        grad_hidden = gh_ref[...]
        vec_ref[0:1] = jnp.sum(grad_hidden * scaled, axis=0, keepdims=True)
        vec_ref[1:2] = jnp.sum(grad_hidden, axis=0, keepdims=True)
        gm = gm_ref[...].astype(F32)
        vec_ref[2:3] = jnp.sum(gm, axis=0, keepdims=True)
        grad_middle = gm + norm_back(grad_hidden * g2_ref[...], scaled, inverse)
        gmid_ref[...] = grad_middle
        grad_attn = grad_middle.astype(BF16)
        vec_ref[3:4] = jnp.sum(grad_attn.astype(F32), axis=0, keepdims=True)
        dwp_ref[...] = t_dot(att_ref[...], grad_attn).astype(BF16)
        gatt_ref[...] = dot_t(grad_attn, wproj_ref[...]).astype(BF16)
        gn_ref[...] = jnp.zeros_like(gn_ref)

    first = lax.broadcasted_iota(jnp.int32, (1, 2 * HEAD_DIM), 1) < HEAD_DIM
    zero = jnp.zeros((), BF16)
    scale = jnp.asarray(HEAD_DIM ** -0.5, BF16)
    pairs = width // 128 // groups
    for group in range(groups):

        @pl.when(step == group + 1)
        def _():
            base = group * pairs * 128

            @pl.loop(0, images)
            def _(i):
                here = pl.ds(pl.multiple_of(i * slots, 16), slots)
                for pair in range(pairs):
                    at = base + pair * 128
                    own = slice(pair * 128, pair * 128 + 128)
                    query = qkv_ref[here, at : at + 128]
                    key = qkv_ref[here, width + at : width + at + 128]
                    value = qkv_ref[here, 2 * width + at : 2 * width + at + 128]
                    grad_att = gatt_ref[here, at : at + 128]
                    gq = gk = gv = None
                    for half in range(2):
                        mine = first if half == 0 else jnp.logical_not(first)
                        low = probs_ref[i, 2 * (base // 128 + pair) + half]
                        probs = low.astype(F32)
                        g_mine = jnp.where(mine, grad_att, zero)
                        grad_probs = dot_t(g_mine, value).astype(BF16).astype(F32)
                        inner = jnp.sum(probs * grad_probs, axis=1, keepdims=True)
                        grad_scores = (probs * (grad_probs - inner)).astype(BF16) * scale
                        tv = t_dot(low, g_mine)
                        tq = dot(grad_scores, jnp.where(mine, key, zero))
                        tk = t_dot(grad_scores, jnp.where(mine, query, zero))
                        gq = tq if gq is None else gq + tq
                        gk = tk if gk is None else gk + tk
                        gv = tv if gv is None else gv + tv
                    gq_ref[here, own] = gq.astype(BF16)
                    gk_ref[here, own] = gk.astype(BF16)
                    gv_ref[here, own] = gv.astype(BF16)

            span = pairs * 128
            vec_ref[4:5, base : base + span] = jnp.sum(gq_ref[...].astype(F32), axis=0, keepdims=True)
            vec_ref[5:6, base : base + span] = jnp.sum(gv_ref[...].astype(F32), axis=0, keepdims=True)
            for part, ref in enumerate((gq_ref, gk_ref, gv_ref)):
                cols = slice(part * width + base, part * width + base + span)
                dwq_ref[:, cols] = t_dot(normed_ref[...], ref[...]).astype(BF16)
                gn_ref[...] += dot_t(ref[...], wqkv_ref[:, cols])

    @pl.when(step == groups + 1)
    def _():
        scaled, inverse = norm_rows(x_ref[...].astype(F32))
        grad_normed = gn_ref[...]
        vec_ref[6:7] = jnp.sum(grad_normed * scaled, axis=0, keepdims=True)
        vec_ref[7:8] = jnp.sum(grad_normed, axis=0, keepdims=True)
        change = gmid_ref[...] + norm_back(grad_normed * g1_ref[...], scaled, inverse)
        high = change.astype(BF16)
        rest = (change - high.astype(F32)).astype(BF16)
        for i in range(images):
            here = slice(i * slots, (i + 1) * slots)
            gi_ref[i] = t_dot(sel_ref[i], high[here]) + t_dot(sel_ref[i], rest[here])


def whole(shape):
    return pl.BlockSpec(shape, lambda *_: (0,) * len(shape), pipeline_mode=pl.Buffered(1))


def on_device(
    images, keep_mask, ln1_gain, ln1_bias, w_qkv, bias_q, bias_v, w_proj, b_proj,
    ln2_gain, ln2_bias, w_fc1, b_fc1, w_fc2, b_fc2, cotangent,
):
    count, patches, width = images.shape
    slots = slots_of(patches)
    rows = count * slots
    heads = width // HEAD_DIM
    shard = w_fc1.shape[1]
    row = lambda v: v.reshape(1, -1)
    whole_w1 = lax.all_gather(w_fc1, "mlp")
    whole_w2 = lax.all_gather(w_fc2, "mlp")
    whole_b1 = lax.all_gather(b_fc1, "mlp").reshape(2, 1, shard)
    shape = jax.ShapeDtypeStruct
    limit = pltpu.CompilerParams(vmem_limit_bytes=60 * 2**20)
    per_image = lambda *tail: pl.BlockSpec((1,) + tail, lambda i: (i,) + (0,) * len(tail))
    per_rows = lambda cols: pl.BlockSpec((slots, cols), lambda i: (i, 0))
    sel, x, normed, qkv, probs, att, mid, hid, gm, sums = pl.pallas_call(
        functools.partial(forward_kernel, slots),
        grid=(count,),
        out_shape=(
            shape((count, slots, patches), BF16),
            shape((rows, width), BF16),
            shape((rows, width), BF16),
            shape((rows, 3 * width), BF16),
            shape((count, heads, slots, slots), BF16),
            shape((rows, width), BF16),
            shape((rows, width), F32),
            shape((rows, width), BF16),
            shape((rows, width), BF16),
            shape((count, 8, width), F32),
        ),
        in_specs=[
            per_image(1, patches), per_image(patches, width), per_image(patches, width),
            whole((1, width)), whole((1, width)), whole((width, 3 * width)), whole((1, width)), whole((1, width)),
            whole((width, width)), whole((1, width)), whole((1, width)), whole((1, width)),
        ],
        out_specs=(
            per_image(slots, patches), per_rows(width), per_rows(width), per_rows(3 * width),
            per_image(heads, slots, slots), per_rows(width), per_rows(width), per_rows(width), per_rows(width),
            per_image(8, width),
        ),
        compiler_params=limit,
        name="attention_forward",
    )(
        keep_mask.reshape(count, 1, patches), images, cotangent, row(ln1_gain), row(ln1_bias), w_qkv,
        row(bias_q), row(bias_v), w_proj, row(b_proj), row(ln2_gain), row(ln2_bias),
    )
    chunk = 512 if shard % 512 == 0 else 256
    each = shard // chunk
    mlp_out, grad_hidden, dw1, dw2, db1 = pl.pallas_call(
        mlp_kernel,
        grid=(2 * each,),
        out_shape=(
            shape((rows, width), F32), shape((rows, width), F32),
            shape((2, width, shard), BF16), shape((2, shard, width), BF16), shape((2, 1, shard), F32),
        ),
        in_specs=[
            whole((rows, width)), whole((rows, width)),
            pl.BlockSpec((1, width, chunk), lambda c: (c // each, 0, c % each)),
            pl.BlockSpec((1, 1, chunk), lambda c: (c // each, 0, c % each)),
            pl.BlockSpec((1, chunk, width), lambda c: (c // each, c % each, 0)),
        ],
        out_specs=(
            whole((rows, width)), whole((rows, width)),
            pl.BlockSpec((1, width, chunk), lambda c: (c // each, 0, c % each)),
            pl.BlockSpec((1, chunk, width), lambda c: (c // each, c % each, 0)),
            pl.BlockSpec((1, 1, chunk), lambda c: (c // each, 0, c % each)),
        ),
        compiler_params=limit,
        name="mlp_both_ways",
    )(hid, gm, whole_w1, whole_b1, whole_w2)
    kept = jnp.sum(keep_mask, axis=1, keepdims=True)
    valid = (jnp.arange(slots, dtype=jnp.int32)[None, :] < kept).astype(F32).reshape(rows, 1)
    groups = 3
    span = width // groups
    low, put, dwp, dwq, vec = pl.pallas_call(
        functools.partial(backward_kernel, count, slots, groups),
        grid=(groups + 2,),
        out_shape=(
            shape((count, patches, width), BF16), shape((count, patches, width), F32),
            shape((width, width), BF16), shape((width, 3 * width), BF16), shape((16, width), F32),
        ),
        in_specs=[
            whole((count, slots, patches)), whole((rows, width)), whole((rows, width)), whole((rows, 3 * width)),
            whole((count, heads, slots, slots)), whole((rows, width)), whole((rows, width)), whole((rows, width)),
            whole((rows, width)), whole((rows, width)), whole((rows, 1)),
            whole((1, width)), whole((1, width)), whole((1, width)), whole((width, 3 * width)), whole((width, width)),
            pl.BlockSpec(memory_space=pl.ANY), pl.BlockSpec(memory_space=pl.ANY),
        ],
        out_specs=(
            whole((count, patches, width)), whole((count, patches, width)),
            whole((width, width)), whole((width, 3 * width)), whole((16, width)),
        ),
        scratch_shapes=[
            pltpu.VMEM((rows, width), F32), pltpu.VMEM((rows, width), BF16),
            pltpu.VMEM((rows, span), BF16), pltpu.VMEM((rows, span), BF16), pltpu.VMEM((rows, span), BF16),
            pltpu.VMEM((rows, width), F32),
        ],
        compiler_params=limit,
        name="attention_backward",
    )(
        sel, x, normed, qkv, probs, att, mid, gm, grad_hidden, mlp_out, valid,
        row(ln1_gain), row(ln2_gain), row(b_fc2), w_qkv, w_proj, images, cotangent,
    )
    kept_at = (keep_mask > 0)[:, :, None]
    layer_out = jnp.where(kept_at, low, images)
    grad_images = jnp.where(kept_at, put, cotangent.astype(F32))
    both = ("img", "mlp")
    place = lax.axis_index("mlp")
    dw1s = lax.psum_scatter(dw1.reshape(2 * width, shard), "mlp", scatter_dimension=0, tiled=True)
    dw2s = lax.psum_scatter(dw2.reshape(2 * shard, width), "mlp", scatter_dimension=0, tiled=True)
    s_w1, s_w2 = lax.psum((dw1s, dw2s), "img")
    s_wq, s_wp = lax.psum((dwq, dwp), both)
    vec, sums, s_b1 = lax.psum((vec, jnp.sum(sums, axis=0), db1.reshape(2, shard)), both)
    s_b1 = lax.dynamic_index_in_dim(s_b1, place, 0, keepdims=False)
    stream_sq, mlp_sq, attn_sq = jnp.sum(vec[8]), jnp.sum(vec[9]), jnp.sum(sums[0])
    root_means = jnp.sqrt(jnp.stack([stream_sq, attn_sq, mlp_sq]) / (sums[1, 0] * width))
    f = lambda v: v.astype(F32)
    return (
        layer_out, grad_images, vec[6], vec[7], f(s_wq), vec[4], vec[5], f(s_wp), vec[3], vec[0], vec[1],
        f(s_w1), s_b1, f(s_w2), vec[2], root_means,
    )


def solution(mesh):
    rows, line = P(("img", "mlp"), None, None), P(("img", "mlp"), None)
    return jax.shard_map(
        on_device,
        mesh=mesh,
        in_specs=(
            rows, line, P(), P(), P(), P(), P(), P(), P(), P(), P(),
            P(None, "mlp"), P("mlp"), P("mlp", None), P(), rows,
        ),
        out_specs=(
            rows, rows, P(), P(), P(), P(), P(), P(), P(), P(), P(),
            P(None, "mlp"), P("mlp"), P("mlp", None), P(), P(),
        ),
        check_vma=False,
    )
```

time: 874 us -> 606 us (0.69); the launches traced: 860 us -> 606 us
  matrix products: 178 us -> 0 us
  local copies, waits for them, and re-layouts: 161 us -> 10.2 us
  Pallas kernels: 0 us -> 103 us
  blocking collectives: 95.9 us -> 2.11 us
  waiting for transfers between devices: 363 us -> 450 us
  other arithmetic: 41.9 us -> 26 us
    dot_general x18 -> x0, matrix products: 178 us -> none  [the longest x1 33.8 us: on_device(): jnp.dot(whole_rows, w_fc1, preferred_element_type=jnp.float32) + b_fc1]
    pallas_call x0 -> x3, Pallas kernels: none -> 103 us  [the longest x1 44.4 us: on_device(): pl.pallas_call(functools.partial(backward_kernel, count, slots, groups),...]
    psum x2 -> x3, waiting for transfers between devices: 349 us -> 437 us  [the longest x1 176 us: on_device(): s_w1, s_w2 = lax.psum((dw1s, dw2s), 'img')]
    psum x2 -> x0, blocking collectives: 84.4 us -> none  [the longest x1 45.3 us: on_device(): lax.psum((part_w_one, part_b_one, part_w_two), 'img')]
    reshape x12 -> x9, local copies, waits for them, and re-layouts: 68.1 us -> 5.25 us  [the longest x8 4.65 us: on_device(): row = lambda v: v.reshape(1, -1)]
    unnamed x125 -> x36, local copies, waits for them, and re-layouts: 53.9 us -> 1.39 us
    convert_element_type x8 -> x1, local copies, waits for them, and re-layouts: 31.3 us -> 1.06 us  [on_device(): (jnp.arange(slots, dtype=jnp.int32)[None, :] < kept).astype(F32)]
    reduce_sum x9 -> x4, other arithmetic: 24.9 us -> 3.9 us  [the longest x1 1.81 us: on_device(): jnp.sum(vec[8])]
  transfers between devices with their start and end apart: 6 -> 7, of which waited for: 3 -> 4; matrix products, arithmetic and copies ran while one was open for 11% -> 5% of each run, Pallas kernels for 0% -> 10%
where the time goes in v1:
time: 606 us
  waiting for transfers between devices  450 us (74%)
  Pallas kernels  103 us (17%)
  other arithmetic  26 us (4%)
  between operations  15 us (2%)
  local copies, waits for them, and re-layouts  10.2 us (2%)
    psum x1, waiting for transfers between devices, on_device(): s_w1, s_w2 = lax.psum((dw1s, dw2s), 'img')  176 us
    psum x1, waiting for transfers between devices, on_device(): s_wq, s_wp = lax.psum((dwq, dwp), both)  144 us
    psum x1, waiting for transfers between devices, on_device(): lax.psum((vec, jnp.sum(sums, axis=0), db1.reshape(2, shard)), both)  117 us
    pallas_call x1, Pallas kernels, on_device(): pl.pallas_call(functools.partial(backward_kernel, count, slots, groups),...  44.4 us
    pallas_call x1, Pallas kernels, on_device(): pl.pallas_call(mlp_kernel, grid=(2 * each,), out_shape=(shape((rows, widt...  39.5 us
    pallas_call x1, Pallas kernels, on_device(): pl.pallas_call(functools.partial(forward_kernel, slots), grid=(count,), o...  18.7 us
    convert_element_type x4, other arithmetic, on_device(): f = lambda v: v.astype(F32)  14.3 us
  transfers between devices with their start and end apart: 7, of which 4 were waited for; matrix products, arithmetic and copies ran while one was open for 5% of the time, Pallas kernels for 10%

profile of v1, /device:TPU:0, one launch (start us, length us, event | category | flops | bytes accessed | tf_op | source)
XLA Modules:
  0.0 605.9 jit_solution(17130567150141166227)
XLA Ops:
  7.3 0.7 all-gather.7.cloned.1.call-update
  8.1 0.7 all-gather.9.cloned.1.call-update
  13.5 18.7 %attention_forward.1 = (bf16[5,160,197]{2,1,0:T(8,128)(2,1)}, bf16[800,768]{1,0:T(8,128)(2,1)}, bf16[800,768]{1,0:T(8,128)(2,1)}, bf16[800,2304]{1,0:T(8,128)(2,...) custom-call(s32[5,1,197]{2,1,0:T(1,128)} %reshape.105.keep_ref, ...), custom_call_target="tpu_custom_call" | custom-call | tf_op jit(solution)/shard_map/attention_forward/pallas_call | solution.py:277
  32.3 2.1 all-gather.3.b1_ref
  34.4 9.6 %all-gather.9.cloned.1.call-done = bf16[3072,768]{1,0:T(8,128)(2,1)} async-done(((bf16[1536,768]{1,0:T(8,128)(2,1)}), bf16[3072,768]{1,0:T(8,128)(2,1)}) %all-gather.9.cloned.1.call-update) | async-done | bytes 4718608 | tf_op jit(solution)/shard_map/all_gather | solution.py:271
  44.0 39.5 %mlp_both_ways.1 = (f32[800,768]{1,0:T(8,128)}, f32[800,768]{1,0:T(8,128)}, bf16[2,768,1536]{2,1,0:T(8,128)(2,1)}, bf16[2,1536,768]{2,1,0:T(8,128)(2,1)}, f32[2,1,1536]{2,1,0:T(1,128)}) custom-call(bf16[800,768]{1,0:T(8,128)(2,1)} %get-tuple-element.44.hid_ref, bf16[800,768]{1,0:T(8,128)(2,1)} %get-tuple-element.43.gm_ref, bf16[2,768,1536]{2,1,0:T(8,128)(2,1)} %bitcast.11, ...), custom_call_target="tpu_custom_call" | custom-call | tf_op jit(solution)/shard_map/mlp_both_ways/pallas_call | solution.py:310
  84.3 1.1 reshape.126.valid_ref
  87.2 44.4 %attention_backward.1 = (bf16[5,197,768]{2,1,0:T(8,128)(2,1)}, f32[5,197,768]{2,1,0:T(8,128)}, bf16[768,768]{1,0:T(8,128)(2,1)}, bf16[768,2304]{1,0:T(8,128)(2,1)}, f32[16,768]{1,0:T(8,128)}) custom-call(bf16[5,160,197]{2,1,0:T(8,128)(2,1)} %get-tuple-element.36.sel_ref, bf16[800,768]{1,0:T(8,128)(2,1)} %get-tuple-element.37.x_ref, ...), custom_call_target="tpu_custom_call" | custom-call | tf_op jit(solution)/shard_map/attention_backward/pallas_call | solution.py:336
  132.3 0.6 all-reduce.11.cloned.1.call-update
  133.0 0.7 copy-done
  133.7 3.1 broadcast_select_fusion
  136.8 2.1 convert_select_fusion
  138.9 117.0 %all-reduce.7.cloned.1.call-done = (f32[16,768]{1,0:T(8,128)}, f32[2,1536]{1,0:T(2,128)}, f32[8,768]{1,0:T(8,128)}) async-done(((f32[16,768]{1,0:T(8,128)}, f32[2,1536]{1,0:T(2,128)}, f32[8,768]{1,0:T(8,128)}), (f32[16,768]{1,0:T(8,128)}, f32[2,1536]{1,0:T(2,128)}, f32[8,768]{1,0:T(8,128)})) %all-reduce.7.cloned.1.call-update) | async-done | bytes 86032 | tf_op jit(solution)/shard_map/psum | solution.py:374
  255.9 1.2 slice.59
  257.7 1.3 dynamic-slice_reduce_fusion
  259.0 1.3 slice_reduce_fusion.1
  260.4 1.8 slice_reduce_fusion.2
  262.2 2.5 fusion.1
  264.7 143.7 %all-reduce.9.cloned.1.call-done = (bf16[768,2304]{1,0:T(8,128)(2,1)}, bf16[768,768]{1,0:T(8,128)(2,1)}) async-done(((bf16[768,2304]{1,0:T(8,128)(2,1)}, bf16[768,768]{1,0:T(8,128)(2,1)}), (bf16[768,2304]{1,0:T(8,128)(2,1)}, bf16[768,768]{1,0:T(8,128)(2,1)})) %all-reduce.9.cloned.1.call-update) | async-done | bytes 4718608 | tf_op jit(solution)/shard_map/psum | solution.py:373
  408.4 5.6 convert_element_type.31
  414.0 1.6 convert_element_type.32
  415.6 176.3 %all-reduce.11.cloned.1.call-done = (bf16[768,1536]{1,0:T(8,128)(2,1)}, bf16[1536,768]{1,0:T(8,128)(2,1)}) async-done(((bf16[768,1536]{1,0:T(8,128)(2,1)}, bf16[1536,768]{1,0:T(8,128)(2,1)}), (bf16[768,1536]{1,0:T(8,128)(2,1)}, bf16[1536,768]{1,0:T(8,128)(2,1)})) %all-reduce.11.cloned.1.call-update) | async-done | bytes 4718608 | tf_op jit(solution)/shard_map/psum | solution.py:372
  591.9 4.6 convert_element_type.33
  596.5 2.5 convert_element_type.34
  (62 shorter events, 8.1 us)
Async XLA Ops:
  7.2 1.6 copy-start.8
  7.2 2.2 copy-start.9
  7.2 2.8 copy-start.6
  7.2 3.4 copy-start.10
  7.2 3.9 copy-start.13
  7.2 4.5 copy-start.14
  7.2 5.1 copy-start.15
  7.3 5.7 copy-start.11
  7.3 6.2 %copy-start.12 = (bf16[1536]{0:T(1024)(128)(2,1)S(1)}, bf16[1536]{0:T(1024)(128)(2,1)}, u32[]{:S(2)}) copy-start(bf16[1536]{0:T(1024)(128)(2,1)} %param.28) | copy-start | bytes 9220
  7.3 27.1 %all-gather.7.cloned.1.call-start = ((), (), s32[]{:S(2)}) async-start(), calls=%async_computation.4 | async-start | bytes 7077888 | tf_op jit(solution)/shard_map/all_gather | solution.py:270
  8.0 36.0 %all-gather.9.cloned.1.call-start = ((), (), s32[]{:S(2)}) async-start(), calls=%async_computation.5 | async-start | bytes 7077888 | tf_op jit(solution)/shard_map/all_gather | solution.py:271
  8.8 123.5 %reduce-scatter.3.cloned.1.call-start = ((), (), s32[]{:S(2)}) async-start(), calls=%async_computation.2 | async-start | bytes 7077888 | tf_op jit(solution)/shard_map/reduce_scatter | solution.py:370
  83.5 48.8 %reduce-scatter.5.cloned.1.call-start = ((), (), s32[]{:S(2)}) async-start(), calls=%async_computation.3 | async-start | bytes 7077888 | tf_op jit(solution)/shard_map/reduce_scatter | solution.py:371
  83.5 1.8 copy-start.16
  83.5 2.4 copy-start.5
  83.5 3.0 copy-start.7
  84.1 171.8 %all-reduce.7.cloned.1.call-start = ((), (), s32[]{:S(2)}) async-start(), calls=%async_computation.6 | async-start | bytes 172032 | tf_op jit(solution)/shard_map/psum | solution.py:374
  131.6 276.8 %all-reduce.9.cloned.1.call-start = ((), (), s32[]{:S(2)}) async-start(), calls=%async_computation.7 | async-start | bytes 9437184 | tf_op jit(solution)/shard_map/psum | solution.py:373
  132.2 459.7 %all-reduce.11.cloned.1.call-start = ((), (), s32[]{:S(2)}) async-start(), calls=%async_computation.8 | async-start | bytes 9437184 | tf_op jit(solution)/shard_map/psum | solution.py:372
  132.3 1.4 copy-start
  133.0 3.8 copy-start.1
  133.0 3.8 copy-start.2
  408.4 5.6 copy-start.4
  591.9 4.7 copy-start.3
Sparse Core Ops, SparseCore 0:
  9.6 17.1 all-gather.6
  28.4 15.5 all-gather.8
  83.6 13.7 reduce-scatter.2
  100.1 13.8 reduce-scatter.4
  131.8 124.0 all-reduce.6
  261.5 146.8 all-reduce.8
  414.2 177.6 all-reduce.10

commit v2 on v1

--- a/solution.py
+++ b/solution.py
@@ -11,6 +11,7 @@
 NORM_EPS = 1e-06
 F32 = jnp.float32
 BF16 = jnp.bfloat16
+MESH = pl.DeviceIdType.MESH
 ERFC_POLY = (
     -0.05792342897865154,
     0.27982426175045266,
@@ -67,11 +68,43 @@
     return values * share, share + values * (decay * 0.3989422804014327)
 
 
+def swap_weights(ours, theirs, send_sem, recv_sem):
+    other = {"mlp": 1 - lax.axis_index("mlp")}
+    copies = [
+        pltpu.make_async_remote_copy(
+            src_ref=ours[j], dst_ref=theirs[j], send_sem=send_sem.at[j], recv_sem=recv_sem.at[j],
+            device_id=other, device_id_type=MESH,
+        )
+        for j in range(len(ours))
+    ]
+
+    def trade(begin):
+        @pl.when(pl.program_id(0) == (0 if begin else pl.num_programs(0) - 1))
+        def _():
+            if begin:
+                barrier = pltpu.get_barrier_semaphore()
+                pl.semaphore_signal(barrier, inc=1, device_id=other, device_id_type=MESH)
+                pl.semaphore_wait(barrier, 1)
+            for copy in copies:
+                if begin:
+                    copy.start()
+                else:
+                    copy.wait()
+
+    return trade
+
+
 def forward_kernel(
-    slots,
+    slots, exchange,
     keep_ref, img_ref, cot_ref, g1_ref, b1_ref, wqkv_ref, bq_ref, bv_ref, wproj_ref, bproj_ref, g2_ref, b2_ref,
-    sel_ref, x_ref, normed_ref, qkv_ref, probs_ref, att_ref, mid_ref, hid_ref, gm_ref, sums_ref,
+    *refs,
 ):
+    if exchange:
+        ours, refs, (send_sem, recv_sem) = refs[:3], refs[3:-2], refs[-2:]
+        theirs, refs = refs[-3:], refs[:-3]
+        trade = swap_weights(ours, theirs, send_sem, recv_sem)
+        trade(True)
+    sel_ref, x_ref, normed_ref, qkv_ref, probs_ref, att_ref, mid_ref, hid_ref, gm_ref, sums_ref = refs
     patches, width = img_ref.shape[1:]
     heads = width // HEAD_DIM
     keep = keep_ref[0].astype(F32)
@@ -127,6 +160,8 @@
     sums_ref[0, 1:2] = jnp.broadcast_to(count, (1, width))
     scaled, _ = norm_rows(middle)
     hid_ref[...] = (scaled * g2_ref[...] + b2_ref[...]).astype(BF16)
+    if exchange:
+        trade(False)
 
 
 def mlp_kernel(hid_ref, gm_ref, w1_ref, b1_ref, w2_ref, out_ref, gh_ref, dw1_ref, dw2_ref, db1_ref):
@@ -257,7 +292,7 @@
     return pl.BlockSpec(shape, lambda *_: (0,) * len(shape), pipeline_mode=pl.Buffered(1))
 
 
-def on_device(
+def plain_device(
     images, keep_mask, ln1_gain, ln1_bias, w_qkv, bias_q, bias_v, w_proj, b_proj,
     ln2_gain, ln2_bias, w_fc1, b_fc1, w_fc2, b_fc2, cotangent,
 ):
@@ -275,7 +310,7 @@
     per_image = lambda *tail: pl.BlockSpec((1,) + tail, lambda i: (i,) + (0,) * len(tail))
     per_rows = lambda cols: pl.BlockSpec((slots, cols), lambda i: (i, 0))
     sel, x, normed, qkv, probs, att, mid, hid, gm, sums = pl.pallas_call(
-        functools.partial(forward_kernel, slots),
+        functools.partial(forward_kernel, slots, False),
         grid=(count,),
         out_shape=(
             shape((count, slots, patches), BF16),
@@ -382,10 +417,678 @@
     )
 
 
+class Place:
+    def __init__(self, deep, width):
+        spot, self.core = lax.axis_index("img"), lax.axis_index("mlp")
+        x, y, self.z = spot % 2, (spot // 2) % 2, spot // 4
+        core = self.core
+        self.bit1 = x * (1 - core) + y * core
+        self.bit2 = y * (1 - core) + x * core
+        step_x, step_y = 1 - 2 * x, 2 - 4 * y
+        self.deep = deep
+        self.other = {"mlp": 1 - core}
+        self.peer1 = {"img": spot + step_x * (1 - core) + step_y * core}
+        self.peer2 = {"img": spot + step_y * (1 - core) + step_x * core}
+        self.peer_z = [{"img": ((self.z + k) % deep) * 4 + spot % 4} for k in range(1, deep)]
+        self.half, self.quarter = width // 2, width // 4
+        self.piece = width // 4 // deep
+        self.half_at = self.bit1 * self.half
+        self.half_off = (1 - self.bit1) * self.half
+        self.quarter_at = self.half_at + self.bit2 * self.quarter
+        self.quarter_off = self.half_at + (1 - self.bit2) * self.quarter
+
+    def piece_at(self, z):
+        return self.quarter_at + z * self.piece
+
+    def everyone(self):
+        return [self.other, self.peer1, self.peer2] + self.peer_z
+
+    def greet(self):
+        for peer in self.everyone():
+            pl.semaphore_signal(pltpu.get_barrier_semaphore(), inc=1, device_id=peer, device_id_type=MESH)
+
+    def all_here(self):
+        pl.semaphore_wait(pltpu.get_barrier_semaphore(), len(self.everyone()))
+
+
+def span(start, size):
+    return pl.ds(pl.multiple_of(start, 16), size)
+
+
+def remote(source, target, send_sem, recv_sem, peer):
+    return pltpu.make_async_remote_copy(
+        src_ref=source, dst_ref=target, send_sem=send_sem, recv_sem=recv_sem, device_id=peer, device_id_type=MESH
+    )
+
+
+def added(left, right):
+    return (left.astype(F32) + right.astype(F32)).astype(BF16)
+
+
+class Reduce:
+    def __init__(self, place, partial, sending, total, got_core, got1, got2, got_z, send, recv, send_z, recv_z):
+        self.place, self.partial, self.sending, self.total = place, partial, sending, total
+        self.got_core, self.got1, self.got2, self.got_z = got_core, got1, got2, got_z
+        self.send, self.recv, self.send_z, self.recv_z = send, recv, send_z, recv_z
+
+    def copies(self, c, stage):
+        p = self.place
+        if stage == 0:
+            return [remote(self.sending(c), self.got_core.at[c], self.send.at[c, 0], self.recv.at[c, 0], p.other)]
+        total = self.total(c)
+        if stage == 1:
+            part = total.at[:, span(p.half_off, p.half), :]
+            return [remote(part, self.got1.at[c], self.send.at[c, 1], self.recv.at[c, 1], p.peer1)]
+        if stage == 2:
+            part = total.at[:, span(p.quarter_off, p.quarter), :]
+            return [remote(part, self.got2.at[c], self.send.at[c, 2], self.recv.at[c, 2], p.peer2)]
+        made = []
+        for k, peer in enumerate(p.peer_z):
+            part = total.at[:, span(p.piece_at((p.z + k + 1) % p.deep), p.piece), :]
+            made.append(remote(part, self.got_z.at[c, k], self.send_z.at[c, k], self.recv_z.at[c, k], peer))
+        return made
+
+    def begin(self, c, stage):
+        for copy in self.copies(c, stage):
+            copy.start()
+
+    def arrive(self, c, stage):
+        for copy in self.copies(c, stage):
+            copy.wait_recv()
+
+    def sent(self, c):
+        for stage in range(4):
+            for copy in self.copies(c, stage):
+                copy.wait_send()
+
+    def plane1(self, c):
+        self.arrive(c, 0)
+        total, partial, got = self.total(c), self.partial(c), self.got_core.at[c]
+        total[...] = added(partial[...], got[...])
+        self.begin(c, 1)
+
+    def plane2(self, c):
+        p = self.place
+        self.arrive(c, 1)
+        rows = span(p.half_at, p.half)
+        total = self.total(c)
+        total[:, rows, :] = added(total[:, rows, :], self.got1[c])
+        self.begin(c, 2)
+
+    def along_z(self, c):
+        p = self.place
+        self.arrive(c, 2)
+        rows = span(p.quarter_at, p.quarter)
+        total = self.total(c)
+        total[:, rows, :] = added(total[:, rows, :], self.got2[c])
+        self.begin(c, 3)
+
+    def finish(self, c):
+        p = self.place
+        self.arrive(c, 3)
+        rows = span(p.piece_at(p.z), p.piece)
+        value = self.total(c)[:, rows, :].astype(F32)
+        for k in range(p.deep - 1):
+            value = value + self.got_z[c, k].astype(F32)
+        return value.astype(BF16)
+
+
+class Gather:
+    def __init__(self, place, piece, result, mirror, local, send, recv, send_z, recv_z):
+        self.place, self.piece, self.result, self.mirror, self.local = place, piece, result, mirror, local
+        self.send, self.recv, self.send_z, self.recv_z = send, recv, send_z, recv_z
+
+    def kept(self, c):
+        p = self.place
+        return pltpu.make_async_copy(
+            self.piece(c), self.result(c).at[:, span(p.piece_at(p.z), p.piece), :], self.local.at[c]
+        )
+
+    def copies(self, c, stage, landing=False):
+        p, result = self.place, self.result(c)
+        if stage == 0:
+            made = []
+            for k, peer in enumerate(p.peer_z):
+                z = (p.z - k - 1 + p.deep) % p.deep if landing else p.z
+                target = result.at[:, span(p.piece_at(z), p.piece), :]
+                made.append(remote(self.piece(c), target, self.send_z.at[c, k], self.recv_z.at[c, k], peer))
+            return made
+        if stage == 1:
+            source = result.at[:, span(p.quarter_at, p.quarter), :]
+            target = result.at[:, span(p.quarter_off if landing else p.quarter_at, p.quarter), :]
+            return [remote(source, target, self.send.at[c, 0], self.recv.at[c, 0], p.peer2)]
+        if stage == 2:
+            source = result.at[:, span(p.half_at, p.half), :]
+            target = result.at[:, span(p.half_off if landing else p.half_at, p.half), :]
+            return [remote(source, target, self.send.at[c, 1], self.recv.at[c, 1], p.peer1)]
+        return [remote(result, self.mirror(c) if landing else result, self.send.at[c, 2], self.recv.at[c, 2], p.other)]
+
+    def begin(self, c, stage):
+        for copy in self.copies(c, stage):
+            copy.start()
+
+    def arrive(self, c, stage):
+        for copy in self.copies(c, stage, landing=True):
+            copy.wait_recv()
+
+    def along_z(self, c):
+        self.kept(c).start()
+        self.begin(c, 0)
+
+    def plane2(self, c):
+        self.kept(c).wait()
+        self.arrive(c, 0)
+        self.begin(c, 1)
+
+    def plane1(self, c):
+        self.arrive(c, 1)
+        self.begin(c, 2)
+
+    def across(self, c):
+        self.arrive(c, 2)
+        self.begin(c, 3)
+
+    def sent(self, c):
+        for stage in range(3 if self.mirror is None else 4):
+            for copy in self.copies(c, stage):
+                copy.wait_send()
+
+
+def vec_slot(slot, width):
+    return slice(slot // 2, slot // 2 + 1), slice(slot % 2 * width, slot % 2 * width + width)
+
+
+def mlp_staged_kernel(
+    deep, images, slots, ticks,
+    hid_ref, gm_ref, att_ref, mid_ref, sel_ref, sums_ref, w1a_ref, w1b_ref, b1a_ref, b1b_ref, w2a_ref, w2b_ref,
+    wproj_ref, g2_ref, bfc2_ref,
+    red_ref, gmid_ref, gatt_ref, dwp_ref, lo_ref, vec_ref,
+    out_ref, gh_ref, give_ref, own_ref, got_core, got1, got2, got_z, send, recv, send_z, recv_z,
+):
+    step = pl.program_id(0)
+    rows, width = hid_ref.shape
+    place = Place(deep, width)
+    panels = 4
+    reduce = Reduce(
+        place, lambda c: own_ref.at[c], lambda c: give_ref.at[c], lambda c: own_ref.at[c],
+        got_core, got1, got2, got_z, send, recv, send_z, recv_z,
+    )
+
+    def put_red(c):
+        red_ref[pl.ds(c * panels, panels)] = reduce.finish(c)
+
+    def half(w1_ref, b1_ref, w2_ref, target, db_row):
+        hid, gm = hid_ref[...], gm_ref[...]
+        w1, w2 = w1_ref[...], w2_ref[...]
+        chunk = w1.shape[1]
+        pre = dot(hid, w1) + b1_ref[...].astype(F32)
+        act, slope = gelu_pair(pre)
+        act = act.astype(BF16)
+        grad_act = dot_t(gm, w2).astype(BF16).astype(F32)
+        grad_pre = (grad_act * slope).astype(BF16)
+        d2 = t_dot(act, gm).astype(BF16)
+        for j in range(width // 128):
+            at = j % 3 * chunk
+            target[2 + j // 3, at : at + chunk, :] = d2[:, j * 128 : j * 128 + 128]
+        d1 = t_dot(hid, grad_pre).astype(BF16)
+        target[0] = d1[:, :128]
+        target[1] = d1[:, 128:]
+        cols = pl.ds(pl.multiple_of(step * chunk, chunk), chunk)
+        vec_ref[pl.ds(db_row, 1), cols] = jnp.sum(grad_pre.astype(F32), axis=0, keepdims=True)
+        out_ref[...] += dot(act, w2)
+        gh_ref[...] += dot_t(grad_pre, w1)
+
+    @pl.when(step == 0)
+    def _():
+        place.greet()
+        out_ref[...] = jnp.zeros_like(out_ref)
+        gh_ref[...] = jnp.zeros_like(gh_ref)
+        place.all_here()
+
+    @pl.when((step >= 1) & (step <= ticks))
+    def _():
+        reduce.plane1(step - 1)
+
+    @pl.when((step >= 2) & (step <= ticks))
+    def _():
+        reduce.plane2(step - 2)
+
+    @pl.when((step >= 3) & (step <= ticks))
+    def _():
+        reduce.along_z(step - 3)
+
+    @pl.when((step >= 4) & (step <= ticks))
+    def _():
+        put_red(step - 4)
+
+    @pl.when(step < ticks)
+    def _():
+        half(w1b_ref, b1b_ref, w2b_ref, give_ref.at[step], 7 - place.core)
+
+    @pl.when(step < ticks)
+    def _():
+        reduce.begin(step, 0)
+        half(w1a_ref, b1a_ref, w2a_ref, own_ref.at[step], 6 + place.core)
+
+    def note(slot, value):
+        at_row, at_col = vec_slot(slot, width)
+        vec_ref[at_row, at_col] = value
+
+    def column_sum(value):
+        return jnp.sum(value, axis=0, keepdims=True)
+
+    @pl.when(step == ticks)
+    def _():
+        stream = mlp_sq = jnp.zeros((1, width), F32)
+        gain = shift = b_two = b_proj = jnp.zeros((1, width), F32)
+        for i in range(images):
+            here = slice(i * slots, i * slots + slots)
+            sel = sel_ref[i]
+            middle = mid_ref[here]
+            valid = jnp.sum(sel.astype(F32), axis=1, keepdims=True) > 0
+            mlp_out = jnp.where(valid, out_ref[here] + bfc2_ref[...].astype(F32), 0.0)
+            block = middle + mlp_out
+            kept = jnp.where(valid, block, 0.0)
+            stream = stream + column_sum(kept * kept)
+            mlp_sq = mlp_sq + column_sum(mlp_out * mlp_out)
+            lo_ref[i] = t_dot(sel, block.astype(BF16)).astype(BF16)
+            scaled, inverse = norm_rows(middle)
+            grad_hidden = gh_ref[here]
+            gain = gain + column_sum(grad_hidden * scaled)
+            shift = shift + column_sum(grad_hidden)
+            gm = gm_ref[here].astype(F32)
+            b_two = b_two + column_sum(gm)
+            grad_middle = gm + norm_back(grad_hidden * g2_ref[...], scaled, inverse)
+            gmid_ref[here] = grad_middle
+            grad_attn = grad_middle.astype(BF16)
+            b_proj = b_proj + column_sum(grad_attn.astype(F32))
+            hid_ref_out = grad_attn
+            gatt_ref[here] = grad_attn
+        for slot, value in enumerate((gain, shift, b_two, b_proj)):
+            note(slot, value)
+        note(8, stream)
+        note(9, mlp_sq)
+        note(10, sum(sums_ref[i, 0:1] for i in range(images)))
+        note(11, sum(sums_ref[i, 1:2] for i in range(images)))
+        reduce.plane2(ticks - 1)
+        reduce.along_z(ticks - 2)
+        put_red(ticks - 3)
+        grad_attn = gatt_ref[...]
+        for part in range(3):
+            cols = slice(part * width // 3, (part + 1) * width // 3)
+            d = t_dot(att_ref[...], grad_attn[:, cols]).astype(BF16)
+            dwp_ref[0, part] = d[:, :128]
+            dwp_ref[1, part] = d[:, 128:]
+        reduce.along_z(ticks - 1)
+        put_red(ticks - 2)
+        gatt_ref[...] = dot_t(grad_attn, wproj_ref[...]).astype(BF16)
+        put_red(ticks - 1)
+
+        @pl.loop(0, ticks)
+        def _(c):
+            reduce.sent(c)
+
+
+def attention_staged_kernel(
+    deep, images, slots, groups, ticks,
+    q_ref, k_ref, v_ref, probs_ref, gatt_ref, wq_ref, wk_ref, wv_ref, normed_ref, x_ref, gmid_ref, sel_ref, g1_ref,
+    dwp_ref, red_ref, vecin_ref,
+    mlp_ref, attn_ref, gi_ref, vec_ref,
+    gq_ref, gk_ref, gv_ref, gn_ref, stage_ref, total_ref, piece_ref, got_core, got1, got2, got_z,
+    vsum_ref, vgot_ref, vz_ref,
+    send, recv, send_z, recv_z, m_local, m_send, m_recv, m_send_z, m_recv_z,
+    a_local, a_send, a_recv, a_send_z, a_recv_z, v_send, v_recv, v_send_z, v_recv_z,
+):
+    step = pl.program_id(0)
+    rows, width = x_ref.shape
+    place = Place(deep, width)
+    core = place.core
+    polls = images + 2
+
+    def partial_of(owner):
+        def pick(c):
+            if isinstance(c, int) and c == 0:
+                return dwp_ref.at[owner]
+            return stage_ref.at[c - 1, owner]
+
+        return pick
+
+    reduce = Reduce(
+        place, partial_of(core), partial_of(1 - core), lambda c: total_ref.at[c],
+        got_core, got1, got2, got_z, send, recv, send_z, recv_z,
+    )
+    back = Gather(
+        place, lambda c: piece_ref.at[c], lambda c: attn_ref.at[core, pl.ds(3 * c, 3)],
+        lambda c: attn_ref.at[1 - core, pl.ds(3 * c, 3)], a_local, a_send, a_recv, a_send_z, a_recv_z,
+    )
+    mlp = Gather(
+        place, lambda c: red_ref.at[pl.ds(4 * c, 4)], lambda c: mlp_ref.at[pl.ds(4 * c, 4)], None,
+        m_local, m_send, m_recv, m_send_z, m_recv_z,
+    )
+
+    def turn(c):
+        piece_ref[c] = reduce.finish(c)
+        back.along_z(c)
+
+    def do(name, c):
+        return {
+            "X": reduce.plane1, "Y": reduce.plane2, "Z": reduce.along_z, "R": turn,
+            "ay": back.plane2, "ax": back.plane1, "ac": back.across,
+            "my": mlp.plane2, "mx": mlp.plane1,
+        }[name](c)
+
+    plan = {}
+    for at, name, c in (
+        (1, "X", 0), (3, "my", 0), (4, "Y", 0), (6, "mx", 0), (6, "Z", 0),
+        (7, "my", 1), (8, "X", 1), (9, "R", 0), (10, "mx", 1), (11, "Y", 1), (11, "my", 2), (12, "ay", 0),
+        (13, "Z", 1), (14, "mx", 2), (15, "X", 2), (15, "ax", 0), (16, "R", 1), (16, "my", 3), (18, "Y", 2),
+        (18, "mx", 3), (19, "ay", 1), (20, "Z", 2),
+    ):
+        plan.setdefault(at, []).append((name, c))
+
+    def run(at, now):
+        for moment, jobs in sorted(plan.items()):
+            if at(moment % polls):
+
+                @pl.when(now == moment)
+                def _(jobs=jobs):
+                    for name, c in jobs:
+                        do(name, c)
+
+    first = lax.broadcasted_iota(jnp.int32, (1, 2 * HEAD_DIM), 1) < HEAD_DIM
+    zero = jnp.zeros((), BF16)
+    scale = jnp.asarray(HEAD_DIM ** -0.5, BF16)
+    pairs = width // 128 // groups
+    wide = pairs * 128
+
+    @pl.when(step == 0)
+    def _():
+        place.greet()
+        gn_ref[...] = jnp.zeros_like(gn_ref)
+        vsum_ref[0] = vecin_ref[...]
+        place.all_here()
+        reduce.begin(0, 0)
+        for c in range(ticks):
+            mlp.along_z(c)
+
+    @pl.when(step < groups)
+    def _():
+        @pl.loop(0, images)
+        def _(i):
+            run(lambda at: at < images, step * polls + i)
+            here = pl.ds(pl.multiple_of(i * slots, 16), slots)
+            for pair in range(pairs):
+                own = slice(pair * 128, pair * 128 + 128)
+                query, key, value = q_ref[here, own], k_ref[here, own], v_ref[here, own]
+                grad_att = gatt_ref[here, own]
+                gq = gk = gv = None
+                for half in range(2):
+                    mine = first if half == 0 else jnp.logical_not(first)
+                    low = probs_ref[i, 2 * pair + half]
+                    probs = low.astype(F32)
+                    g_mine = jnp.where(mine, grad_att, zero)
+                    grad_probs = dot_t(g_mine, value).astype(BF16).astype(F32)
+                    inner = jnp.sum(probs * grad_probs, axis=1, keepdims=True)
+                    grad_scores = (probs * (grad_probs - inner)).astype(BF16) * scale
+                    tv = t_dot(low, g_mine)
+                    tq = dot(grad_scores, jnp.where(mine, key, zero))
+                    tk = t_dot(grad_scores, jnp.where(mine, query, zero))
+                    gq = tq if gq is None else gq + tq
+                    gk = tk if gk is None else gk + tk
+                    gv = tv if gv is None else gv + tv
+                gq_ref[here, own] = gq.astype(BF16)
+                gk_ref[here, own] = gk.astype(BF16)
+                gv_ref[here, own] = gv.astype(BF16)
+
+        run(lambda at: at == images, step * polls + images)
+        cols = pl.ds(pl.multiple_of(step * wide, wide), wide)
+        shifted = pl.ds(pl.multiple_of(width + step * wide, wide), wide)
+        vsum_ref[0, 2:3, cols] = jnp.sum(gq_ref[...].astype(F32), axis=0, keepdims=True)
+        vsum_ref[0, 2:3, shifted] = jnp.sum(gv_ref[...].astype(F32), axis=0, keepdims=True)
+        for part, (ref, w_ref) in enumerate(((gq_ref, wq_ref), (gk_ref, wk_ref), (gv_ref, wv_ref))):
+            d = t_dot(normed_ref[...], ref[...]).astype(BF16)
+            stage_ref[step, 0, part] = d[:, :128]
+            stage_ref[step, 1, part] = d[:, 128:]
+            gn_ref[...] += dot_t(ref[...], w_ref[...])
+        reduce.begin(step + 1, 0)
+        run(lambda at: at == images + 1, step * polls + images + 1)
+
+    def vec_copies(stage):
+        if stage < 3:
+            peer = (place.other, place.peer1, place.peer2)[stage]
+            return [remote(vsum_ref.at[stage], vgot_ref.at[stage], v_send.at[stage], v_recv.at[stage], peer)]
+        return [
+            remote(vsum_ref.at[3], vz_ref.at[k], v_send_z.at[k], v_recv_z.at[k], peer)
+            for k, peer in enumerate(place.peer_z)
+        ]
+
+    def vec_begin(stage):
+        for copy in vec_copies(stage):
+            copy.start()
+
+    def vec_next(stage):
+        for copy in vec_copies(stage):
+            copy.wait_recv()
+        if stage < 3:
+            vsum_ref[stage + 1] = vsum_ref[stage] + vgot_ref[stage]
+            vec_begin(stage + 1)
+
+    @pl.when(step == groups)
+    def _():
+        last = groups
+        do("X", last)
+        gain = shift = jnp.zeros((1, width), F32)
+        for i in range(images):
+            here = slice(i * slots, i * slots + slots)
+            sel = sel_ref[i]
+            scaled, inverse = norm_rows(x_ref[here].astype(F32))
+            grad_normed = gn_ref[here]
+            gain = gain + jnp.sum(grad_normed * scaled, axis=0, keepdims=True)
+            shift = shift + jnp.sum(grad_normed, axis=0, keepdims=True)
+            change = gmid_ref[here] + norm_back(grad_normed * g1_ref[...], scaled, inverse)
+            high = change.astype(BF16)
+            rest = (change - high.astype(F32)).astype(BF16)
+            gi_ref[i] = t_dot(sel, high) + t_dot(sel, rest)
+            if i == 1:
+                do("R", 2)
+                do("ax", 1)
+                do("my", 4)
+            if i == 3:
+                do("Y", last)
+                do("mx", 4)
+                do("ac", 0)
+        at_row, at_col = vec_slot(6, width)
+        vsum_ref[0, at_row, at_col] = gain
+        at_row, at_col = vec_slot(7, width)
+        vsum_ref[0, at_row, at_col] = shift
+        vec_begin(0)
+        do("Z", last)
+        do("ay", 2)
+        vec_next(0)
+        do("my", 5)
+        do("R", last)
+        vec_next(1)
+        do("ax", 2)
+        do("ac", 1)
+        do("ay", last)
+        vec_next(2)
+        do("mx", 5)
+        do("ax", last)
+        vec_next(3)
+        value = None
+        for z in range(deep):
+            mine = vsum_ref[3]
+            from_k = [vz_ref[k] for k in range(deep - 1)]
+            term = mine
+            for k in range(deep - 1):
+                term = jnp.where((place.z - k - 1 + deep) % deep == z, from_k[k], term)
+            value = term if value is None else value + term
+        vec_ref[...] = value
+        do("ac", 2)
+        do("ac", last)
+        for c in range(ticks):
+            mlp.arrive(c, 2)
+            mlp.sent(c)
+        for c in range(groups + 1):
+            back.arrive(c, 3)
+            back.sent(c)
+            reduce.sent(c)
+        for stage in range(4):
+            for copy in vec_copies(stage):
+                copy.wait_send()
+
+
+def staged_device(
+    deep, images, keep_mask, ln1_gain, ln1_bias, w_qkv, bias_q, bias_v, w_proj, b_proj,
+    ln2_gain, ln2_bias, w_fc1, b_fc1, w_fc2, b_fc2, cotangent,
+):
+    count, patches, width = images.shape
+    slots = slots_of(patches)
+    rows = count * slots
+    heads = width // HEAD_DIM
+    shard = w_fc1.shape[1]
+    row = lambda v: v.reshape(1, -1)
+    shape = jax.ShapeDtypeStruct
+    limit = 62 * 2**20
+    any_space = pl.BlockSpec(memory_space=pl.ANY)
+    per_image = lambda *tail: pl.BlockSpec((1,) + tail, lambda i: (i,) + (0,) * len(tail))
+    per_rows = lambda cols: pl.BlockSpec((slots, cols), lambda i: (i, 0))
+    dma = pltpu.SemaphoreType.DMA
+    sel, x, normed, qkv, probs, att, mid, hid, gm, sums, far_w1, far_b1, far_w2 = pl.pallas_call(
+        functools.partial(forward_kernel, slots, True),
+        grid=(count,),
+        out_shape=(
+            shape((count, slots, patches), BF16),
+            shape((rows, width), BF16),
+            shape((rows, width), BF16),
+            shape((rows, 3 * width), BF16),
+            shape((count, heads, slots, slots), BF16),
+            shape((rows, width), BF16),
+            shape((rows, width), F32),
+            shape((rows, width), BF16),
+            shape((rows, width), BF16),
+            shape((count, 8, width), F32),
+            shape((width, shard), BF16), shape((1, shard), BF16), shape((shard, width), BF16),
+        ),
+        in_specs=[
+            per_image(1, patches), per_image(patches, width), per_image(patches, width),
+            whole((1, width)), whole((1, width)), whole((width, 3 * width)), whole((1, width)), whole((1, width)),
+            whole((width, width)), whole((1, width)), whole((1, width)), whole((1, width)),
+            any_space, any_space, any_space,
+        ],
+        out_specs=(
+            per_image(slots, patches), per_rows(width), per_rows(width), per_rows(3 * width),
+            per_image(heads, slots, slots), per_rows(width), per_rows(width), per_rows(width), per_rows(width),
+            per_image(8, width), any_space, any_space, any_space,
+        ),
+        scratch_shapes=[dma((3,)), dma((3,))],
+        compiler_params=pltpu.CompilerParams(vmem_limit_bytes=limit, collective_id=0, has_side_effects=True),
+        name="attention_forward",
+    )(
+        keep_mask.reshape(count, 1, patches), images, cotangent, row(ln1_gain), row(ln1_bias), w_qkv,
+        row(bias_q), row(bias_v), w_proj, row(b_proj), row(ln2_gain), row(ln2_bias),
+        w_fc1, row(b_fc1), w_fc2,
+    )
+    chunk = 256
+    ticks = shard // chunk
+    groups = 3
+    piece = width // 4 // deep
+    by_cols = lambda *lead: pl.BlockSpec(lead + (chunk,), lambda c: (0, c - c // ticks))
+    by_rows = pl.BlockSpec((chunk, width), lambda c: (c - c // ticks, 0))
+    red, gmid, gatt, dwp, low, vec = pl.pallas_call(
+        functools.partial(mlp_staged_kernel, deep, count, slots, ticks),
+        grid=(ticks + 1,),
+        out_shape=(
+            shape((4 * ticks, piece, 128), BF16), shape((rows, width), F32), shape((rows, width), BF16),
+            shape((2, 3, width, 128), BF16), shape((count, patches, width), BF16), shape((8, 2 * width), F32),
+        ),
+        in_specs=[
+            whole((rows, width)), whole((rows, width)), whole((rows, width)), whole((rows, width)),
+            whole((count, slots, patches)), whole((count, 8, width)),
+            by_cols(width), by_cols(width), by_cols(1), by_cols(1), by_rows, by_rows,
+            whole((width, width)), whole((1, width)), whole((1, width)),
+        ],
+        out_specs=(
+            whole((4 * ticks, piece, 128)), whole((rows, width)), whole((rows, width)),
+            whole((2, 3, width, 128)), whole((count, patches, width)), whole((8, 2 * width)),
+        ),
+        scratch_shapes=[
+            pltpu.VMEM((rows, width), F32), pltpu.VMEM((rows, width), F32),
+            pltpu.VMEM((ticks, 4, width, 128), BF16), pltpu.VMEM((ticks, 4, width, 128), BF16),
+            pltpu.VMEM((ticks, 4, width, 128), BF16), pltpu.VMEM((ticks, 4, width // 2, 128), BF16),
+            pltpu.VMEM((ticks, 4, width // 4, 128), BF16), pltpu.VMEM((ticks, deep - 1, 4, piece, 128), BF16),
+            dma((ticks, 3)), dma((ticks, 3)), dma((ticks, deep - 1)), dma((ticks, deep - 1)),
+        ],
+        compiler_params=pltpu.CompilerParams(vmem_limit_bytes=limit, collective_id=1, has_side_effects=True),
+        name="mlp_both_ways",
+    )(
+        hid, gm, att, mid, sel, sums, w_fc1, far_w1, row(b_fc1), far_b1, w_fc2, far_w2, w_proj, row(ln2_gain), row(b_fc2),
+    )
+    wide = width // groups
+    chunks = groups + 1
+    now = lambda g: g - g // groups
+    third = lambda lead, part: pl.BlockSpec((lead, wide), lambda g: (0, part * groups + now(g)))
+    big, attn, put, vec = pl.pallas_call(
+        functools.partial(attention_staged_kernel, deep, count, slots, groups, ticks),
+        grid=(groups + 1,),
+        out_shape=(
+            shape((4 * ticks, width, 128), BF16), shape((2, 3 * chunks, width, 128), BF16),
+            shape((count, patches, width), F32), shape((8, 2 * width), F32),
+        ),
+        in_specs=[
+            third(rows, 0), third(rows, 1), third(rows, 2),
+            pl.BlockSpec((count, heads // groups, slots, slots), lambda g: (0, now(g), 0, 0)),
+            third(rows, 0), third(width, 0), third(width, 1), third(width, 2),
+            whole((rows, width)), whole((rows, width)), whole((rows, width)), whole((count, slots, patches)),
+            whole((1, width)), whole((2, 3, width, 128)), whole((4 * ticks, piece, 128)), whole((8, 2 * width)),
+        ],
+        out_specs=(any_space, any_space, whole((count, patches, width)), whole((8, 2 * width))),
+        scratch_shapes=[
+            pltpu.VMEM((rows, wide), BF16), pltpu.VMEM((rows, wide), BF16), pltpu.VMEM((rows, wide), BF16),
+            pltpu.VMEM((rows, width), F32),
+            pltpu.VMEM((groups, 2, 3, width, 128), BF16), pltpu.VMEM((chunks, 3, width, 128), BF16),
+            pltpu.VMEM((chunks, 3, piece, 128), BF16), pltpu.VMEM((chunks, 3, width, 128), BF16),
+            pltpu.VMEM((chunks, 3, width // 2, 128), BF16), pltpu.VMEM((chunks, 3, width // 4, 128), BF16),
+            pltpu.VMEM((chunks, deep - 1, 3, piece, 128), BF16),
+            pltpu.VMEM((4, 8, 2 * width), F32), pltpu.VMEM((3, 8, 2 * width), F32),
+            pltpu.VMEM((deep - 1, 8, 2 * width), F32),
+            dma((chunks, 3)), dma((chunks, 3)), dma((chunks, deep - 1)), dma((chunks, deep - 1)),
+            dma((ticks,)), dma((ticks, 2)), dma((ticks, 2)), dma((ticks, deep - 1)), dma((ticks, deep - 1)),
+            dma((chunks,)), dma((chunks, 3)), dma((chunks, 3)), dma((chunks, deep - 1)), dma((chunks, deep - 1)),
+            dma((3,)), dma((3,)), dma((deep - 1,)), dma((deep - 1,)),
+        ],
+        compiler_params=pltpu.CompilerParams(vmem_limit_bytes=limit, collective_id=2, has_side_effects=True),
+        name="attention_backward",
+    )(
+        qkv, qkv, qkv, probs, gatt, w_qkv, w_qkv, w_qkv, normed, x, gmid, sel, row(ln1_gain), dwp, red, vec,
+    )
+    kept_at = (keep_mask > 0)[:, :, None]
+    layer_out = jnp.where(kept_at, low, images)
+    grad_images = jnp.where(kept_at, put, cotangent.astype(F32))
+    big = big.reshape(ticks, 4, width, 128)
+    s_w1 = big[:, :2].transpose(2, 0, 1, 3).reshape(width, shard).astype(F32)
+    s_w2 = big[:, 2:].reshape(ticks, 2, 3, chunk, 128).transpose(0, 3, 1, 2, 4).reshape(shard, width).astype(F32)
+    s_wp = attn[:, :3].transpose(2, 1, 0, 3).reshape(width, width).astype(F32)
+    s_wq = (
+        attn[:, 3:].reshape(2, groups, 3, width, 128).transpose(3, 2, 1, 0, 4).reshape(width, 3 * width).astype(F32)
+    )
+    flat = vec[:6].reshape(12, width)
+    root_means = jnp.sqrt(
+        jnp.stack([jnp.sum(flat[8]), jnp.sum(flat[10]), jnp.sum(flat[9])]) / (flat[11, 0] * width)
+    )
+    s_b1 = lax.dynamic_index_in_dim(vec[6:8], lax.axis_index("mlp"), 0, keepdims=False)
+    return (
+        layer_out, grad_images, flat[6], flat[7], s_wq, flat[4], flat[5], s_wp, flat[3], flat[0], flat[1],
+        s_w1, s_b1, s_w2, flat[2], root_means,
+    )
+
+
 def solution(mesh):
     rows, line = P(("img", "mlp"), None, None), P(("img", "mlp"), None)
+    deep = mesh.shape["img"] // 4
+    staged = mesh.shape["img"] == 4 * deep and mesh.shape["mlp"] == 2 and 1 < deep <= 4
     return jax.shard_map(
-        on_device,
+        functools.partial(staged_device, deep) if staged else plain_device,
         mesh=mesh,
         in_specs=(
             rows, line, P(), P(), P(), P(), P(), P(), P(), P(), P(),

time: 606 us -> 297 us (0.49)
  waiting for transfers between devices: 450 us -> 0 us
  Pallas kernels: 103 us -> 202 us
  local copies, waits for them, and re-layouts: 10.2 us -> 70.6 us
  between operations: 15 us -> 1.67 us
  other arithmetic: 26 us -> 18.3 us
    psum x3 -> x0, waiting for transfers between devices: 437 us -> none  [the longest x1 176 us: on_device(): s_w1, s_w2 = lax.psum((dw1s, dw2s), 'img')]
    pallas_call x3, Pallas kernels: 103 us -> 202 us  [the longest x1 106 us: staged_device(): pl.pallas_call(functools.partial(attention_staged_kernel, deep, count, sl...]
    unnamed x36 -> x13, local copies, waits for them, and re-layouts: 1.39 us -> 26.1 us
    convert_element_type x1 -> x3, local copies, waits for them, and re-layouts: 1.06 us -> 23.3 us  [the longest x2 21.3 us: staged_device(): attn[:, 3:].reshape(2, groups, 3, width, 128).transpose(3, 2, 1, 0, 4)]
    all_gather x2 -> x0, waiting for transfers between devices: 9.62 us -> none  [the longest x1 9.62 us: on_device(): whole_w2 = lax.all_gather(w_fc2, 'mlp')]
    reshape x9 -> x11, local copies, waits for them, and re-layouts: 5.25 us -> 12.8 us  [the longest x9 10.7 us: staged_device(): row = lambda v: v.reshape(1, -1)]
    slice x1 -> x4, local copies, waits for them, and re-layouts: 1.19 us -> 7.77 us  [the longest x1 4.15 us: staged_device(): big[:, 2:].reshape(ticks, 2, 3, chunk, 128).transpose(0, 3, 1, 2, 4)]
    convert_element_type x5 -> x4, other arithmetic: 14.4 us -> 8.32 us  [the longest x1 3.71 us: staged_device(): attn[:, 3:].reshape(2, groups, 3, width, 128).transpose(3, 2, 1, 0, 4)]
  transfers between devices with their start and end apart: 7 -> 0, of which waited for: 4 -> 0; matrix products, arithmetic and copies ran while one was open for 5% -> 0% of each run, Pallas kernels for 10% -> 0%
where the time goes in v2:
time: 297 us; the launch traced here: 293 us
  Pallas kernels  202 us (68%)
  local copies, waits for them, and re-layouts  70.6 us (24%)
  other arithmetic  18.3 us (6%)
    pallas_call x1, Pallas kernels, staged_device(): pl.pallas_call(functools.partial(attention_staged_kernel, deep, count, sl...  106 us
    pallas_call x1, Pallas kernels, staged_device(): pl.pallas_call(functools.partial(mlp_staged_kernel, deep, count, slots, t...  75.3 us
    unnamed x13, local copies, waits for them, and re-layouts  26.1 us
    convert_element_type x2, local copies, waits for them, and re-layouts, staged_device(): attn[:, 3:].reshape(2, groups, 3, width, 128).transpose(3, 2, 1, 0, 4)  21.3 us
    pallas_call x1, Pallas kernels, staged_device(): pl.pallas_call(functools.partial(forward_kernel, slots, True), grid=(coun...  20.4 us
    reshape x9, local copies, waits for them, and re-layouts, staged_device(): row = lambda v: v.reshape(1, -1)  10.7 us

profile of v2, /device:TPU:0, one launch (start us, length us, event | category | flops | bytes accessed | tf_op | source)
XLA Modules:
  0.0 292.6 jit_solution(15528067592525025372)
XLA Ops:
  0.6 1.3 reshape.100.refs_1_.b1a_ref
  1.9 1.3 reshape.93.g1_ref
  3.2 1.3 reshape.98.g2_ref
  4.5 1.3 reshape.92.keep_ref
  5.8 1.3 reshape.94.b1_ref
  12.1 20.4 %attention_forward.1 = (bf16[5,160,197]{2,1,0:T(8,128)(2,1)}, bf16[800,768]{1,0:T(8,128)(2,1)}, bf16[800,768]{1,0:T(8,128)(2,1)}, bf16[800,2304]{1,0:T(8,128)(2,...) custom-call(s32[5,1,197]{2,1,0:T(1,128)} %reshape.92.keep_ref, ...), custom_call_target="tpu_custom_call" | custom-call | tf_op jit(solution)/shard_map/attention_forward/pallas_call | solution.py:957
  33.1 75.3 %mlp_both_ways.1 = (bf16[24,48,128]{2,1,0:T(8,128)(2,1)}, f32[800,768]{1,0:T(8,128)}, bf16[800,768]{1,0:T(8,128)(2,1)}, bf16[2,3,768,128]{3,2,1,0:T(8,128)(2,1)}...) custom-call(bf16[800,768]{1,0:T(8,128)(2,1)} %get-tuple-element.39.hid_ref, bf16[800,768]{1,0:T(8,128)(2,1)} %get-tuple-element.40.gm_ref, ...), custom_call_target="tpu_custom_call" | custom-call | tf_op jit(solution)/shard_map/mlp_both_ways/pallas_call | solution.py:998
  108.4 106.4 %attention_backward.1 = (bf16[24,768,128]{2,1,0:T(8,128)(2,1)}, bf16[2,12,768,128]{3,2,1,0:T(8,128)(2,1)}, f32[5,197,768]{2,1,0:T(8,128)}, f32[8,1536]{1,0:T(8,128)}) custom-call(bf16[800,2304]{1,0:T(8,128)(2,1)} %get-tuple-element.49.q_ref.k_ref.v_ref, bf16[800,2304]{1,0:T(8,128)(2,1)} %get-tuple-element.49.q_ref.k_ref.v_ref, ...), custom_call_target="tpu_custom_call" | custom-call | tf_op jit(solution)/shard_map/attention_backward/pallas_call | solution.py:1031
  217.5 2.5 fusion
  220.0 2.3 slice.57
  222.3 3.7 %convert_bitcast_fusion = f32[768,3,3,2,128]{4,0,1,2,3:T(8,128)} fusion(bf16[2,3,3,768,128]{4,3,2,1,0:T(8,128)(2,1)S(1)} %bitcast.21), kind=kLoop, calls=%fused_computation | loop fusion | flops 1769472 | bytes 10616832 | tf_op jit(solution)/shard_map/convert_element_type | solution.py:1073
  226.0 11.3 %copy.45 = f32[768,3,3,2,128]{4,3,2,1,0:T(2,128)} copy(f32[768,3,3,2,128]{4,0,1,2,3:T(8,128)} %convert_bitcast_fusion) | data formatting | bytes 14155776 | tf_op jit(solution)/shard_map/convert_element_type | solution.py:1073
  237.3 10.0 %reshape.104 = f32[768,2304]{1,0:T(8,128)} reshape(f32[768,3,3,2,128]{4,3,2,1,0:T(2,128)} %copy.45) | data formatting | bytes 14155776 | tf_op jit(solution)/shard_map/convert_element_type | solution.py:1073
  247.3 4.2 %fusion.1 = (bf16[6,2,768,128]{3,2,1,0:T(8,128)(2,1)S(1)}, bf16[6,2,768,128]{3,2,1,0:T(8,128)(2,1)}) fusion(bf16[6,4,768,128]{3,2,1,0:T(8,128)(2,1)} %bitcast.24), kind=kLoop, calls=%fused_computation.20 | loop fusion | bytes 9437184 | tf_op jit(solution)/shard_map/slice | solution.py:1070
  252.0 5.9 %copy.52 = f32[6,256,2,3,128]{4,3,2,1,0:T(4,128)} copy(f32[6,256,2,3,128]{4,1,3,2,0:T(8,128)S(1)} %convert_bitcast_fusion.1) | data formatting | bytes 9437184
  257.9 8.2 %reshape.110 = f32[1536,768]{1,0:T(8,128)} reshape(f32[6,256,2,3,128]{4,3,2,1,0:T(4,128)} %copy.52) | data formatting | bytes 9437184
  266.1 2.8 copy.54
  268.9 2.6 convert_element_type.66
  271.6 6.0 %copy.50 = f32[768,1536]{1,0:T(8,128)} copy(f32[768,1536]{0,1:T(8,128)} %bitcast.20) | data formatting | bytes 9437184
  277.6 1.4 convert_bitcast_fusion.2
  279.0 2.0 copy.46
  281.0 3.2 %copy.49 = f32[768,768]{1,0:T(8,128)} copy(f32[768,768]{0,1:T(8,128)} %bitcast.23) | data formatting | bytes 4718592
  284.2 4.0 %convert_select_fusion = f32[5,197,768]{2,1,0:T(8,128)} fusion(f32[5,197,768]{2,1,0:T(8,128)} %get-tuple-element.58, bf16[5,197,768]{2,1,0:T(8,128)(2,1)S(1)} %copy-done, pred[5,197]{1,0:T(8,128)(4,1)S(1)} %broadcast_compare_fusion), kind=kLoop, calls=%fused_computation.2 | loop fusion | flops 1512960 | bytes 7565785 | tf_op jit(solution)/shard_map/jit(_where)/select_n | solution.py:1067
  289.6 2.8 broadcast_select_fusion
  (20 shorter events, 9.7 us)
Async XLA Ops:
  12.1 20.4 %copy-start.3 = (bf16[768]{0:T(1024)(128)(2,1)S(1)}, bf16[768]{0:T(1024)(128)(2,1)}, u32[]{:S(2)}) copy-start(bf16[768]{0:T(1024)(128)(2,1)} %param.30) | copy-start | bytes 4612
  281.0 3.2 %copy-start.2 = (s32[5,197]{1,0:T(8,128)S(1)}, s32[5,197]{1,0:T(8,128)}, u32[]{:S(2)}) copy-start(s32[5,197]{1,0:T(8,128)} %param.17) | copy-start | bytes 11824
  281.0 3.2 %copy-start = (bf16[5,197,768]{2,1,0:T(8,128)(2,1)S(1)}, bf16[5,197,768]{2,1,0:T(8,128)(2,1)}, u32[]{:S(2)}) copy-start(bf16[5,197,768]{2,1,0:T(8,128)(2,1)} %cot_ref.1) | copy-start | bytes 4538884
  284.2 5.4 %copy-start.1 = (bf16[5,197,768]{2,1,0:T(8,128)(2,1)S(1)}, bf16[5,197,768]{2,1,0:T(8,128)(2,1)}, u32[]{:S(2)}) copy-start(bf16[5,197,768]{2,1,0:T(8,128)(2,1)} %img_ref.1) | copy-start | bytes 4538884

commit v3 on v2

--- a/solution.py
+++ b/solution.py
@@ -94,6 +94,10 @@
     return trade
 
 
+def as_row(ref):
+    return ref[...].astype(F32).reshape(1, -1)
+
+
 def forward_kernel(
     slots, exchange,
     keep_ref, img_ref, cot_ref, g1_ref, b1_ref, wqkv_ref, bq_ref, bv_ref, wproj_ref, bproj_ref, g2_ref, b2_ref,
@@ -107,7 +111,7 @@
     sel_ref, x_ref, normed_ref, qkv_ref, probs_ref, att_ref, mid_ref, hid_ref, gm_ref, sums_ref = refs
     patches, width = img_ref.shape[1:]
     heads = width // HEAD_DIM
-    keep = keep_ref[0].astype(F32)
+    keep = keep_ref[pl.ds(pl.program_id(0), 1)].astype(F32)
     upto = lax.broadcasted_iota(jnp.int32, (patches, patches), 0) <= lax.broadcasted_iota(
         jnp.int32, (patches, patches), 1
     )
@@ -121,15 +125,15 @@
     rows = dot(sel, img_ref[0])
     x_ref[...] = rows.astype(BF16)
     scaled, _ = norm_rows(rows)
-    normed = (scaled * g1_ref[...] + b1_ref[...]).astype(BF16)
+    normed = (scaled * as_row(g1_ref) + as_row(b1_ref)).astype(BF16)
     normed_ref[...] = normed
     for part in range(3):
         cols = slice(part * width, (part + 1) * width)
         block = dot(normed, wqkv_ref[:, cols])
         if part == 0:
-            block = block + bq_ref[...].astype(F32)
+            block = block + as_row(bq_ref)
         if part == 2:
-            block = block + bv_ref[...].astype(F32)
+            block = block + as_row(bv_ref)
         qkv_ref[:, cols] = block.astype(BF16)
     closed = jnp.where(
         lax.broadcasted_iota(jnp.int32, (1, slots), 1).astype(F32) < count, 0.0, -1e30
@@ -151,7 +155,7 @@
             term = dot(probs, jnp.where(mine, value, zero))
             total = term if total is None else total + term
         att_ref[:, lanes] = total.astype(BF16)
-    attn_out = dot(att_ref[...], wproj_ref[...]) + bproj_ref[...].astype(F32)
+    attn_out = dot(att_ref[...], wproj_ref[...]) + as_row(bproj_ref)
     valid = lax.broadcasted_iota(jnp.int32, (slots, 1), 0).astype(F32) < count
     attn_kept = jnp.where(valid, attn_out, 0.0)
     middle = rows + attn_kept
@@ -159,7 +163,7 @@
     sums_ref[0, 0:1] = jnp.sum(attn_kept * attn_kept, axis=0, keepdims=True)
     sums_ref[0, 1:2] = jnp.broadcast_to(count, (1, width))
     scaled, _ = norm_rows(middle)
-    hid_ref[...] = (scaled * g2_ref[...] + b2_ref[...]).astype(BF16)
+    hid_ref[...] = (scaled * as_row(g2_ref) + as_row(b2_ref)).astype(BF16)
     if exchange:
         trade(False)
 
@@ -325,9 +329,9 @@
             shape((count, 8, width), F32),
         ),
         in_specs=[
-            per_image(1, patches), per_image(patches, width), per_image(patches, width),
-            whole((1, width)), whole((1, width)), whole((width, 3 * width)), whole((1, width)), whole((1, width)),
-            whole((width, width)), whole((1, width)), whole((1, width)), whole((1, width)),
+            whole((count, patches)), per_image(patches, width), per_image(patches, width),
+            whole((width,)), whole((width,)), whole((width, 3 * width)), whole((width,)), whole((width,)),
+            whole((width, width)), whole((width,)), whole((width,)), whole((width,)),
         ],
         out_specs=(
             per_image(slots, patches), per_rows(width), per_rows(width), per_rows(3 * width),
@@ -337,8 +341,7 @@
         compiler_params=limit,
         name="attention_forward",
     )(
-        keep_mask.reshape(count, 1, patches), images, cotangent, row(ln1_gain), row(ln1_bias), w_qkv,
-        row(bias_q), row(bias_v), w_proj, row(b_proj), row(ln2_gain), row(ln2_bias),
+        keep_mask, images, cotangent, ln1_gain, ln1_bias, w_qkv, bias_q, bias_v, w_proj, b_proj, ln2_gain, ln2_bias,
     )
     chunk = 512 if shard % 512 == 0 else 256
     each = shard // chunk
@@ -603,12 +606,13 @@
     hid_ref, gm_ref, att_ref, mid_ref, sel_ref, sums_ref, w1a_ref, w1b_ref, b1a_ref, b1b_ref, w2a_ref, w2b_ref,
     wproj_ref, g2_ref, bfc2_ref,
     red_ref, gmid_ref, gatt_ref, dwp_ref, lo_ref, vec_ref,
-    out_ref, gh_ref, give_ref, own_ref, got_core, got1, got2, got_z, send, recv, send_z, recv_z,
+    out_ref, gh_ref, bias_ref, give_ref, own_ref, got_core, got1, got2, got_z, send, recv, send_z, recv_z,
 ):
     step = pl.program_id(0)
     rows, width = hid_ref.shape
     place = Place(deep, width)
     panels = 4
+    chunk = w1a_ref.shape[1]
     reduce = Reduce(
         place, lambda c: own_ref.at[c], lambda c: give_ref.at[c], lambda c: own_ref.at[c],
         got_core, got1, got2, got_z, send, recv, send_z, recv_z,
@@ -617,11 +621,10 @@
     def put_red(c):
         red_ref[pl.ds(c * panels, panels)] = reduce.finish(c)
 
-    def half(w1_ref, b1_ref, w2_ref, target, db_row):
+    def half(w1_ref, b1, w2_ref, target, db_row):
         hid, gm = hid_ref[...], gm_ref[...]
         w1, w2 = w1_ref[...], w2_ref[...]
-        chunk = w1.shape[1]
-        pre = dot(hid, w1) + b1_ref[...].astype(F32)
+        pre = dot(hid, w1) + bias_ref[b1, pl.ds(step, 1)]
         act, slope = gelu_pair(pre)
         act = act.astype(BF16)
         grad_act = dot_t(gm, w2).astype(BF16).astype(F32)
@@ -643,6 +646,10 @@
         place.greet()
         out_ref[...] = jnp.zeros_like(out_ref)
         gh_ref[...] = jnp.zeros_like(gh_ref)
+        for side, ref in enumerate((b1a_ref, b1b_ref)):
+            line = as_row(ref)
+            for c in range(ticks):
+                bias_ref[side, c : c + 1] = line[:, c * chunk : (c + 1) * chunk]
         place.all_here()
 
     @pl.when((step >= 1) & (step <= ticks))
@@ -663,12 +670,12 @@
 
     @pl.when(step < ticks)
     def _():
-        half(w1b_ref, b1b_ref, w2b_ref, give_ref.at[step], 7 - place.core)
+        half(w1b_ref, 1, w2b_ref, give_ref.at[step], 7 - place.core)
 
     @pl.when(step < ticks)
     def _():
         reduce.begin(step, 0)
-        half(w1a_ref, b1a_ref, w2a_ref, own_ref.at[step], 6 + place.core)
+        half(w1a_ref, 0, w2a_ref, own_ref.at[step], 6 + place.core)
 
     def note(slot, value):
         at_row, at_col = vec_slot(slot, width)
@@ -686,7 +693,7 @@
             sel = sel_ref[i]
             middle = mid_ref[here]
             valid = jnp.sum(sel.astype(F32), axis=1, keepdims=True) > 0
-            mlp_out = jnp.where(valid, out_ref[here] + bfc2_ref[...].astype(F32), 0.0)
+            mlp_out = jnp.where(valid, out_ref[here] + as_row(bfc2_ref), 0.0)
             block = middle + mlp_out
             kept = jnp.where(valid, block, 0.0)
             stream = stream + column_sum(kept * kept)
@@ -698,7 +705,7 @@
             shift = shift + column_sum(grad_hidden)
             gm = gm_ref[here].astype(F32)
             b_two = b_two + column_sum(gm)
-            grad_middle = gm + norm_back(grad_hidden * g2_ref[...], scaled, inverse)
+            grad_middle = gm + norm_back(grad_hidden * as_row(g2_ref), scaled, inverse)
             gmid_ref[here] = grad_middle
             grad_attn = grad_middle.astype(BF16)
             b_proj = b_proj + column_sum(grad_attn.astype(F32))
@@ -885,7 +892,7 @@
             grad_normed = gn_ref[here]
             gain = gain + jnp.sum(grad_normed * scaled, axis=0, keepdims=True)
             shift = shift + jnp.sum(grad_normed, axis=0, keepdims=True)
-            change = gmid_ref[here] + norm_back(grad_normed * g1_ref[...], scaled, inverse)
+            change = gmid_ref[here] + norm_back(grad_normed * as_row(g1_ref), scaled, inverse)
             high = change.astype(BF16)
             rest = (change - high.astype(F32)).astype(BF16)
             gi_ref[i] = t_dot(sel, high) + t_dot(sel, rest)
@@ -938,6 +945,51 @@
                 copy.wait_send()
 
 
+def finish_kernel(
+    groups,
+    big_ref, attn_ref, low_ref, put_ref, img_ref, cot_ref, keep_ref, vec_ref,
+    lo_ref, gi_ref, wq_ref, wp_ref, w1_ref, w2_ref, b1_ref, root_ref, *small_refs,
+):
+    step = pl.program_id(0)
+    width = low_ref.shape[2]
+    chunk = w1_ref.shape[1]
+    for j in range(chunk // 128):
+        w1_ref[:, j * 128 : j * 128 + 128] = big_ref[j].astype(F32)
+    for j in range(width // 128):
+        at = j % 3 * chunk
+        w2_ref[:, j * 128 : j * 128 + 128] = big_ref[2 + j // 3, at : at + chunk].astype(F32)
+    for owner in range(2):
+        for j in range(3):
+            at = (2 * j + owner) * 128
+            wp_ref[:, at : at + 128] = attn_ref[owner, j].astype(F32)
+            for group in range(groups):
+                at = j * width + (2 * group + owner) * 128
+                wq_ref[:, at : at + 128] = attn_ref[owner, 3 + 3 * group + j].astype(F32)
+
+    @pl.when(step < keep_ref.shape[0])
+    def _():
+        keep = keep_ref[pl.ds(step, 1)].astype(F32)
+        eight = jnp.broadcast_to(keep, (8, keep.shape[1])).astype(BF16)
+        once = jnp.where(lax.broadcasted_iota(jnp.int32, (8, 128), 0) == 0, 1.0, 0.0).astype(BF16)
+        kept = t_dot(eight, once)[:, 0:1] > 0.5
+        lo_ref[0] = jnp.where(kept, low_ref[0], img_ref[0])
+        gi_ref[0] = jnp.where(kept, put_ref[0], cot_ref[0].astype(F32))
+
+    @pl.when(step == 0)
+    def _():
+        def line(slot):
+            at_row, at_col = vec_slot(slot, width)
+            return vec_ref[at_row, at_col]
+
+        for slot, ref in enumerate(small_refs):
+            ref[...] = line(slot).reshape(width)
+        b1_ref[...] = vec_ref[pl.ds(6 + lax.axis_index("mlp"), 1)].reshape(2 * width)
+        count = line(11)[:, 0:1]
+        lane = lax.broadcasted_iota(jnp.int32, (1, 128), 1)
+        sums = jnp.where(lane == 0, jnp.sum(line(8)), jnp.where(lane == 1, jnp.sum(line(10)), jnp.sum(line(9))))
+        root_ref[...] = jnp.sqrt(sums / (count * width)).reshape(128)[:3]
+
+
 def staged_device(
     deep, images, keep_mask, ln1_gain, ln1_bias, w_qkv, bias_q, bias_v, w_proj, b_proj,
     ln2_gain, ln2_bias, w_fc1, b_fc1, w_fc2, b_fc2, cotangent,
@@ -968,12 +1020,12 @@
             shape((rows, width), BF16),
             shape((rows, width), BF16),
             shape((count, 8, width), F32),
-            shape((width, shard), BF16), shape((1, shard), BF16), shape((shard, width), BF16),
+            shape((width, shard), BF16), shape((shard,), BF16), shape((shard, width), BF16),
         ),
         in_specs=[
-            per_image(1, patches), per_image(patches, width), per_image(patches, width),
-            whole((1, width)), whole((1, width)), whole((width, 3 * width)), whole((1, width)), whole((1, width)),
-            whole((width, width)), whole((1, width)), whole((1, width)), whole((1, width)),
+            whole((count, patches)), per_image(patches, width), per_image(patches, width),
+            whole((width,)), whole((width,)), whole((width, 3 * width)), whole((width,)), whole((width,)),
+            whole((width, width)), whole((width,)), whole((width,)), whole((width,)),
             any_space, any_space, any_space,
         ],
         out_specs=(
@@ -985,9 +1037,8 @@
         compiler_params=pltpu.CompilerParams(vmem_limit_bytes=limit, collective_id=0, has_side_effects=True),
         name="attention_forward",
     )(
-        keep_mask.reshape(count, 1, patches), images, cotangent, row(ln1_gain), row(ln1_bias), w_qkv,
-        row(bias_q), row(bias_v), w_proj, row(b_proj), row(ln2_gain), row(ln2_bias),
-        w_fc1, row(b_fc1), w_fc2,
+        keep_mask, images, cotangent, ln1_gain, ln1_bias, w_qkv, bias_q, bias_v, w_proj, b_proj, ln2_gain, ln2_bias,
+        w_fc1, b_fc1, w_fc2,
     )
     chunk = 256
     ticks = shard // chunk
@@ -1005,15 +1056,15 @@
         in_specs=[
             whole((rows, width)), whole((rows, width)), whole((rows, width)), whole((rows, width)),
             whole((count, slots, patches)), whole((count, 8, width)),
-            by_cols(width), by_cols(width), by_cols(1), by_cols(1), by_rows, by_rows,
-            whole((width, width)), whole((1, width)), whole((1, width)),
+            by_cols(width), by_cols(width), whole((shard,)), whole((shard,)), by_rows, by_rows,
+            whole((width, width)), whole((width,)), whole((width,)),
         ],
         out_specs=(
             whole((4 * ticks, piece, 128)), whole((rows, width)), whole((rows, width)),
             whole((2, 3, width, 128)), whole((count, patches, width)), whole((8, 2 * width)),
         ),
         scratch_shapes=[
-            pltpu.VMEM((rows, width), F32), pltpu.VMEM((rows, width), F32),
+            pltpu.VMEM((rows, width), F32), pltpu.VMEM((rows, width), F32), pltpu.VMEM((2, 8, chunk), F32),
             pltpu.VMEM((ticks, 4, width, 128), BF16), pltpu.VMEM((ticks, 4, width, 128), BF16),
             pltpu.VMEM((ticks, 4, width, 128), BF16), pltpu.VMEM((ticks, 4, width // 2, 128), BF16),
             pltpu.VMEM((ticks, 4, width // 4, 128), BF16), pltpu.VMEM((ticks, deep - 1, 4, piece, 128), BF16),
@@ -1022,7 +1073,7 @@
         compiler_params=pltpu.CompilerParams(vmem_limit_bytes=limit, collective_id=1, has_side_effects=True),
         name="mlp_both_ways",
     )(
-        hid, gm, att, mid, sel, sums, w_fc1, far_w1, row(b_fc1), far_b1, w_fc2, far_w2, w_proj, row(ln2_gain), row(b_fc2),
+        hid, gm, att, mid, sel, sums, w_fc1, far_w1, b_fc1, far_b1, w_fc2, far_w2, w_proj, ln2_gain, b_fc2,
     )
     wide = width // groups
     chunks = groups + 1
@@ -1040,7 +1091,7 @@
             pl.BlockSpec((count, heads // groups, slots, slots), lambda g: (0, now(g), 0, 0)),
             third(rows, 0), third(width, 0), third(width, 1), third(width, 2),
             whole((rows, width)), whole((rows, width)), whole((rows, width)), whole((count, slots, patches)),
-            whole((1, width)), whole((2, 3, width, 128)), whole((4 * ticks, piece, 128)), whole((8, 2 * width)),
+            whole((width,)), whole((2, 3, width, 128)), whole((4 * ticks, piece, 128)), whole((8, 2 * width)),
         ],
         out_specs=(any_space, any_space, whole((count, patches, width)), whole((8, 2 * width))),
         scratch_shapes=[
@@ -1060,26 +1111,38 @@
         compiler_params=pltpu.CompilerParams(vmem_limit_bytes=limit, collective_id=2, has_side_effects=True),
         name="attention_backward",
     )(
-        qkv, qkv, qkv, probs, gatt, w_qkv, w_qkv, w_qkv, normed, x, gmid, sel, row(ln1_gain), dwp, red, vec,
-    )
-    kept_at = (keep_mask > 0)[:, :, None]
-    layer_out = jnp.where(kept_at, low, images)
-    grad_images = jnp.where(kept_at, put, cotangent.astype(F32))
-    big = big.reshape(ticks, 4, width, 128)
-    s_w1 = big[:, :2].transpose(2, 0, 1, 3).reshape(width, shard).astype(F32)
-    s_w2 = big[:, 2:].reshape(ticks, 2, 3, chunk, 128).transpose(0, 3, 1, 2, 4).reshape(shard, width).astype(F32)
-    s_wp = attn[:, :3].transpose(2, 1, 0, 3).reshape(width, width).astype(F32)
-    s_wq = (
-        attn[:, 3:].reshape(2, groups, 3, width, 128).transpose(3, 2, 1, 0, 4).reshape(width, 3 * width).astype(F32)
-    )
-    flat = vec[:6].reshape(12, width)
-    root_means = jnp.sqrt(
-        jnp.stack([jnp.sum(flat[8]), jnp.sum(flat[10]), jnp.sum(flat[9])]) / (flat[11, 0] * width)
-    )
-    s_b1 = lax.dynamic_index_in_dim(vec[6:8], lax.axis_index("mlp"), 0, keepdims=False)
+        qkv, qkv, qkv, probs, gatt, w_qkv, w_qkv, w_qkv, normed, x, gmid, sel, ln1_gain, dwp, red, vec,
+    )
+    deal = width // ticks
+    turn = lambda t: (t - t // count, 0, 0)
+    layer_out, grad_images, s_wq, s_wp, s_w1, s_w2, s_b1, root_means, *small = pl.pallas_call(
+        functools.partial(finish_kernel, groups),
+        grid=(ticks,),
+        out_shape=(
+            shape((count, patches, width), BF16), shape((count, patches, width), F32),
+            shape((width, 3 * width), F32), shape((width, width), F32), shape((width, shard), F32),
+            shape((shard, width), F32), shape((shard,), F32), shape((3,), F32),
+        ) + 8 * (shape((width,), F32),),
+        in_specs=[
+            pl.BlockSpec((4, width, 128), lambda t: (t, 0, 0)),
+            pl.BlockSpec((2, 3 * chunks, deal, 128), lambda t: (0, 0, t, 0)),
+            pl.BlockSpec((1, patches, width), turn), pl.BlockSpec((1, patches, width), turn),
+            pl.BlockSpec((1, patches, width), turn), pl.BlockSpec((1, patches, width), turn),
+            whole((count, patches)), whole((8, 2 * width)),
+        ],
+        out_specs=(
+            pl.BlockSpec((1, patches, width), turn), pl.BlockSpec((1, patches, width), turn),
+            pl.BlockSpec((deal, 3 * width), lambda t: (t, 0)), pl.BlockSpec((deal, width), lambda t: (t, 0)),
+            pl.BlockSpec((width, chunk), lambda t: (0, t)), pl.BlockSpec((chunk, width), lambda t: (t, 0)),
+            whole((shard,)), whole((3,)),
+        ) + 8 * (whole((width,)),),
+        compiler_params=pltpu.CompilerParams(vmem_limit_bytes=limit),
+        name="results",
+    )(big, attn, low, put, images, cotangent, keep_mask, vec)
+    gain2, shift2, b_two, b_project, b_query, b_value, gain1, shift1 = small
     return (
-        layer_out, grad_images, flat[6], flat[7], s_wq, flat[4], flat[5], s_wp, flat[3], flat[0], flat[1],
-        s_w1, s_b1, s_w2, flat[2], root_means,
+        layer_out, grad_images, gain1, shift1, s_wq, b_query, b_value, s_wp, b_project, gain2, shift2,
+        s_w1, s_b1, s_w2, b_two, root_means,
     )
 
 

time: 297 us -> 218 us (0.73); the launches traced: 293 us -> 217 us
  local copies, waits for them, and re-layouts: 70.6 us -> 0 us
  other arithmetic: 18.3 us -> 0 us
  Pallas kernels: 202 us -> 216 us
    unnamed x13 -> x0, local copies, waits for them, and re-layouts: 26.1 us -> none
    convert_element_type x3 -> x0, local copies, waits for them, and re-layouts: 23.3 us -> none  [the longest x2 21.3 us: staged_device(): attn[:, 3:].reshape(2, groups, 3, width, 128).transpose(3, 2, 1, 0, 4)]
    pallas_call x0 -> x1, Pallas kernels: none -> 15.2 us  [staged_device(): pl.pallas_call(functools.partial(finish_kernel, groups), grid=(ticks,), o...]
    reshape x11 -> x0, local copies, waits for them, and re-layouts: 12.8 us -> none  [the longest x9 10.7 us: staged_device(): row = lambda v: v.reshape(1, -1)]
    convert_element_type x4 -> x0, other arithmetic: 8.32 us -> none  [the longest x1 3.71 us: staged_device(): attn[:, 3:].reshape(2, groups, 3, width, 128).transpose(3, 2, 1, 0, 4)]
    slice x4 -> x0, local copies, waits for them, and re-layouts: 7.77 us -> none  [the longest x1 4.15 us: staged_device(): big[:, 2:].reshape(ticks, 2, 3, chunk, 128).transpose(0, 3, 1, 2, 4)]
    select_n x2 -> x0, other arithmetic: 6.72 us -> none  [the longest x1 3.96 us: staged_device(): grad_images = jnp.where(kept_at, put, cotangent.astype(F32))]
where the time goes in v3:
time: 218 us; the launch traced here: 217 us
  Pallas kernels  216 us (99%)
    pallas_call x1, Pallas kernels, staged_device(): pl.pallas_call(functools.partial(attention_staged_kernel, deep, count, sl...  106 us
    pallas_call x1, Pallas kernels, staged_device(): pl.pallas_call(functools.partial(mlp_staged_kernel, deep, count, slots, t...  74.8 us
    pallas_call x1, Pallas kernels, staged_device(): pl.pallas_call(functools.partial(forward_kernel, slots, True), grid=(coun...  20.1 us
    pallas_call x1, Pallas kernels, staged_device(): pl.pallas_call(functools.partial(finish_kernel, groups), grid=(ticks,), o...  15.2 us

profile of v3, /device:TPU:0, one launch (start us, length us, event | category | flops | bytes accessed | tf_op | source)
XLA Modules:
  0.0 217.1 jit_solution(4197630486963549688)
XLA Ops:
  0.6 20.1 %attention_forward.1 = (bf16[5,160,197]{2,1,0:T(8,128)(2,1)}, bf16[800,768]{1,0:T(8,128)(2,1)}, bf16[800,768]{1,0:T(8,128)(2,1)}, bf16[800,2304]{1,0:T(8,128)(2,...) custom-call(s32[5,197]{1,0:T(8,128)} %keep_ref.3, ...), custom_call_target="tpu_custom_call" | custom-call | tf_op jit(solution)/shard_map/attention_forward/pallas_call | solution.py:1009
  20.8 74.8 %mlp_both_ways.1 = (bf16[24,48,128]{2,1,0:T(8,128)(2,1)}, f32[800,768]{1,0:T(8,128)}, bf16[800,768]{1,0:T(8,128)(2,1)}, bf16[2,3,768,128]{3,2,1,0:T(8,128)(2,1)}...) custom-call(bf16[800,768]{1,0:T(8,128)(2,1)} %get-tuple-element.57.hid_ref, bf16[800,768]{1,0:T(8,128)(2,1)} %get-tuple-element.58.gm_ref, ...), custom_call_target="tpu_custom_call" | custom-call | tf_op jit(solution)/shard_map/mlp_both_ways/pallas_call | solution.py:1049
  95.6 106.1 %attention_backward.1 = (bf16[24,768,128]{2,1,0:T(8,128)(2,1)}, bf16[2,12,768,128]{3,2,1,0:T(8,128)(2,1)}, f32[5,197,768]{2,1,0:T(8,128)}, f32[8,1536]{1,0:T(8,128)}) custom-call(bf16[800,2304]{1,0:T(8,128)(2,1)} %get-tuple-element.55.q_ref.k_ref.v_ref, bf16[800,2304]{1,0:T(8,128)(2,1)} %get-tuple-element.55.q_ref.k_ref.v_ref, ...), custom_call_target="tpu_custom_call" | custom-call | tf_op jit(solution)/shard_map/attention_backward/pallas_call | solution.py:1082
  201.7 15.2 %results.1 = (bf16[5,197,768]{2,1,0:T(8,128)(2,1)}, f32[5,197,768]{2,1,0:T(8,128)}, f32[768,2304]{1,0:T(8,128)}, f32[768,768]{1,0:T(8,128)}, f32[768,1536]{1,0:T...) custom-call(bf16[24,768,128]{2,1,0:T(8,128)(2,1)} %get-tuple-element, ...), custom_call_target="tpu_custom_call" | custom-call | tf_op jit(solution)/shard_map/results/pallas_call | solution.py:1118

commit v4 on v3

--- a/solution.py
+++ b/solution.py
@@ -605,8 +605,9 @@
     deep, images, slots, ticks,
     hid_ref, gm_ref, att_ref, mid_ref, sel_ref, sums_ref, w1a_ref, w1b_ref, b1a_ref, b1b_ref, w2a_ref, w2b_ref,
     wproj_ref, g2_ref, bfc2_ref,
-    red_ref, gmid_ref, gatt_ref, dwp_ref, lo_ref, vec_ref,
+    red_ref, gmid_ref, gatt_ref, dwp_ref, lo_ref, vec_ref, early_ref,
     out_ref, gh_ref, bias_ref, give_ref, own_ref, got_core, got1, got2, got_z, send, recv, send_z, recv_z,
+    b_local, b_send, b_recv, b_send_z, b_recv_z,
 ):
     step = pl.program_id(0)
     rows, width = hid_ref.shape
@@ -617,6 +618,12 @@
         place, lambda c: own_ref.at[c], lambda c: give_ref.at[c], lambda c: own_ref.at[c],
         got_core, got1, got2, got_z, send, recv, send_z, recv_z,
     )
+
+    back = Gather(
+        place, lambda c: red_ref.at[pl.ds(c * panels, panels)], lambda c: early_ref.at[pl.ds(c * panels, panels)],
+        None, b_local, b_send, b_recv, b_send_z, b_recv_z,
+    )
+    early = early_ref.shape[0] // panels
 
     def put_red(c):
         red_ref[pl.ds(c * panels, panels)] = reduce.finish(c)
@@ -656,6 +663,10 @@
     def _():
         reduce.plane1(step - 1)
 
+    @pl.when(step == ticks)
+    def _():
+        back.plane1(0)
+
     @pl.when((step >= 2) & (step <= ticks))
     def _():
         reduce.plane2(step - 2)
@@ -667,10 +678,15 @@
     @pl.when((step >= 4) & (step <= ticks))
     def _():
         put_red(step - 4)
+        back.along_z(step - 4)
 
     @pl.when(step < ticks)
     def _():
         half(w1b_ref, 1, w2b_ref, give_ref.at[step], 7 - place.core)
+
+    @pl.when(step == ticks - 1)
+    def _():
+        back.plane2(0)
 
     @pl.when(step < ticks)
     def _():
@@ -709,8 +725,9 @@
             gmid_ref[here] = grad_middle
             grad_attn = grad_middle.astype(BF16)
             b_proj = b_proj + column_sum(grad_attn.astype(F32))
-            hid_ref_out = grad_attn
             gatt_ref[here] = grad_attn
+            if i == 2:
+                back.plane2(1)
         for slot, value in enumerate((gain, shift, b_two, b_proj)):
             note(slot, value)
         note(8, stream)
@@ -720,6 +737,8 @@
         reduce.plane2(ticks - 1)
         reduce.along_z(ticks - 2)
         put_red(ticks - 3)
+        back.plane1(1)
+        back.plane2(2)
         grad_attn = gatt_ref[...]
         for part in range(3):
             cols = slice(part * width // 3, (part + 1) * width // 3)
@@ -729,11 +748,17 @@
         reduce.along_z(ticks - 1)
         put_red(ticks - 2)
         gatt_ref[...] = dot_t(grad_attn, wproj_ref[...]).astype(BF16)
+        back.plane1(2)
         put_red(ticks - 1)
 
         @pl.loop(0, ticks)
         def _(c):
             reduce.sent(c)
+
+        @pl.loop(0, early)
+        def _(c):
+            back.arrive(c, 2)
+            back.sent(c)
 
 
 def attention_staged_kernel(
@@ -768,8 +793,9 @@
         place, lambda c: piece_ref.at[c], lambda c: attn_ref.at[core, pl.ds(3 * c, 3)],
         lambda c: attn_ref.at[1 - core, pl.ds(3 * c, 3)], a_local, a_send, a_recv, a_send_z, a_recv_z,
     )
+    late = mlp_ref.shape[0] // 4
     mlp = Gather(
-        place, lambda c: red_ref.at[pl.ds(4 * c, 4)], lambda c: mlp_ref.at[pl.ds(4 * c, 4)], None,
+        place, lambda c: red_ref.at[pl.ds(4 * (ticks - late + c), 4)], lambda c: mlp_ref.at[pl.ds(4 * c, 4)], None,
         m_local, m_send, m_recv, m_send_z, m_recv_z,
     )
 
@@ -782,20 +808,23 @@
             "X": reduce.plane1, "Y": reduce.plane2, "Z": reduce.along_z, "R": turn,
             "ay": back.plane2, "ax": back.plane1, "ac": back.across,
             "my": mlp.plane2, "mx": mlp.plane1,
-        }[name](c)
+        }[name](c - (ticks - late) if name[0] == "m" else c)
 
     plan = {}
     for at, name, c in (
-        (1, "X", 0), (3, "my", 0), (4, "Y", 0), (6, "mx", 0), (6, "Z", 0),
-        (7, "my", 1), (8, "X", 1), (9, "R", 0), (10, "mx", 1), (11, "Y", 1), (11, "my", 2), (12, "ay", 0),
-        (13, "Z", 1), (14, "mx", 2), (15, "X", 2), (15, "ax", 0), (16, "R", 1), (16, "my", 3), (18, "Y", 2),
-        (18, "mx", 3), (19, "ay", 1), (20, "Z", 2),
+        (2, "X", 0), (6, "Y", 0), (8, "my", 3), (9, "X", 1), (9, "my", 4), (10, "Z", 0), (12, "my", 5),
+        (13, "mx", 3), (15, "R", 0), (16, "X", 2), (16, "Y", 1), (20, "ay", 0), (20, "Z", 1), (23, "X", 3),
     ):
         plan.setdefault(at, []).append((name, c))
+    tail = (
+        ("ax", 0), ("Y", 2), ("R", 1), ("Y", 3), ("Z", 2), ("mx", 5), ("ay", 1), ("Z", 3), ("ac", 0), ("R", 2),
+        ("ax", 1), ("R", 3), ("mx", 4), ("ac", 1), ("ay", 2), ("ay", 3), ("ax", 2), ("ax", 3), ("ac", 2),
+        ("ac", 3),
+    )
 
     def run(at, now):
         for moment, jobs in sorted(plan.items()):
-            if at(moment % polls):
+            if moment < groups * polls and at(moment % polls):
 
                 @pl.when(now == moment)
                 def _(jobs=jobs):
@@ -815,7 +844,7 @@
         vsum_ref[0] = vecin_ref[...]
         place.all_here()
         reduce.begin(0, 0)
-        for c in range(ticks):
+        for c in range(late):
             mlp.along_z(c)
 
     @pl.when(step < groups)
@@ -852,12 +881,13 @@
         shifted = pl.ds(pl.multiple_of(width + step * wide, wide), wide)
         vsum_ref[0, 2:3, cols] = jnp.sum(gq_ref[...].astype(F32), axis=0, keepdims=True)
         vsum_ref[0, 2:3, shifted] = jnp.sum(gv_ref[...].astype(F32), axis=0, keepdims=True)
-        for part, (ref, w_ref) in enumerate(((gq_ref, wq_ref), (gk_ref, wk_ref), (gv_ref, wv_ref))):
+        for part, ref in enumerate((gq_ref, gk_ref, gv_ref)):
             d = t_dot(normed_ref[...], ref[...]).astype(BF16)
             stage_ref[step, 0, part] = d[:, :128]
             stage_ref[step, 1, part] = d[:, 128:]
+        reduce.begin(step + 1, 0)
+        for ref, w_ref in ((gq_ref, wq_ref), (gk_ref, wk_ref), (gv_ref, wv_ref)):
             gn_ref[...] += dot_t(ref[...], w_ref[...])
-        reduce.begin(step + 1, 0)
         run(lambda at: at == images + 1, step * polls + images + 1)
 
     def vec_copies(stage):
@@ -882,46 +912,30 @@
 
     @pl.when(step == groups)
     def _():
-        last = groups
-        do("X", last)
+        g1 = as_row(g1_ref)
         gain = shift = jnp.zeros((1, width), F32)
         for i in range(images):
+            for name, c in plan.get(groups * polls + i, ()):
+                do(name, c)
             here = slice(i * slots, i * slots + slots)
             sel = sel_ref[i]
             scaled, inverse = norm_rows(x_ref[here].astype(F32))
             grad_normed = gn_ref[here]
             gain = gain + jnp.sum(grad_normed * scaled, axis=0, keepdims=True)
             shift = shift + jnp.sum(grad_normed, axis=0, keepdims=True)
-            change = gmid_ref[here] + norm_back(grad_normed * as_row(g1_ref), scaled, inverse)
+            change = gmid_ref[here] + norm_back(grad_normed * g1, scaled, inverse)
             high = change.astype(BF16)
             rest = (change - high.astype(F32)).astype(BF16)
             gi_ref[i] = t_dot(sel, high) + t_dot(sel, rest)
-            if i == 1:
-                do("R", 2)
-                do("ax", 1)
-                do("my", 4)
-            if i == 3:
-                do("Y", last)
-                do("mx", 4)
-                do("ac", 0)
         at_row, at_col = vec_slot(6, width)
         vsum_ref[0, at_row, at_col] = gain
         at_row, at_col = vec_slot(7, width)
         vsum_ref[0, at_row, at_col] = shift
         vec_begin(0)
-        do("Z", last)
-        do("ay", 2)
-        vec_next(0)
-        do("my", 5)
-        do("R", last)
-        vec_next(1)
-        do("ax", 2)
-        do("ac", 1)
-        do("ay", last)
-        vec_next(2)
-        do("mx", 5)
-        do("ax", last)
-        vec_next(3)
+        for at, (name, c) in enumerate(tail):
+            do(name, c)
+            if at % 3 == 2 and at // 3 < 4:
+                vec_next(at // 3)
         value = None
         for z in range(deep):
             mine = vsum_ref[3]
@@ -931,9 +945,7 @@
                 term = jnp.where((place.z - k - 1 + deep) % deep == z, from_k[k], term)
             value = term if value is None else value + term
         vec_ref[...] = value
-        do("ac", 2)
-        do("ac", last)
-        for c in range(ticks):
+        for c in range(late):
             mlp.arrive(c, 2)
             mlp.sent(c)
         for c in range(groups + 1):
@@ -946,18 +958,23 @@
 
 
 def finish_kernel(
-    groups,
-    big_ref, attn_ref, low_ref, put_ref, img_ref, cot_ref, keep_ref, vec_ref,
+    groups, early,
+    first_ref, second_ref, attn_ref, low_ref, put_ref, img_ref, cot_ref, keep_ref, vec_ref,
     lo_ref, gi_ref, wq_ref, wp_ref, w1_ref, w2_ref, b1_ref, root_ref, *small_refs,
 ):
     step = pl.program_id(0)
     width = low_ref.shape[2]
     chunk = w1_ref.shape[1]
-    for j in range(chunk // 128):
-        w1_ref[:, j * 128 : j * 128 + 128] = big_ref[j].astype(F32)
-    for j in range(width // 128):
-        at = j % 3 * chunk
-        w2_ref[:, j * 128 : j * 128 + 128] = big_ref[2 + j // 3, at : at + chunk].astype(F32)
+    for big_ref, mine in ((first_ref, step < early), (second_ref, step >= early)):
+
+        @pl.when(mine)
+        def _(big_ref=big_ref):
+            for j in range(chunk // 128):
+                w1_ref[:, j * 128 : j * 128 + 128] = big_ref[j].astype(F32)
+            for j in range(width // 128):
+                at = j % 3 * chunk
+                w2_ref[:, j * 128 : j * 128 + 128] = big_ref[2 + j // 3, at : at + chunk].astype(F32)
+
     for owner in range(2):
         for j in range(3):
             at = (2 * j + owner) * 128
@@ -1046,12 +1063,14 @@
     piece = width // 4 // deep
     by_cols = lambda *lead: pl.BlockSpec(lead + (chunk,), lambda c: (0, c - c // ticks))
     by_rows = pl.BlockSpec((chunk, width), lambda c: (c - c // ticks, 0))
-    red, gmid, gatt, dwp, low, vec = pl.pallas_call(
+    early = ticks // 2
+    red, gmid, gatt, dwp, low, vec, first = pl.pallas_call(
         functools.partial(mlp_staged_kernel, deep, count, slots, ticks),
         grid=(ticks + 1,),
         out_shape=(
             shape((4 * ticks, piece, 128), BF16), shape((rows, width), F32), shape((rows, width), BF16),
             shape((2, 3, width, 128), BF16), shape((count, patches, width), BF16), shape((8, 2 * width), F32),
+            shape((4 * early, width, 128), BF16),
         ),
         in_specs=[
             whole((rows, width)), whole((rows, width)), whole((rows, width)), whole((rows, width)),
@@ -1061,7 +1080,7 @@
         ],
         out_specs=(
             whole((4 * ticks, piece, 128)), whole((rows, width)), whole((rows, width)),
-            whole((2, 3, width, 128)), whole((count, patches, width)), whole((8, 2 * width)),
+            whole((2, 3, width, 128)), whole((count, patches, width)), whole((8, 2 * width)), any_space,
         ),
         scratch_shapes=[
             pltpu.VMEM((rows, width), F32), pltpu.VMEM((rows, width), F32), pltpu.VMEM((2, 8, chunk), F32),
@@ -1069,6 +1088,7 @@
             pltpu.VMEM((ticks, 4, width, 128), BF16), pltpu.VMEM((ticks, 4, width // 2, 128), BF16),
             pltpu.VMEM((ticks, 4, width // 4, 128), BF16), pltpu.VMEM((ticks, deep - 1, 4, piece, 128), BF16),
             dma((ticks, 3)), dma((ticks, 3)), dma((ticks, deep - 1)), dma((ticks, deep - 1)),
+            dma((early,)), dma((early, 2)), dma((early, 2)), dma((early, deep - 1)), dma((early, deep - 1)),
         ],
         compiler_params=pltpu.CompilerParams(vmem_limit_bytes=limit, collective_id=1, has_side_effects=True),
         name="mlp_both_ways",
@@ -1079,11 +1099,12 @@
     chunks = groups + 1
     now = lambda g: g - g // groups
     third = lambda lead, part: pl.BlockSpec((lead, wide), lambda g: (0, part * groups + now(g)))
-    big, attn, put, vec = pl.pallas_call(
+    late = ticks - early
+    second, attn, put, vec = pl.pallas_call(
         functools.partial(attention_staged_kernel, deep, count, slots, groups, ticks),
         grid=(groups + 1,),
         out_shape=(
-            shape((4 * ticks, width, 128), BF16), shape((2, 3 * chunks, width, 128), BF16),
+            shape((4 * late, width, 128), BF16), shape((2, 3 * chunks, width, 128), BF16),
             shape((count, patches, width), F32), shape((8, 2 * width), F32),
         ),
         in_specs=[
@@ -1104,7 +1125,7 @@
             pltpu.VMEM((4, 8, 2 * width), F32), pltpu.VMEM((3, 8, 2 * width), F32),
             pltpu.VMEM((deep - 1, 8, 2 * width), F32),
             dma((chunks, 3)), dma((chunks, 3)), dma((chunks, deep - 1)), dma((chunks, deep - 1)),
-            dma((ticks,)), dma((ticks, 2)), dma((ticks, 2)), dma((ticks, deep - 1)), dma((ticks, deep - 1)),
+            dma((late,)), dma((late, 2)), dma((late, 2)), dma((late, deep - 1)), dma((late, deep - 1)),
             dma((chunks,)), dma((chunks, 3)), dma((chunks, 3)), dma((chunks, deep - 1)), dma((chunks, deep - 1)),
             dma((3,)), dma((3,)), dma((deep - 1,)), dma((deep - 1,)),
         ],
@@ -1116,7 +1137,7 @@
     deal = width // ticks
     turn = lambda t: (t - t // count, 0, 0)
     layer_out, grad_images, s_wq, s_wp, s_w1, s_w2, s_b1, root_means, *small = pl.pallas_call(
-        functools.partial(finish_kernel, groups),
+        functools.partial(finish_kernel, groups, early),
         grid=(ticks,),
         out_shape=(
             shape((count, patches, width), BF16), shape((count, patches, width), F32),
@@ -1124,7 +1145,8 @@
             shape((shard, width), F32), shape((shard,), F32), shape((3,), F32),
         ) + 8 * (shape((width,), F32),),
         in_specs=[
-            pl.BlockSpec((4, width, 128), lambda t: (t, 0, 0)),
+            pl.BlockSpec((4, width, 128), lambda t: (jnp.minimum(t, early - 1), 0, 0)),
+            pl.BlockSpec((4, width, 128), lambda t: (jnp.maximum(t - early, 0), 0, 0)),
             pl.BlockSpec((2, 3 * chunks, deal, 128), lambda t: (0, 0, t, 0)),
             pl.BlockSpec((1, patches, width), turn), pl.BlockSpec((1, patches, width), turn),
             pl.BlockSpec((1, patches, width), turn), pl.BlockSpec((1, patches, width), turn),
@@ -1138,7 +1160,7 @@
         ) + 8 * (whole((width,)),),
         compiler_params=pltpu.CompilerParams(vmem_limit_bytes=limit),
         name="results",
-    )(big, attn, low, put, images, cotangent, keep_mask, vec)
+    )(first, second, attn, low, put, images, cotangent, keep_mask, vec)
     gain2, shift2, b_two, b_project, b_query, b_value, gain1, shift1 = small
     return (
         layer_out, grad_images, gain1, shift1, s_wq, b_query, b_value, s_wp, b_project, gain2, shift2,

time: 218 us -> 205 us (0.940)
  Pallas kernels: 216 us -> 204 us
    pallas_call x1, Pallas kernels: 106 us -> 81.7 us  [staged_device(): pl.pallas_call(functools.partial(attention_staged_kernel, deep, count, sl...]
    pallas_call x1, Pallas kernels: 74.8 us -> 87 us  [staged_device(): pl.pallas_call(functools.partial(mlp_staged_kernel, deep, count, slots, t...]
where the time goes in v4:
time: 205 us
  Pallas kernels  204 us (100%)
    pallas_call x1, Pallas kernels, staged_device(): pl.pallas_call(functools.partial(mlp_staged_kernel, deep, count, slots, t...  87 us
    pallas_call x1, Pallas kernels, staged_device(): pl.pallas_call(functools.partial(attention_staged_kernel, deep, count, sl...  81.7 us
    pallas_call x1, Pallas kernels, staged_device(): pl.pallas_call(functools.partial(forward_kernel, slots, True), grid=(coun...  20.1 us
    pallas_call x1, Pallas kernels, staged_device(): pl.pallas_call(functools.partial(finish_kernel, groups, early), grid=(tic...  15.5 us

profile of v4, /device:TPU:0, one launch (start us, length us, event | category | flops | bytes accessed | tf_op | source)
XLA Modules:
  0.0 205.2 jit_solution(7644975394104552226)
XLA Ops:
  0.6 20.1 %attention_forward.1 = (bf16[5,160,197]{2,1,0:T(8,128)(2,1)}, bf16[800,768]{1,0:T(8,128)(2,1)}, bf16[800,768]{1,0:T(8,128)(2,1)}, bf16[800,2304]{1,0:T(8,128)(2,...) custom-call(s32[5,197]{1,0:T(8,128)} %keep_ref.3, ...), custom_call_target="tpu_custom_call" | custom-call | tf_op jit(solution)/shard_map/attention_forward/pallas_call | solution.py:1026
  20.8 87.0 %mlp_both_ways.1 = (bf16[24,48,128]{2,1,0:T(8,128)(2,1)}, f32[800,768]{1,0:T(8,128)}, bf16[800,768]{1,0:T(8,128)(2,1)}, bf16[2,3,768,128]{3,2,1,0:T(8,128)(2,1)}...) custom-call(bf16[800,768]{1,0:T(8,128)(2,1)} %get-tuple-element.56.hid_ref, ...), custom_call_target="tpu_custom_call" | custom-call | tf_op jit(solution)/shard_map/mlp_both_ways/pallas_call | solution.py:1067
  107.8 81.7 %attention_backward.1 = (bf16[12,768,128]{2,1,0:T(8,128)(2,1)}, bf16[2,12,768,128]{3,2,1,0:T(8,128)(2,1)}, f32[5,197,768]{2,1,0:T(8,128)}, f32[8,1536]{1,0:T(8,128)}) custom-call(bf16[800,2304]{1,0:T(8,128)(2,1)} %get-tuple-element.66.q_ref.k_ref.v_ref, bf16[800,2304]{1,0:T(8,128)(2,1)} %get-tuple-element.66.q_ref.k_ref.v_ref, ...), custom_call_target="tpu_custom_call" | custom-call | tf_op jit(solution)/shard_map/attention_backward/pallas_call | solution.py:1103
  189.5 15.5 %results.1 = (bf16[5,197,768]{2,1,0:T(8,128)(2,1)}, f32[5,197,768]{2,1,0:T(8,128)}, f32[768,2304]{1,0:T(8,128)}, f32[768,768]{1,0:T(8,128)}, f32[768,1536]{1,0:T...) custom-call(bf16[12,768,128]{2,1,0:T(8,128)(2,1)} %get-tuple-element, ...), custom_call_target="tpu_custom_call" | custom-call | tf_op jit(solution)/shard_map/results/pallas_call | solution.py:1139

commit v5 on v4

--- a/solution.py
+++ b/solution.py
@@ -601,11 +601,43 @@
     return slice(slot // 2, slot // 2 + 1), slice(slot % 2 * width, slot % 2 * width + width)
 
 
+def head_back(slots, i, q_ref, k_ref, v_ref, probs_ref, gatt_ref, gq_ref, gk_ref, gv_ref):
+    first = lax.broadcasted_iota(jnp.int32, (1, 2 * HEAD_DIM), 1) < HEAD_DIM
+    zero = jnp.zeros((), BF16)
+    scale = jnp.asarray(HEAD_DIM ** -0.5, BF16)
+    pairs = q_ref.shape[1] // 128
+    here = pl.ds(pl.multiple_of(i * slots, 16), slots)
+    for pair in range(pairs):
+        own = slice(pair * 128, pair * 128 + 128)
+        query, key, value = q_ref[here, own], k_ref[here, own], v_ref[here, own]
+        grad_att = gatt_ref[here, own]
+        gq = gk = gv = None
+        for half in range(2):
+            mine = first if half == 0 else jnp.logical_not(first)
+            low = probs_ref[i, 2 * pair + half]
+            probs = low.astype(F32)
+            g_mine = jnp.where(mine, grad_att, zero)
+            grad_probs = dot_t(g_mine, value).astype(BF16).astype(F32)
+            inner = jnp.sum(probs * grad_probs, axis=1, keepdims=True)
+            grad_scores = (probs * (grad_probs - inner)).astype(BF16) * scale
+            tv = t_dot(low, g_mine)
+            tq = dot(grad_scores, jnp.where(mine, key, zero))
+            tk = t_dot(grad_scores, jnp.where(mine, query, zero))
+            gq = tq if gq is None else gq + tq
+            gk = tk if gk is None else gk + tk
+            gv = tv if gv is None else gv + tv
+        gq_ref[here, own] = gq.astype(BF16)
+        gk_ref[here, own] = gk.astype(BF16)
+        gv_ref[here, own] = gv.astype(BF16)
+
+
 def mlp_staged_kernel(
     deep, images, slots, ticks,
-    hid_ref, gm_ref, att_ref, mid_ref, sel_ref, sums_ref, w1a_ref, w1b_ref, b1a_ref, b1b_ref, w2a_ref, w2b_ref,
-    wproj_ref, g2_ref, bfc2_ref,
-    red_ref, gmid_ref, gatt_ref, dwp_ref, lo_ref, vec_ref, early_ref,
+    hid_ref, gm_ref, sums_ref, w1a_ref, w1b_ref, b1a_ref, b1b_ref, w2a_ref, w2b_ref, g2_ref, bfc2_ref,
+    att_hbm, mid_hbm, sel_hbm, wproj_hbm, normed_hbm, qkv_hbm, probs_hbm, wqkv_hbm,
+    red_ref, gmid_ref, gatt_ref, dwp_ref, lo_ref, vec_ref, early_ref, dwh_ref, gn_hbm,
+    att_ref, mid_ref, sel_ref, wproj_ref, normed_ref, q_ref, k_ref, v_ref, probs_ref, wq_ref, wk_ref, wv_ref,
+    gq_ref, gk_ref, gv_ref, fetch_sem,
     out_ref, gh_ref, bias_ref, give_ref, own_ref, got_core, got1, got2, got_z, send, recv, send_z, recv_z,
     b_local, b_send, b_recv, b_send_z, b_recv_z,
 ):
@@ -624,6 +656,15 @@
         None, b_local, b_send, b_recv, b_send_z, b_recv_z,
     )
     early = early_ref.shape[0] // panels
+
+    wide = q_ref.shape[1]
+    thirds = [slice(part * width, part * width + wide) for part in range(3)]
+    sources = [att_hbm, mid_hbm, sel_hbm, wproj_hbm, normed_hbm] + [qkv_hbm.at[:, cols] for cols in thirds]
+    sources += [probs_hbm.at[:, 0 : probs_ref.shape[1]]] + [wqkv_hbm.at[:, cols] for cols in thirds]
+    held = [att_ref, mid_ref, sel_ref, wproj_ref, normed_ref, q_ref, k_ref, v_ref, probs_ref, wq_ref, wk_ref, wv_ref]
+    fetched = [
+        pltpu.make_async_copy(source, target, fetch_sem.at[j]) for j, (source, target) in enumerate(zip(sources, held))
+    ]
 
     def put_red(c):
         red_ref[pl.ds(c * panels, panels)] = reduce.finish(c)
@@ -650,6 +691,8 @@
 
     @pl.when(step == 0)
     def _():
+        for copy in fetched:
+            copy.start()
         place.greet()
         out_ref[...] = jnp.zeros_like(out_ref)
         gh_ref[...] = jnp.zeros_like(gh_ref)
@@ -702,6 +745,8 @@
 
     @pl.when(step == ticks)
     def _():
+        for copy in fetched:
+            copy.wait()
         stream = mlp_sq = jnp.zeros((1, width), F32)
         gain = shift = b_two = b_proj = jnp.zeros((1, width), F32)
         for i in range(images):
@@ -745,11 +790,35 @@
             d = t_dot(att_ref[...], grad_attn[:, cols]).astype(BF16)
             dwp_ref[0, part] = d[:, :128]
             dwp_ref[1, part] = d[:, 128:]
-        reduce.along_z(ticks - 1)
-        put_red(ticks - 2)
         gatt_ref[...] = dot_t(grad_attn, wproj_ref[...]).astype(BF16)
-        back.plane1(2)
+
+        @pl.loop(0, images)
+        def _(i):
+            @pl.when(i == 2)
+            def _():
+                reduce.along_z(ticks - 1)
+                back.plane1(2)
+
+            @pl.when(i == 4)
+            def _():
+                put_red(ticks - 2)
+
+            head_back(slots, i, q_ref, k_ref, v_ref, probs_ref, gatt_ref, gq_ref, gk_ref, gv_ref)
+
+        vec_ref[2:3, 0:wide] = column_sum(gq_ref[...].astype(F32))
+        vec_ref[2:3, width : width + wide] = column_sum(gv_ref[...].astype(F32))
+        total = None
+        for part, (ref, w_ref) in enumerate(((gq_ref, wq_ref), (gk_ref, wk_ref), (gv_ref, wv_ref))):
+            d = t_dot(normed_ref[...], ref[...]).astype(BF16)
+            dwh_ref[0, part] = d[:, :128]
+            dwh_ref[1, part] = d[:, 128:]
+            term = dot_t(ref[...], w_ref[...])
+            total = term if total is None else total + term
+        gh_ref[...] = total
+        keep_gn = pltpu.make_async_copy(gh_ref, gn_hbm, fetch_sem.at[0])
+        keep_gn.start()
         put_red(ticks - 1)
+        keep_gn.wait()
 
         @pl.loop(0, ticks)
         def _(c):
@@ -763,25 +832,32 @@
 
 def attention_staged_kernel(
     deep, images, slots, groups, ticks,
-    q_ref, k_ref, v_ref, probs_ref, gatt_ref, wq_ref, wk_ref, wv_ref, normed_ref, x_ref, gmid_ref, sel_ref, g1_ref,
-    dwp_ref, red_ref, vecin_ref,
+    q_ref, k_ref, v_ref, probs_ref, gatt_ref, wq_ref, wk_ref, wv_ref, g1_ref, dwp_ref, dwh_ref, red_ref, vecin_ref,
+    normed_hbm, x_hbm, gmid_hbm, sel_hbm, gn_hbm,
     mlp_ref, attn_ref, gi_ref, vec_ref,
     gq_ref, gk_ref, gv_ref, gn_ref, stage_ref, total_ref, piece_ref, got_core, got1, got2, got_z,
     vsum_ref, vgot_ref, vz_ref,
     send, recv, send_z, recv_z, m_local, m_send, m_recv, m_send_z, m_recv_z,
     a_local, a_send, a_recv, a_send_z, a_recv_z, v_send, v_recv, v_send_z, v_recv_z,
+    normed_ref, x_ref, gmid_ref, sel_ref, fetch_sem,
 ):
     step = pl.program_id(0)
     rows, width = x_ref.shape
+    fetched = [
+        pltpu.make_async_copy(source, target, fetch_sem.at[j])
+        for j, (source, target) in enumerate(
+            ((normed_hbm, normed_ref), (gn_hbm, gn_ref), (x_hbm, x_ref), (gmid_hbm, gmid_ref), (sel_hbm, sel_ref))
+        )
+    ]
     place = Place(deep, width)
     core = place.core
     polls = images + 2
 
     def partial_of(owner):
         def pick(c):
-            if isinstance(c, int) and c == 0:
-                return dwp_ref.at[owner]
-            return stage_ref.at[c - 1, owner]
+            if isinstance(c, int) and c < 2:
+                return (dwp_ref, dwh_ref)[c].at[owner]
+            return stage_ref.at[c - 2, owner]
 
         return pick
 
@@ -812,13 +888,13 @@
 
     plan = {}
     for at, name, c in (
-        (2, "X", 0), (6, "Y", 0), (8, "my", 3), (9, "X", 1), (9, "my", 4), (10, "Z", 0), (12, "my", 5),
-        (13, "mx", 3), (15, "R", 0), (16, "X", 2), (16, "Y", 1), (20, "ay", 0), (20, "Z", 1), (23, "X", 3),
+        (2, "X", 0), (2, "X", 1), (6, "Y", 0), (8, "my", 3), (9, "X", 2), (9, "Y", 1), (10, "Z", 0), (12, "my", 5),
+        (13, "mx", 3), (15, "Z", 1), (16, "Y", 2), (16, "X", 3), (16, "R", 0), (18, "my", 4),
     ):
         plan.setdefault(at, []).append((name, c))
     tail = (
-        ("ax", 0), ("Y", 2), ("R", 1), ("Y", 3), ("Z", 2), ("mx", 5), ("ay", 1), ("Z", 3), ("ac", 0), ("R", 2),
-        ("ax", 1), ("R", 3), ("mx", 4), ("ac", 1), ("ay", 2), ("ay", 3), ("ax", 2), ("ax", 3), ("ac", 2),
+        ("Z", 2), ("R", 1), ("ay", 0), ("mx", 5), ("Y", 3), ("R", 2), ("ax", 0), ("ay", 1), ("Z", 3), ("ay", 2),
+        ("ax", 1), ("ac", 0), ("R", 3), ("mx", 4), ("ax", 2), ("ac", 1), ("ay", 3), ("ac", 2), ("ax", 3),
         ("ac", 3),
     )
 
@@ -831,19 +907,17 @@
                     for name, c in jobs:
                         do(name, c)
 
-    first = lax.broadcasted_iota(jnp.int32, (1, 2 * HEAD_DIM), 1) < HEAD_DIM
-    zero = jnp.zeros((), BF16)
-    scale = jnp.asarray(HEAD_DIM ** -0.5, BF16)
-    pairs = width // 128 // groups
-    wide = pairs * 128
+    wide = width // (groups + 1)
 
     @pl.when(step == 0)
     def _():
+        for copy in fetched:
+            copy.start()
         place.greet()
-        gn_ref[...] = jnp.zeros_like(gn_ref)
         vsum_ref[0] = vecin_ref[...]
         place.all_here()
         reduce.begin(0, 0)
+        reduce.begin(1, 0)
         for c in range(late):
             mlp.along_z(c)
 
@@ -852,40 +926,24 @@
         @pl.loop(0, images)
         def _(i):
             run(lambda at: at < images, step * polls + i)
-            here = pl.ds(pl.multiple_of(i * slots, 16), slots)
-            for pair in range(pairs):
-                own = slice(pair * 128, pair * 128 + 128)
-                query, key, value = q_ref[here, own], k_ref[here, own], v_ref[here, own]
-                grad_att = gatt_ref[here, own]
-                gq = gk = gv = None
-                for half in range(2):
-                    mine = first if half == 0 else jnp.logical_not(first)
-                    low = probs_ref[i, 2 * pair + half]
-                    probs = low.astype(F32)
-                    g_mine = jnp.where(mine, grad_att, zero)
-                    grad_probs = dot_t(g_mine, value).astype(BF16).astype(F32)
-                    inner = jnp.sum(probs * grad_probs, axis=1, keepdims=True)
-                    grad_scores = (probs * (grad_probs - inner)).astype(BF16) * scale
-                    tv = t_dot(low, g_mine)
-                    tq = dot(grad_scores, jnp.where(mine, key, zero))
-                    tk = t_dot(grad_scores, jnp.where(mine, query, zero))
-                    gq = tq if gq is None else gq + tq
-                    gk = tk if gk is None else gk + tk
-                    gv = tv if gv is None else gv + tv
-                gq_ref[here, own] = gq.astype(BF16)
-                gk_ref[here, own] = gk.astype(BF16)
-                gv_ref[here, own] = gv.astype(BF16)
+            head_back(slots, i, q_ref, k_ref, v_ref, probs_ref, gatt_ref, gq_ref, gk_ref, gv_ref)
 
         run(lambda at: at == images, step * polls + images)
-        cols = pl.ds(pl.multiple_of(step * wide, wide), wide)
-        shifted = pl.ds(pl.multiple_of(width + step * wide, wide), wide)
+
+        @pl.when(step == 0)
+        def _():
+            for copy in fetched[:2]:
+                copy.wait()
+
+        cols = pl.ds(pl.multiple_of((step + 1) * wide, wide), wide)
+        shifted = pl.ds(pl.multiple_of(width + (step + 1) * wide, wide), wide)
         vsum_ref[0, 2:3, cols] = jnp.sum(gq_ref[...].astype(F32), axis=0, keepdims=True)
         vsum_ref[0, 2:3, shifted] = jnp.sum(gv_ref[...].astype(F32), axis=0, keepdims=True)
         for part, ref in enumerate((gq_ref, gk_ref, gv_ref)):
             d = t_dot(normed_ref[...], ref[...]).astype(BF16)
             stage_ref[step, 0, part] = d[:, :128]
             stage_ref[step, 1, part] = d[:, 128:]
-        reduce.begin(step + 1, 0)
+        reduce.begin(step + 2, 0)
         for ref, w_ref in ((gq_ref, wq_ref), (gk_ref, wk_ref), (gv_ref, wv_ref)):
             gn_ref[...] += dot_t(ref[...], w_ref[...])
         run(lambda at: at == images + 1, step * polls + images + 1)
@@ -912,6 +970,8 @@
 
     @pl.when(step == groups)
     def _():
+        for copy in fetched[2:]:
+            copy.wait()
         g1 = as_row(g1_ref)
         gain = shift = jnp.zeros((1, width), F32)
         for i in range(images):
@@ -948,7 +1008,7 @@
         for c in range(late):
             mlp.arrive(c, 2)
             mlp.sent(c)
-        for c in range(groups + 1):
+        for c in range(groups + 2):
             back.arrive(c, 3)
             back.sent(c)
             reduce.sent(c)
@@ -1064,25 +1124,32 @@
     by_cols = lambda *lead: pl.BlockSpec(lead + (chunk,), lambda c: (0, c - c // ticks))
     by_rows = pl.BlockSpec((chunk, width), lambda c: (c - c // ticks, 0))
     early = ticks // 2
-    red, gmid, gatt, dwp, low, vec, first = pl.pallas_call(
+    wide = width // groups
+    red, gmid, gatt, dwp, low, vec, first, dwh, gn = pl.pallas_call(
         functools.partial(mlp_staged_kernel, deep, count, slots, ticks),
         grid=(ticks + 1,),
         out_shape=(
             shape((4 * ticks, piece, 128), BF16), shape((rows, width), F32), shape((rows, width), BF16),
             shape((2, 3, width, 128), BF16), shape((count, patches, width), BF16), shape((8, 2 * width), F32),
-            shape((4 * early, width, 128), BF16),
+            shape((4 * early, width, 128), BF16), shape((2, 3, width, 128), BF16), shape((rows, width), F32),
         ),
         in_specs=[
-            whole((rows, width)), whole((rows, width)), whole((rows, width)), whole((rows, width)),
-            whole((count, slots, patches)), whole((count, 8, width)),
+            whole((rows, width)), whole((rows, width)), whole((count, 8, width)),
             by_cols(width), by_cols(width), whole((shard,)), whole((shard,)), by_rows, by_rows,
-            whole((width, width)), whole((width,)), whole((width,)),
-        ],
+            whole((width,)), whole((width,)),
+        ] + 8 * [any_space],
         out_specs=(
             whole((4 * ticks, piece, 128)), whole((rows, width)), whole((rows, width)),
             whole((2, 3, width, 128)), whole((count, patches, width)), whole((8, 2 * width)), any_space,
+            whole((2, 3, width, 128)), any_space,
         ),
         scratch_shapes=[
+            pltpu.VMEM((rows, width), BF16), pltpu.VMEM((rows, width), F32), pltpu.VMEM((count, slots, patches), BF16),
+            pltpu.VMEM((width, width), BF16), pltpu.VMEM((rows, width), BF16),
+            pltpu.VMEM((rows, wide), BF16), pltpu.VMEM((rows, wide), BF16), pltpu.VMEM((rows, wide), BF16),
+            pltpu.VMEM((count, heads // groups, slots, slots), BF16),
+            pltpu.VMEM((width, wide), BF16), pltpu.VMEM((width, wide), BF16), pltpu.VMEM((width, wide), BF16),
+            pltpu.VMEM((rows, wide), BF16), pltpu.VMEM((rows, wide), BF16), pltpu.VMEM((rows, wide), BF16), dma((12,)),
             pltpu.VMEM((rows, width), F32), pltpu.VMEM((rows, width), F32), pltpu.VMEM((2, 8, chunk), F32),
             pltpu.VMEM((ticks, 4, width, 128), BF16), pltpu.VMEM((ticks, 4, width, 128), BF16),
             pltpu.VMEM((ticks, 4, width, 128), BF16), pltpu.VMEM((ticks, 4, width // 2, 128), BF16),
@@ -1093,16 +1160,17 @@
         compiler_params=pltpu.CompilerParams(vmem_limit_bytes=limit, collective_id=1, has_side_effects=True),
         name="mlp_both_ways",
     )(
-        hid, gm, att, mid, sel, sums, w_fc1, far_w1, b_fc1, far_b1, w_fc2, far_w2, w_proj, ln2_gain, b_fc2,
-    )
-    wide = width // groups
+        hid, gm, sums, w_fc1, far_w1, b_fc1, far_b1, w_fc2, far_w2, ln2_gain, b_fc2,
+        att, mid, sel, w_proj, normed, qkv, probs, w_qkv,
+    )
     chunks = groups + 1
-    now = lambda g: g - g // groups
+    left = groups - 1
+    now = lambda g: 1 + g - g // left
     third = lambda lead, part: pl.BlockSpec((lead, wide), lambda g: (0, part * groups + now(g)))
     late = ticks - early
     second, attn, put, vec = pl.pallas_call(
-        functools.partial(attention_staged_kernel, deep, count, slots, groups, ticks),
-        grid=(groups + 1,),
+        functools.partial(attention_staged_kernel, deep, count, slots, left, ticks),
+        grid=(left + 1,),
         out_shape=(
             shape((4 * late, width, 128), BF16), shape((2, 3 * chunks, width, 128), BF16),
             shape((count, patches, width), F32), shape((8, 2 * width), F32),
@@ -1111,14 +1179,14 @@
             third(rows, 0), third(rows, 1), third(rows, 2),
             pl.BlockSpec((count, heads // groups, slots, slots), lambda g: (0, now(g), 0, 0)),
             third(rows, 0), third(width, 0), third(width, 1), third(width, 2),
-            whole((rows, width)), whole((rows, width)), whole((rows, width)), whole((count, slots, patches)),
-            whole((width,)), whole((2, 3, width, 128)), whole((4 * ticks, piece, 128)), whole((8, 2 * width)),
-        ],
+            whole((width,)), whole((2, 3, width, 128)), whole((2, 3, width, 128)), whole((4 * ticks, piece, 128)),
+            whole((8, 2 * width)),
+        ] + 5 * [any_space],
         out_specs=(any_space, any_space, whole((count, patches, width)), whole((8, 2 * width))),
         scratch_shapes=[
             pltpu.VMEM((rows, wide), BF16), pltpu.VMEM((rows, wide), BF16), pltpu.VMEM((rows, wide), BF16),
             pltpu.VMEM((rows, width), F32),
-            pltpu.VMEM((groups, 2, 3, width, 128), BF16), pltpu.VMEM((chunks, 3, width, 128), BF16),
+            pltpu.VMEM((left, 2, 3, width, 128), BF16), pltpu.VMEM((chunks, 3, width, 128), BF16),
             pltpu.VMEM((chunks, 3, piece, 128), BF16), pltpu.VMEM((chunks, 3, width, 128), BF16),
             pltpu.VMEM((chunks, 3, width // 2, 128), BF16), pltpu.VMEM((chunks, 3, width // 4, 128), BF16),
             pltpu.VMEM((chunks, deep - 1, 3, piece, 128), BF16),
@@ -1128,11 +1196,13 @@
             dma((late,)), dma((late, 2)), dma((late, 2)), dma((late, deep - 1)), dma((late, deep - 1)),
             dma((chunks,)), dma((chunks, 3)), dma((chunks, 3)), dma((chunks, deep - 1)), dma((chunks, deep - 1)),
             dma((3,)), dma((3,)), dma((deep - 1,)), dma((deep - 1,)),
+            pltpu.VMEM((rows, width), BF16), pltpu.VMEM((rows, width), BF16), pltpu.VMEM((rows, width), F32),
+            pltpu.VMEM((count, slots, patches), BF16), dma((5,)),
         ],
         compiler_params=pltpu.CompilerParams(vmem_limit_bytes=limit, collective_id=2, has_side_effects=True),
         name="attention_backward",
     )(
-        qkv, qkv, qkv, probs, gatt, w_qkv, w_qkv, w_qkv, normed, x, gmid, sel, ln1_gain, dwp, red, vec,
+        qkv, qkv, qkv, probs, gatt, w_qkv, w_qkv, w_qkv, ln1_gain, dwp, dwh, red, vec, normed, x, gmid, sel, gn,
     )
     deal = width // ticks
     turn = lambda t: (t - t // count, 0, 0)

time: 205 us -> 200 us (0.976)
  Pallas kernels: 204 us -> 199 us
    pallas_call x1, Pallas kernels: 81.7 us -> 77.3 us  [staged_device(): pl.pallas_call(functools.partial(attention_staged_kernel, deep, count, sl...]
where the time goes in v5:
time: 200 us
  Pallas kernels  199 us (100%)
    pallas_call x1, Pallas kernels, staged_device(): pl.pallas_call(functools.partial(mlp_staged_kernel, deep, count, slots, t...  86.1 us
    pallas_call x1, Pallas kernels, staged_device(): pl.pallas_call(functools.partial(attention_staged_kernel, deep, count, sl...  77.3 us
    pallas_call x1, Pallas kernels, staged_device(): pl.pallas_call(functools.partial(forward_kernel, slots, True), grid=(coun...  20.2 us
    pallas_call x1, Pallas kernels, staged_device(): pl.pallas_call(functools.partial(finish_kernel, groups, early), grid=(tic...  15.5 us

profile of v5, /device:TPU:0, one launch (start us, length us, event | category | flops | bytes accessed | tf_op | source)
XLA Modules:
  0.0 199.9 jit_solution(5261902773806392270)
XLA Ops:
  0.6 20.2 %attention_forward.1 = (bf16[5,160,197]{2,1,0:T(8,128)(2,1)}, bf16[800,768]{1,0:T(8,128)(2,1)}, bf16[800,768]{1,0:T(8,128)(2,1)}, bf16[800,2304]{1,0:T(8,128)(2,...) custom-call(s32[5,197]{1,0:T(8,128)} %keep_ref.3, ...), custom_call_target="tpu_custom_call" | custom-call | tf_op jit(solution)/shard_map/attention_forward/pallas_call | solution.py:1086
  20.8 86.1 %mlp_both_ways.1 = (bf16[24,48,128]{2,1,0:T(8,128)(2,1)}, f32[800,768]{1,0:T(8,128)}, bf16[800,768]{1,0:T(8,128)(2,1)}, bf16[2,3,768,128]{3,2,1,0:T(8,128)(2,1)}...) custom-call(bf16[800,768]{1,0:T(8,128)(2,1)} %get-tuple-element.58.h, ...), custom_call_target="tpu_custom_call" | custom-call | tf_op jit(solution)/shard_map/mlp_both_ways/pallas_call | solution.py:1128
  106.9 77.3 %attention_backward.1 = (bf16[12,768,128]{2,1,0:T(8,128)(2,1)}, bf16[2,12,768,128]{3,2,1,0:T(8,128)(2,1)}, f32[5,197,768]{2,1,0:T(8,128)}, f32[8,1536]{1,0:T(8,128)}) custom-call(bf16[800,2304]{1,0:T(8,128)(2,1)} %get-tuple-element.68.qkv_hbm.q_ref.k_ref.v_ref, bf16[800,2304]{1,0:T(8,128)(2,1)} %get-tuple-element.68.qkv_hbm.q_ref.k_ref.v_ref, ...), custom_call_target="tpu_custom_call" | custom-call | tf_op jit(solution)/shard_map/attention_backward/pallas_call | solution.py:1171
  184.2 15.5 %results.1 = (bf16[5,197,768]{2,1,0:T(8,128)(2,1)}, f32[5,197,768]{2,1,0:T(8,128)}, f32[768,2304]{1,0:T(8,128)}, f32[768,768]{1,0:T(8,128)}, f32[768,1536]{1,0:T...) custom-call(bf16[12,768,128]{2,1,0:T(8,128)(2,1)} %get-tuple-element, ...), custom_call_target="tpu_custom_call" | custom-call | tf_op jit(solution)/shard_map/results/pallas_call | solution.py:1209

commit v6 on v5

--- a/solution.py
+++ b/solution.py
@@ -99,16 +99,10 @@
 
 
 def forward_kernel(
-    slots, exchange,
+    slots,
     keep_ref, img_ref, cot_ref, g1_ref, b1_ref, wqkv_ref, bq_ref, bv_ref, wproj_ref, bproj_ref, g2_ref, b2_ref,
-    *refs,
+    sel_ref, x_ref, normed_ref, qkv_ref, probs_ref, att_ref, mid_ref, hid_ref, gm_ref, sums_ref,
 ):
-    if exchange:
-        ours, refs, (send_sem, recv_sem) = refs[:3], refs[3:-2], refs[-2:]
-        theirs, refs = refs[-3:], refs[:-3]
-        trade = swap_weights(ours, theirs, send_sem, recv_sem)
-        trade(True)
-    sel_ref, x_ref, normed_ref, qkv_ref, probs_ref, att_ref, mid_ref, hid_ref, gm_ref, sums_ref = refs
     patches, width = img_ref.shape[1:]
     heads = width // HEAD_DIM
     keep = keep_ref[pl.ds(pl.program_id(0), 1)].astype(F32)
@@ -164,8 +158,154 @@
     sums_ref[0, 1:2] = jnp.broadcast_to(count, (1, width))
     scaled, _ = norm_rows(middle)
     hid_ref[...] = (scaled * as_row(g2_ref) + as_row(b2_ref)).astype(BF16)
-    if exchange:
-        trade(False)
+
+
+def forward_staged_kernel(
+    slots,
+    keep_ref, g1_ref, b1_ref, bq_ref, bv_ref, bproj_ref, g2_ref, b2_ref,
+    img_hbm, cot_hbm, wqkv_hbm, wproj_hbm, w1_hbm, bias1_hbm, w2_hbm,
+    sums_ref, sel_hbm, x_hbm, normed_hbm, qkv_hbm, probs_hbm, att_hbm, mid_hbm, hid_hbm, gm_hbm,
+    far_w1, far_bias1, far_w2,
+    img_ref, cot_ref,
+    wqkv_ref, wproj_ref, sel_ref, x_ref, normed_ref, qkv_ref, probs_ref, att_ref, mid_ref, hid_ref, gm_ref,
+    row_sem, in_sem, out_sem, probs_sem, part_sem, send_sem, recv_sem,
+):
+    images, patches, width = img_ref.shape
+    heads = width // HEAD_DIM
+    fetched = [
+        pltpu.make_async_copy(wqkv_hbm, wqkv_ref, in_sem.at[0]), pltpu.make_async_copy(wproj_hbm, wproj_ref, in_sem.at[1])
+    ]
+
+    def row_copies(i):
+        return [
+            pltpu.make_async_copy(img_hbm.at[i], img_ref.at[i], row_sem.at[i, 0]),
+            pltpu.make_async_copy(cot_hbm.at[i], cot_ref.at[i], row_sem.at[i, 1]),
+        ]
+
+    for i in range(images):
+        for copy in row_copies(i):
+            copy.start()
+    for copy in fetched:
+        copy.start()
+    trade = swap_weights((w1_hbm, bias1_hbm, w2_hbm), (far_w1, far_bias1, far_w2), send_sem, recv_sem)
+    trade(True)
+    upto = lax.broadcasted_iota(jnp.int32, (patches, patches), 0) <= lax.broadcasted_iota(
+        jnp.int32, (patches, patches), 1
+    )
+    upto = upto.astype(F32).astype(BF16)
+    slot = lax.broadcasted_iota(jnp.int32, (slots, patches), 0).astype(F32)
+    g1, b1, g2, b2 = (as_row(ref) for ref in (g1_ref, b1_ref, g2_ref, b2_ref))
+
+    def rows_of(i):
+        return pl.ds(pl.multiple_of(i * slots, 16), slots)
+
+    def count_of(i):
+        return jnp.sum(keep_ref[pl.ds(i, 1)].astype(F32), axis=1, keepdims=True)
+
+    @pl.loop(0, images)
+    def _(i):
+        for copy in row_copies(i):
+            copy.wait()
+        here = rows_of(i)
+        keep = keep_ref[pl.ds(i, 1)].astype(F32)
+        keep8 = jnp.broadcast_to(keep, (8, patches)).astype(BF16)
+        rank = dot(keep8, upto)[0:1]
+        sel = jnp.where((slot == rank - 1.0) & (keep > 0), 1.0, 0.0).astype(BF16)
+        sel_ref[i] = sel
+        gm_ref[here] = dot(sel, cot_ref[i]).astype(BF16)
+        rows = dot(sel, img_ref[i])
+        x_ref[here] = rows.astype(BF16)
+        scaled, _ = norm_rows(rows)
+        normed_ref[here] = (scaled * g1 + b1).astype(BF16)
+
+    sent = [
+        pltpu.make_async_copy(source, target, out_sem.at[j])
+        for j, (source, target) in enumerate(
+            (
+                (sel_ref, sel_hbm), (x_ref, x_hbm), (normed_ref, normed_hbm), (gm_ref, gm_hbm), (qkv_ref, qkv_hbm),
+                (att_ref, att_hbm),
+            )
+        )
+    ]
+    for copy in sent[:4]:
+        copy.start()
+    fetched[0].wait()
+    wide = width // 3
+    for j in range(9):
+        cols = slice(j * wide, j * wide + wide)
+        block = dot(normed_ref[...], wqkv_ref[:, cols])
+        own = slice(j % 3 * wide, j % 3 * wide + wide)
+        if j < 3:
+            block = block + as_row(bq_ref)[:, own]
+        if j >= 6:
+            block = block + as_row(bv_ref)[:, own]
+        qkv_ref[:, cols] = block.astype(BF16)
+    sent[4].start()
+    first = lax.broadcasted_iota(jnp.int32, (1, 2 * HEAD_DIM), 1) < HEAD_DIM
+    zero = jnp.zeros((), BF16)
+
+    def probs_copy(i):
+        return pltpu.make_async_copy(probs_ref.at[i], probs_hbm.at[i], probs_sem.at[i])
+
+    @pl.loop(0, images)
+    def _(i):
+        here = rows_of(i)
+        closed = jnp.where(
+            lax.broadcasted_iota(jnp.int32, (1, slots), 1).astype(F32) < count_of(i), 0.0, -1e30
+        )
+        for pair in range(heads // 2):
+            lanes = slice(pair * 128, pair * 128 + 128)
+            query = qkv_ref[here, lanes] * jnp.asarray(HEAD_DIM ** -0.5, BF16)
+            key = qkv_ref[here, width + pair * 128 : width + pair * 128 + 128]
+            value = qkv_ref[here, 2 * width + pair * 128 : 2 * width + pair * 128 + 128]
+            total = None
+            for half in range(2):
+                mine = first if half == 0 else jnp.logical_not(first)
+                scores = dot_t(query, jnp.where(mine, key, zero)) + closed
+                raised = jnp.exp(scores - jnp.max(scores, axis=1, keepdims=True))
+                probs = (raised * (1.0 / jnp.sum(raised, axis=1, keepdims=True))).astype(BF16)
+                probs_ref[i, 2 * pair + half] = probs
+                term = dot(probs, jnp.where(mine, value, zero))
+                total = term if total is None else total + term
+            att_ref[here, lanes] = total.astype(BF16)
+        probs_copy(i).start()
+
+    sent[5].start()
+    fetched[1].wait()
+    mid_ref[...] = dot(att_ref[...], wproj_ref[...]) + as_row(bproj_ref)
+
+    def part_copies(i):
+        here = rows_of(i)
+        return [
+            pltpu.make_async_copy(mid_ref.at[here], mid_hbm.at[here], part_sem.at[i, 0]),
+            pltpu.make_async_copy(hid_ref.at[here], hid_hbm.at[here], part_sem.at[i, 1]),
+        ]
+
+    @pl.loop(0, images)
+    def _(i):
+        here = rows_of(i)
+        count = count_of(i)
+        valid = lax.broadcasted_iota(jnp.int32, (slots, 1), 0).astype(F32) < count
+        attn_kept = jnp.where(valid, mid_ref[here], 0.0)
+        middle = x_ref[here].astype(F32) + attn_kept
+        mid_ref[here] = middle
+        sums_ref[i, 0:1] = jnp.sum(attn_kept * attn_kept, axis=0, keepdims=True)
+        sums_ref[i, 1:2] = jnp.broadcast_to(count, (1, width))
+        scaled, _ = norm_rows(middle)
+        hid_ref[here] = (scaled * g2 + b2).astype(BF16)
+        for copy in part_copies(i):
+            copy.start()
+
+    for copy in sent:
+        copy.wait()
+
+    @pl.loop(0, images)
+    def _(i):
+        probs_copy(i).wait()
+        for copy in part_copies(i):
+            copy.wait()
+
+    trade(False)
 
 
 def mlp_kernel(hid_ref, gm_ref, w1_ref, b1_ref, w2_ref, out_ref, gh_ref, dw1_ref, dw2_ref, db1_ref):
@@ -314,7 +454,7 @@
     per_image = lambda *tail: pl.BlockSpec((1,) + tail, lambda i: (i,) + (0,) * len(tail))
     per_rows = lambda cols: pl.BlockSpec((slots, cols), lambda i: (i, 0))
     sel, x, normed, qkv, probs, att, mid, hid, gm, sums = pl.pallas_call(
-        functools.partial(forward_kernel, slots, False),
+        functools.partial(forward_kernel, slots),
         grid=(count,),
         out_shape=(
             shape((count, slots, patches), BF16),
@@ -1083,39 +1223,33 @@
     per_image = lambda *tail: pl.BlockSpec((1,) + tail, lambda i: (i,) + (0,) * len(tail))
     per_rows = lambda cols: pl.BlockSpec((slots, cols), lambda i: (i, 0))
     dma = pltpu.SemaphoreType.DMA
-    sel, x, normed, qkv, probs, att, mid, hid, gm, sums, far_w1, far_b1, far_w2 = pl.pallas_call(
-        functools.partial(forward_kernel, slots, True),
-        grid=(count,),
-        out_shape=(
-            shape((count, slots, patches), BF16),
-            shape((rows, width), BF16),
-            shape((rows, width), BF16),
-            shape((rows, 3 * width), BF16),
-            shape((count, heads, slots, slots), BF16),
-            shape((rows, width), BF16),
-            shape((rows, width), F32),
-            shape((rows, width), BF16),
-            shape((rows, width), BF16),
-            shape((count, 8, width), F32),
+    vmem = pltpu.VMEM
+    stored = (
+        shape((count, slots, patches), BF16), shape((rows, width), BF16), shape((rows, width), BF16),
+        shape((rows, 3 * width), BF16), shape((count, heads, slots, slots), BF16), shape((rows, width), BF16),
+        shape((rows, width), F32), shape((rows, width), BF16), shape((rows, width), BF16),
+    )
+    sums, sel, x, normed, qkv, probs, att, mid, hid, gm, far_w1, far_b1, far_w2 = pl.pallas_call(
+        functools.partial(forward_staged_kernel, slots),
+        grid=(1,),
+        out_shape=(shape((count, 8, width), F32),) + stored + (
             shape((width, shard), BF16), shape((shard,), BF16), shape((shard, width), BF16),
         ),
         in_specs=[
-            whole((count, patches)), per_image(patches, width), per_image(patches, width),
-            whole((width,)), whole((width,)), whole((width, 3 * width)), whole((width,)), whole((width,)),
-            whole((width, width)), whole((width,)), whole((width,)), whole((width,)),
-            any_space, any_space, any_space,
-        ],
-        out_specs=(
-            per_image(slots, patches), per_rows(width), per_rows(width), per_rows(3 * width),
-            per_image(heads, slots, slots), per_rows(width), per_rows(width), per_rows(width), per_rows(width),
-            per_image(8, width), any_space, any_space, any_space,
-        ),
-        scratch_shapes=[dma((3,)), dma((3,))],
+            whole((count, patches)),
+        ] + 7 * [whole((width,))] + 7 * [any_space],
+        out_specs=(whole((count, 8, width)),) + 12 * (any_space,),
+        scratch_shapes=[
+            vmem((count, patches, width), BF16), vmem((count, patches, width), BF16),
+            vmem((width, 3 * width), BF16), vmem((width, width), BF16),
+        ]
+        + [vmem(s.shape, s.dtype) for s in stored]
+        + [dma((count, 2)), dma((2,)), dma((6,)), dma((count,)), dma((count, 2)), dma((3,)), dma((3,))],
         compiler_params=pltpu.CompilerParams(vmem_limit_bytes=limit, collective_id=0, has_side_effects=True),
         name="attention_forward",
     )(
-        keep_mask, images, cotangent, ln1_gain, ln1_bias, w_qkv, bias_q, bias_v, w_proj, b_proj, ln2_gain, ln2_bias,
-        w_fc1, b_fc1, w_fc2,
+        keep_mask, ln1_gain, ln1_bias, bias_q, bias_v, b_proj, ln2_gain, ln2_bias,
+        images, cotangent, w_qkv, w_proj, w_fc1, b_fc1, w_fc2,
     )
     chunk = 256
     ticks = shard // chunk

time: 200 us -> 200 us (level)
  no operation moved by 1% of the time
where the time goes in v6:
time: 200 us; the launch traced here: 199 us
  Pallas kernels  198 us (99%)
    pallas_call x1, Pallas kernels, staged_device(): pl.pallas_call(functools.partial(mlp_staged_kernel, deep, count, slots, t...  86 us
    pallas_call x1, Pallas kernels, staged_device(): pl.pallas_call(functools.partial(attention_staged_kernel, deep, count, sl...  77.5 us
    pallas_call x1, Pallas kernels, staged_device(): pl.pallas_call(functools.partial(forward_staged_kernel, slots), grid=(1,)...  19.4 us
    pallas_call x1, Pallas kernels, staged_device(): pl.pallas_call(functools.partial(finish_kernel, groups, early), grid=(tic...  15.5 us

profile of v6, /device:TPU:0, one launch (start us, length us, event | category | flops | bytes accessed | tf_op | source)
XLA Modules:
  0.0 199.3 jit_solution(10739368453188544944)
XLA Ops:
  0.6 19.4 %attention_forward.1 = (f32[5,8,768]{2,1,0:T(8,128)}, bf16[5,160,197]{2,1,0:T(8,128)(2,1)}, bf16[800,768]{1,0:T(8,128)(2,1)}, bf16[800,768]{1,0:T(8,128)(2,1)}, ...) custom-call(s32[5,197]{1,0:T(8,128)} %keep_ref.3, ...), custom_call_target="tpu_custom_call" | custom-call | tf_op jit(solution)/shard_map/attention_forward/pallas_call | solution.py:1232
  20.1 86.0 %mlp_both_ways.1 = (bf16[24,48,128]{2,1,0:T(8,128)(2,1)}, f32[800,768]{1,0:T(8,128)}, bf16[800,768]{1,0:T(8,128)(2,1)}, bf16[2,3,768,128]{3,2,1,0:T(8,128)(2,1)}...) custom-call(bf16[800,768]{1,0:T(8,128)(2,1)} %get-tuple-element.58.h, ...), custom_call_target="tpu_custom_call" | custom-call | tf_op jit(solution)/shard_map/mlp_both_ways/pallas_call | solution.py:1262
  106.1 77.5 %attention_backward.1 = (bf16[12,768,128]{2,1,0:T(8,128)(2,1)}, bf16[2,12,768,128]{3,2,1,0:T(8,128)(2,1)}, f32[5,197,768]{2,1,0:T(8,128)}, f32[8,1536]{1,0:T(8,128)}) custom-call(bf16[800,2304]{1,0:T(8,128)(2,1)} %get-tuple-element.68.qkv_hbm.q_ref.k_ref.v_ref, bf16[800,2304]{1,0:T(8,128)(2,1)} %get-tuple-element.68.qkv_hbm.q_ref.k_ref.v_ref, ...), custom_call_target="tpu_custom_call" | custom-call | tf_op jit(solution)/shard_map/attention_backward/pallas_call | solution.py:1305
  183.6 15.5 %results.1 = (bf16[5,197,768]{2,1,0:T(8,128)(2,1)}, f32[5,197,768]{2,1,0:T(8,128)}, f32[768,2304]{1,0:T(8,128)}, f32[768,768]{1,0:T(8,128)}, f32[768,1536]{1,0:T...) custom-call(bf16[12,768,128]{2,1,0:T(8,128)(2,1)} %get-tuple-element, ...), custom_call_target="tpu_custom_call" | custom-call | tf_op jit(solution)/shard_map/results/pallas_call | solution.py:1343

commit v7 on v6

--- a/solution.py
+++ b/solution.py
@@ -775,7 +775,8 @@
     deep, images, slots, ticks,
     hid_ref, gm_ref, sums_ref, w1a_ref, w1b_ref, b1a_ref, b1b_ref, w2a_ref, w2b_ref, g2_ref, bfc2_ref,
     att_hbm, mid_hbm, sel_hbm, wproj_hbm, normed_hbm, qkv_hbm, probs_hbm, wqkv_hbm,
-    red_ref, gmid_ref, gatt_ref, dwp_ref, lo_ref, vec_ref, early_ref, dwh_ref, gn_hbm,
+    red_ref, gmid_hbm, gatt_hbm, dwp_hbm, lo_hbm, vec_ref, early_ref, dwh_ref, gn_hbm,
+    gmid_ref, gatt_ref, dwp_ref, lo_ref, give_sem,
     att_ref, mid_ref, sel_ref, wproj_ref, normed_ref, q_ref, k_ref, v_ref, probs_ref, wq_ref, wk_ref, wv_ref,
     gq_ref, gk_ref, gv_ref, fetch_sem,
     out_ref, gh_ref, bias_ref, give_ref, own_ref, got_core, got1, got2, got_z, send, recv, send_z, recv_z,
@@ -931,6 +932,14 @@
             dwp_ref[0, part] = d[:, :128]
             dwp_ref[1, part] = d[:, 128:]
         gatt_ref[...] = dot_t(grad_attn, wproj_ref[...]).astype(BF16)
+        handed = [
+            pltpu.make_async_copy(source, target, give_sem.at[j])
+            for j, (source, target) in enumerate(
+                ((gmid_ref, gmid_hbm), (lo_ref, lo_hbm), (dwp_ref, dwp_hbm), (gatt_ref, gatt_hbm))
+            )
+        ]
+        for copy in handed:
+            copy.start()
 
         @pl.loop(0, images)
         def _(i):
@@ -959,6 +968,8 @@
         keep_gn.start()
         put_red(ticks - 1)
         keep_gn.wait()
+        for copy in handed:
+            copy.wait()
 
         @pl.loop(0, ticks)
         def _(c):
@@ -974,12 +985,12 @@
     deep, images, slots, groups, ticks,
     q_ref, k_ref, v_ref, probs_ref, gatt_ref, wq_ref, wk_ref, wv_ref, g1_ref, dwp_ref, dwh_ref, red_ref, vecin_ref,
     normed_hbm, x_hbm, gmid_hbm, sel_hbm, gn_hbm,
-    mlp_ref, attn_ref, gi_ref, vec_ref,
+    mlp_ref, attn_ref, gi_hbm, vec_ref,
     gq_ref, gk_ref, gv_ref, gn_ref, stage_ref, total_ref, piece_ref, got_core, got1, got2, got_z,
     vsum_ref, vgot_ref, vz_ref,
     send, recv, send_z, recv_z, m_local, m_send, m_recv, m_send_z, m_recv_z,
     a_local, a_send, a_recv, a_send_z, a_recv_z, v_send, v_recv, v_send_z, v_recv_z,
-    normed_ref, x_ref, gmid_ref, sel_ref, fetch_sem,
+    normed_ref, x_ref, gmid_ref, sel_ref, fetch_sem, gi_ref, gi_sem,
 ):
     step = pl.program_id(0)
     rows, width = x_ref.shape
@@ -1131,6 +1142,8 @@
         vsum_ref[0, at_row, at_col] = gain
         at_row, at_col = vec_slot(7, width)
         vsum_ref[0, at_row, at_col] = shift
+        leave = pltpu.make_async_copy(gi_ref, gi_hbm, gi_sem.at[0])
+        leave.start()
         vec_begin(0)
         for at, (name, c) in enumerate(tail):
             do(name, c)
@@ -1145,6 +1158,7 @@
                 term = jnp.where((place.z - k - 1 + deep) % deep == z, from_k[k], term)
             value = term if value is None else value + term
         vec_ref[...] = value
+        leave.wait()
         for c in range(late):
             mlp.arrive(c, 2)
             mlp.sent(c)
@@ -1273,11 +1287,12 @@
             whole((width,)), whole((width,)),
         ] + 8 * [any_space],
         out_specs=(
-            whole((4 * ticks, piece, 128)), whole((rows, width)), whole((rows, width)),
-            whole((2, 3, width, 128)), whole((count, patches, width)), whole((8, 2 * width)), any_space,
+            whole((4 * ticks, piece, 128)), any_space, any_space, any_space, any_space, whole((8, 2 * width)), any_space,
             whole((2, 3, width, 128)), any_space,
         ),
         scratch_shapes=[
+            vmem((rows, width), F32), vmem((rows, width), BF16), vmem((2, 3, width, 128), BF16),
+            vmem((count, patches, width), BF16), dma((4,)),
             pltpu.VMEM((rows, width), BF16), pltpu.VMEM((rows, width), F32), pltpu.VMEM((count, slots, patches), BF16),
             pltpu.VMEM((width, width), BF16), pltpu.VMEM((rows, width), BF16),
             pltpu.VMEM((rows, wide), BF16), pltpu.VMEM((rows, wide), BF16), pltpu.VMEM((rows, wide), BF16),
@@ -1316,7 +1331,7 @@
             whole((width,)), whole((2, 3, width, 128)), whole((2, 3, width, 128)), whole((4 * ticks, piece, 128)),
             whole((8, 2 * width)),
         ] + 5 * [any_space],
-        out_specs=(any_space, any_space, whole((count, patches, width)), whole((8, 2 * width))),
+        out_specs=(any_space, any_space, any_space, whole((8, 2 * width))),
         scratch_shapes=[
             pltpu.VMEM((rows, wide), BF16), pltpu.VMEM((rows, wide), BF16), pltpu.VMEM((rows, wide), BF16),
             pltpu.VMEM((rows, width), F32),
@@ -1331,7 +1346,7 @@
             dma((chunks,)), dma((chunks, 3)), dma((chunks, 3)), dma((chunks, deep - 1)), dma((chunks, deep - 1)),
             dma((3,)), dma((3,)), dma((deep - 1,)), dma((deep - 1,)),
             pltpu.VMEM((rows, width), BF16), pltpu.VMEM((rows, width), BF16), pltpu.VMEM((rows, width), F32),
-            pltpu.VMEM((count, slots, patches), BF16), dma((5,)),
+            pltpu.VMEM((count, slots, patches), BF16), dma((5,)), vmem((count, patches, width), F32), dma((1,)),
         ],
         compiler_params=pltpu.CompilerParams(vmem_limit_bytes=limit, collective_id=2, has_side_effects=True),
         name="attention_backward",

time: 200 us -> 197 us (0.985)
  Pallas kernels: 198 us -> 195 us
    pallas_call x1, Pallas kernels: 86 us -> 83.9 us  [staged_device(): pl.pallas_call(functools.partial(mlp_staged_kernel, deep, count, slots, t...]
where the time goes in v7:
time: 197 us; the launch traced here: 196 us
  Pallas kernels  195 us (99%)
    pallas_call x1, Pallas kernels, staged_device(): pl.pallas_call(functools.partial(mlp_staged_kernel, deep, count, slots, t...  83.9 us
    pallas_call x1, Pallas kernels, staged_device(): pl.pallas_call(functools.partial(attention_staged_kernel, deep, count, sl...  76.5 us
    pallas_call x1, Pallas kernels, staged_device(): pl.pallas_call(functools.partial(forward_staged_kernel, slots), grid=(1,)...  19.4 us
    pallas_call x1, Pallas kernels, staged_device(): pl.pallas_call(functools.partial(finish_kernel, groups, early), grid=(tic...  15.5 us

profile of v7, /device:TPU:0, one launch (start us, length us, event | category | flops | bytes accessed | tf_op | source)
XLA Modules:
  0.0 196.2 jit_solution(1191670106631775077)
XLA Ops:
  0.6 19.4 %attention_forward.1 = (f32[5,8,768]{2,1,0:T(8,128)}, bf16[5,160,197]{2,1,0:T(8,128)(2,1)}, bf16[800,768]{1,0:T(8,128)(2,1)}, bf16[800,768]{1,0:T(8,128)(2,1)}, ...) custom-call(s32[5,197]{1,0:T(8,128)} %keep_ref.3, ...), custom_call_target="tpu_custom_call" | custom-call | tf_op jit(solution)/shard_map/attention_forward/pallas_call | solution.py:1246
  20.1 83.9 %mlp_both_ways.1 = (bf16[24,48,128]{2,1,0:T(8,128)(2,1)}, f32[800,768]{1,0:T(8,128)}, bf16[800,768]{1,0:T(8,128)(2,1)}, bf16[2,3,768,128]{3,2,1,0:T(8,128)(2,1)}...) custom-call(bf16[800,768]{1,0:T(8,128)(2,1)} %get-tuple-element.58.h, ...), custom_call_target="tpu_custom_call" | custom-call | tf_op jit(solution)/shard_map/mlp_both_ways/pallas_call | solution.py:1276
  104.0 76.5 %attention_backward.1 = (bf16[12,768,128]{2,1,0:T(8,128)(2,1)}, bf16[2,12,768,128]{3,2,1,0:T(8,128)(2,1)}, f32[5,197,768]{2,1,0:T(8,128)}, f32[8,1536]{1,0:T(8,128)}) custom-call(bf16[800,2304]{1,0:T(8,128)(2,1)} %get-tuple-element.68.qkv_hbm.q_ref.k_ref.v_ref, bf16[800,2304]{1,0:T(8,128)(2,1)} %get-tuple-element.68.qkv_hbm.q_ref.k_ref.v_ref, ...), custom_call_target="tpu_custom_call" | custom-call | tf_op jit(solution)/shard_map/attention_backward/pallas_call | solution.py:1320
  180.5 15.5 %results.1 = (bf16[5,197,768]{2,1,0:T(8,128)(2,1)}, f32[5,197,768]{2,1,0:T(8,128)}, f32[768,2304]{1,0:T(8,128)}, f32[768,768]{1,0:T(8,128)}, f32[768,1536]{1,0:T...) custom-call(bf16[12,768,128]{2,1,0:T(8,128)(2,1)} %get-tuple-element, ...), custom_call_target="tpu_custom_call" | custom-call | tf_op jit(solution)/shard_map/results/pallas_call | solution.py:1358
